TPU v7x, 32 devices: a whole 2x2x4 slice. The times are simulated.
32 devices in a mesh: dp: 8 (over z, y), seq: 4 (over x, core).
Axes of the slice: x: 2, y: 2, z: 4, core: 2. Of those that a mesh axis runs over, the one named last changes fastest.
Arguments:
- block_input: bfloat16 [16, 1024, 1024], P('dp', 'seq'), may hold values from -6 to 6
- doc_ids: int32 [16, 1024], P('dp'), may hold values from 0 to 5, never falling along the last dimension, each value on 1 to 512 neighbouring positions
- gain_attn: float32 [1024], P(('dp', 'seq')), may hold values from 0.25 to 1.75
- shift_attn: float32 [1024], P(('dp', 'seq')), may hold values from -4 to 4
- w_qkv: float32 [1024, 3072], P(('dp', 'seq')), may hold values from -0.1875 to 0.1875
- bias_qv: float32 [2048], P(('dp', 'seq')), may hold values from -6 to 6
- w_proj: float32 [1024, 1024], P(('dp', 'seq')), may hold values from -6 to 6
- bias_proj: float32 [1024], P(('dp', 'seq')), may hold values from -6 to 6
- gain_mlp: float32 [1024], P(('dp', 'seq')), may hold values from 0.25 to 1.75
- shift_mlp: float32 [1024], P(('dp', 'seq')), may hold values from -4 to 4
- w_up: float32 [1024, 4096], P(('dp', 'seq')), may hold values from -0.1875 to 0.1875
- bias_up: float32 [4096], P(('dp', 'seq')), may hold values from -6 to 6
- w_down: float32 [4096, 1024], P(('dp', 'seq')), may hold values from -0.875 to 0.875
- bias_down: float32 [1024], P(('dp', 'seq')), may hold values from -6 to 6
- out_grad: bfloat16 [16, 1024, 1024], P('dp', 'seq'), may hold values from -6 to 6
Outputs:
- block_out: bfloat16 [16, 1024, 1024], P('dp', 'seq')
- grad_input: float32 [16, 1024, 1024], P('dp', 'seq')
- d_gain_attn: float32 [1024], P(('dp', 'seq'))
- d_shift_attn: float32 [1024], P(('dp', 'seq'))
- d_w_qkv: float32 [1024, 3072], P(('dp', 'seq'))
- d_bias_qv: float32 [2048], P(('dp', 'seq'))
- d_w_proj: float32 [1024, 1024], P(('dp', 'seq'))
- d_bias_proj: float32 [1024], P(('dp', 'seq'))
- d_gain_mlp: float32 [1024], P(('dp', 'seq'))
- d_shift_mlp: float32 [1024], P(('dp', 'seq'))
- d_w_up: float32 [1024, 4096], P(('dp', 'seq'))
- d_bias_up: float32 [4096], P(('dp', 'seq'))
- d_w_down: float32 [4096, 1024], P(('dp', 'seq'))
- d_bias_down: float32 [1024], P(('dp', 'seq'))
Inputs may be any that keep to these rules, and one draw needn't show every extreme that they name: `doc_ids`: in each row the document numbers never fall; every one of the 6 documents has 1 to 512 tokens.
All inputs are finite; a program needn't handle non-finite values.
Results may differ from a plain program's by a relative error of at most 0.012.
The roundings to bfloat16 on the way count: a program that leaves them out, or rounds other values in their place, can miss the bound.
Values may be sent and summed in bfloat16 or wider, within the bound.
No kernel may reach another device: no remote copies, remote signals or barrier semaphores. Data moves between devices by JAX's collectives and lax.ppermute only.
A program may use at most 256 MiB of HBM per device.

v0:
```python
from functools import partial

import jax
import jax.numpy as jnp
from jax import lax
from jax.sharding import PartitionSpec as P

H = 16
LAYERS = 24


EPSILON = 1e-05


def half(values):
    return values.astype(jnp.bfloat16)


def norm_parts(values):
    mean = jnp.mean(values, axis=-1, keepdims=True)
    centred = values - mean
    spread = jnp.mean(centred * centred, axis=-1, keepdims=True)
    inverse = lax.rsqrt(spread + EPSILON)
    return (centred * inverse, inverse)


def norm_back(grad_out, normal, inverse, gain):
    scaled = grad_out * gain
    return inverse * (
        scaled
        - jnp.mean(scaled, axis=-1, keepdims=True)
        - normal * jnp.mean(scaled * normal, axis=-1, keepdims=True)
    )


def matmul(left, right):
    return jnp.einsum("rtk,kn->rtn", left, right, preferred_element_type=jnp.float32)


def weight_grad(left, right):
    return jnp.einsum("rtk,rtn->kn", left, right, preferred_element_type=jnp.float32)


def back_matmul(grad, weight):
    return jnp.einsum("rtn,kn->rtk", grad, weight, preferred_element_type=jnp.float32)


def token_sum(values):
    return jnp.sum(values, axis=(0, 1), dtype=jnp.float32)


def visible(doc_row, start, block):
    query_docs = lax.dynamic_slice_in_dim(doc_row, start, block)
    query_pos = start + lax.iota(jnp.int32, block)
    key_pos = lax.iota(jnp.int32, doc_row.shape[0])
    return (query_docs[:, None] == doc_row[None, :]) & (query_pos[:, None] >= key_pos[None, :])


def attend_row(packed, doc_row, heads, block):
    length = packed.shape[0]
    query = packed[:, 0].reshape(length, heads, -1)
    key = packed[:, 1].reshape(length, heads, -1)
    value = packed[:, 2].reshape(length, heads, -1)
    scale = query.shape[-1] ** (-0.5)

    def one_block(start):
        q_part = lax.dynamic_slice_in_dim(query, start, block, 0)
        scores = jnp.einsum("qhd,khd->hqk", q_part, key, preferred_element_type=jnp.float32) * scale
        scores = jnp.where(visible(doc_row, start, block)[None], scores, -1e30)
        row_max = jnp.max(scores, axis=-1, keepdims=True)
        exponent = jnp.exp(scores - row_max)
        total = jnp.sum(exponent, axis=-1, keepdims=True)
        attn_probs = half(exponent / total)
        result = jnp.einsum("hqk,khd->qhd", attn_probs, value, preferred_element_type=jnp.float32)
        return (half(result).reshape(block, -1), (row_max + jnp.log(total))[..., 0])

    starts = jnp.arange(length // block, dtype=jnp.int32) * block
    results, log_totals = lax.map(one_block, starts)
    return (results.reshape(length, -1), log_totals)


def attend_back(packed, grad_out, log_totals, doc_row, heads, block):
    length = packed.shape[0]
    query = packed[:, 0].reshape(length, heads, -1)
    key = packed[:, 1].reshape(length, heads, -1)
    value = packed[:, 2].reshape(length, heads, -1)
    grad_o = grad_out.reshape(length, heads, -1)
    scale = query.shape[-1] ** (-0.5)

    def one_block(carry, item):
        key_sum, value_sum = carry
        start, log_total = item
        q_part = lax.dynamic_slice_in_dim(query, start, block, 0)
        g_part = lax.dynamic_slice_in_dim(grad_o, start, block, 0)
        scores = jnp.einsum("qhd,khd->hqk", q_part, key, preferred_element_type=jnp.float32) * scale
        scores = jnp.where(visible(doc_row, start, block)[None], scores, -1e30)
        probs_full = jnp.exp(scores - log_total[..., None])
        probs_low = half(probs_full)
        grad_prob = jnp.einsum("qhd,khd->hqk", g_part, value, preferred_element_type=jnp.float32)
        delta = jnp.sum(grad_prob * probs_full, axis=-1, keepdims=True)
        grad_score = half(probs_full * (grad_prob - delta))
        grad_q = (
            jnp.einsum("hqk,khd->qhd", grad_score, key, preferred_element_type=jnp.float32) * scale
        )
        key_sum = (
            key_sum
            + jnp.einsum("hqk,qhd->khd", grad_score, q_part, preferred_element_type=jnp.float32)
            * scale
        )
        value_sum = value_sum + jnp.einsum(
            "hqk,qhd->khd", probs_low, g_part, preferred_element_type=jnp.float32
        )
        return ((key_sum, value_sum), half(grad_q).reshape(block, -1))

    starts = jnp.arange(length // block, dtype=jnp.int32) * block
    empty = jnp.zeros(key.shape, jnp.float32)
    (key_sum, value_sum), grad_query = lax.scan(one_block, (empty, empty), (starts, log_totals))
    grad_query = grad_query.reshape(length, -1)
    return jnp.stack(
        [grad_query, half(key_sum).reshape(length, -1), half(value_sum).reshape(length, -1)], axis=1
    )


def body(
    block_input,
    doc_ids,
    gain_attn,
    shift_attn,
    w_qkv,
    bias_qv,
    w_proj,
    bias_proj,
    gain_mlp,
    shift_mlp,
    w_up,
    bias_up,
    w_down,
    bias_down,
    out_grad,
):
    seq_count = lax.axis_size("seq")
    heads = H // seq_count
    length = doc_ids.shape[1]
    block = min(512, length)
    depth = LAYERS ** (-0.5)
    rows = block_input.shape[0]
    local_len = block_input.shape[1]
    width = block_input.shape[2]
    (
        half_gain_attn,
        half_shift_attn,
        half_qkv,
        half_bias_qv,
        half_proj,
        half_bias_proj,
        half_gain_mlp,
        half_shift_mlp,
        half_up,
        half_bias_up,
        half_down,
        half_bias_down,
    ) = (
        lax.all_gather(half(gain_attn), ("dp", "seq"), axis=0, tiled=True),
        lax.all_gather(half(shift_attn), ("dp", "seq"), axis=0, tiled=True),
        lax.all_gather(half(w_qkv), ("dp", "seq"), axis=0, tiled=True),
        lax.all_gather(half(bias_qv), ("dp", "seq"), axis=0, tiled=True),
        lax.all_gather(half(w_proj), ("dp", "seq"), axis=0, tiled=True),
        lax.all_gather(half(bias_proj), ("dp", "seq"), axis=0, tiled=True),
        lax.all_gather(half(gain_mlp), ("dp", "seq"), axis=0, tiled=True),
        lax.all_gather(half(shift_mlp), ("dp", "seq"), axis=0, tiled=True),
        lax.all_gather(half(w_up), ("dp", "seq"), axis=0, tiled=True),
        lax.all_gather(half(bias_up), ("dp", "seq"), axis=0, tiled=True),
        lax.all_gather(half(w_down), ("dp", "seq"), axis=0, tiled=True),
        lax.all_gather(half(bias_down), ("dp", "seq"), axis=0, tiled=True),
    )
    inputs = block_input.astype(jnp.float32)
    normal_one, inverse_one = norm_parts(inputs)
    normed_attn = half(normal_one * half_gain_attn + half_shift_attn)
    bias_full = jnp.concatenate(
        [half_bias_qv[:width], jnp.zeros((width,), jnp.bfloat16), half_bias_qv[width:]]
    ).astype(jnp.float32)
    mixed = half(matmul(normed_attn, half_qkv) + bias_full).reshape(rows, local_len, 3, width)
    by_heads = lax.all_to_all(mixed, "seq", split_axis=3, concat_axis=1, tiled=True)

    def forward_row(item):
        return attend_row(item[0], item[1], heads, block)

    attended_heads, log_totals = lax.map(forward_row, (by_heads, doc_ids))
    attended = lax.all_to_all(attended_heads, "seq", split_axis=1, concat_axis=2, tiled=True)
    branch = matmul(attended, half_proj) + half_bias_proj
    hidden = inputs + depth * branch
    normal_two, inverse_two = norm_parts(hidden)
    normed_mlp = half(normal_two * half_gain_mlp + half_shift_mlp)
    upward = matmul(normed_mlp, half_up) + half_bias_up
    active = half(jax.nn.gelu(upward, approximate=True))
    lowered = matmul(active, half_down) + half_bias_down
    block_out = half(hidden + depth * lowered)
    back_gain_attn, back_qkv, back_proj, back_gain_mlp, back_up, back_down = (
        lax.all_gather(half(gain_attn), ("dp", "seq"), axis=0, tiled=True),
        lax.all_gather(half(w_qkv), ("dp", "seq"), axis=0, tiled=True),
        lax.all_gather(half(w_proj), ("dp", "seq"), axis=0, tiled=True),
        lax.all_gather(half(gain_mlp), ("dp", "seq"), axis=0, tiled=True),
        lax.all_gather(half(w_up), ("dp", "seq"), axis=0, tiled=True),
        lax.all_gather(half(w_down), ("dp", "seq"), axis=0, tiled=True),
    )
    grad_out = out_grad.astype(jnp.float32)
    grad_down = half(depth * grad_out)
    d_bias_down = token_sum(grad_down)
    gelu_value, gelu_pull = jax.vjp(partial(jax.nn.gelu, approximate=True), upward)
    d_w_down = weight_grad(active, grad_down)
    grad_active = back_matmul(grad_down, back_down)
    grad_up = half(gelu_pull(grad_active)[0])
    d_bias_up = token_sum(grad_up)
    d_w_up = weight_grad(normed_mlp, grad_up)
    grad_normed_mlp = back_matmul(grad_up, back_up)
    d_gain_mlp = jnp.sum(grad_normed_mlp * normal_two, axis=(0, 1))
    d_shift_mlp = jnp.sum(grad_normed_mlp, axis=(0, 1))
    grad_hidden = grad_out + norm_back(grad_normed_mlp, normal_two, inverse_two, back_gain_mlp)
    grad_branch = half(depth * grad_hidden)
    d_bias_proj = token_sum(grad_branch)
    d_w_proj = weight_grad(attended, grad_branch)
    grad_attended = half(back_matmul(grad_branch, back_proj))
    grad_by_heads = lax.all_to_all(grad_attended, "seq", split_axis=2, concat_axis=1, tiled=True)

    def backward_row(item):
        return attend_back(item[0], item[1], item[2], item[3], heads, block)

    grad_packed = lax.map(backward_row, (by_heads, grad_by_heads, log_totals, doc_ids))
    grad_mixed = lax.all_to_all(
        grad_packed, "seq", split_axis=1, concat_axis=3, tiled=True
    ).reshape(rows, local_len, 3 * width)
    d_bias_qv = jnp.concatenate(
        [token_sum(grad_mixed[:, :, :width]), token_sum(grad_mixed[:, :, 2 * width :])]
    )
    d_w_qkv = weight_grad(normed_attn, grad_mixed)
    grad_normed_attn = back_matmul(grad_mixed, back_qkv)
    d_gain_attn = jnp.sum(grad_normed_attn * normal_one, axis=(0, 1))
    d_shift_attn = jnp.sum(grad_normed_attn, axis=(0, 1))
    grad_input = grad_hidden + norm_back(grad_normed_attn, normal_one, inverse_one, back_gain_attn)
    sum_up, sum_bias_up, sum_down = (
        lax.psum_scatter(d_w_up, ("dp", "seq"), scatter_dimension=0, tiled=True),
        lax.psum_scatter(d_bias_up, ("dp", "seq"), scatter_dimension=0, tiled=True),
        lax.psum_scatter(d_w_down, ("dp", "seq"), scatter_dimension=0, tiled=True),
    )
    (
        sum_gain_attn,
        sum_shift_attn,
        sum_qkv,
        sum_bias_qv,
        sum_proj,
        sum_bias_proj,
        sum_gain_mlp,
        sum_shift_mlp,
        sum_bias_down,
    ) = (
        lax.psum_scatter(d_gain_attn, ("dp", "seq"), scatter_dimension=0, tiled=True),
        lax.psum_scatter(d_shift_attn, ("dp", "seq"), scatter_dimension=0, tiled=True),
        lax.psum_scatter(d_w_qkv, ("dp", "seq"), scatter_dimension=0, tiled=True),
        lax.psum_scatter(d_bias_qv, ("dp", "seq"), scatter_dimension=0, tiled=True),
        lax.psum_scatter(d_w_proj, ("dp", "seq"), scatter_dimension=0, tiled=True),
        lax.psum_scatter(d_bias_proj, ("dp", "seq"), scatter_dimension=0, tiled=True),
        lax.psum_scatter(d_gain_mlp, ("dp", "seq"), scatter_dimension=0, tiled=True),
        lax.psum_scatter(d_shift_mlp, ("dp", "seq"), scatter_dimension=0, tiled=True),
        lax.psum_scatter(d_bias_down, ("dp", "seq"), scatter_dimension=0, tiled=True),
    )
    return (
        block_out,
        grad_input,
        sum_gain_attn,
        sum_shift_attn,
        sum_qkv,
        sum_bias_qv,
        sum_proj,
        sum_bias_proj,
        sum_gain_mlp,
        sum_shift_mlp,
        sum_up,
        sum_bias_up,
        sum_down,
        sum_bias_down,
    )


def solution(mesh):
    placed = (
        P("dp", "seq", None),
        P("dp", None),
        P(("dp", "seq")),
        P(("dp", "seq")),
        P(("dp", "seq"), None),
        P(("dp", "seq")),
        P(("dp", "seq"), None),
        P(("dp", "seq")),
        P(("dp", "seq")),
        P(("dp", "seq")),
        P(("dp", "seq"), None),
        P(("dp", "seq")),
        P(("dp", "seq"), None),
        P(("dp", "seq")),
        P("dp", "seq", None),
    )
    return jax.shard_map(
        body,
        mesh=mesh,
        in_specs=placed,
        out_specs=(
            P("dp", "seq", None),
            P("dp", "seq", None),
            P(("dp", "seq")),
            P(("dp", "seq")),
            P(("dp", "seq"), None),
            P(("dp", "seq")),
            P(("dp", "seq"), None),
            P(("dp", "seq")),
            P(("dp", "seq")),
            P(("dp", "seq")),
            P(("dp", "seq"), None),
            P(("dp", "seq")),
            P(("dp", "seq"), None),
            P(("dp", "seq")),
        ),
        check_vma=False,
    )
```

profile of v0, /device:TPU:0, one launch (start us, length us, event | category | flops | bytes accessed | tf_op | source)
XLA Modules:
  0.0 1059.8 jit_solution(17322499189606672461)
XLA Ops:
  18.5 42.4 %all-reduce.16 = (bf16[2048]{0:T(1024)(128)(2,1)S(1)}, bf16[1024]{0:T(1024)(128)(2,1)S(1)}, bf16[1024]{0:T(1024)(128)(2,1)S(1)}, bf16[1024]{0:T(1024)(128)(2,1)}...) all-reduce(bf16[2048]{0:T(1024)(128)(2,1)S(1)} %dynamic-update-slic, ...), channel_id=1, replica_groups=mesh['dp'=8,'seq'=4] {'dp','seq'}, use_global_device_ids=true, to_apply=%add.2 | all-reduce | flops 8192 | bytes 32768
  62.9 20.8 %all-gather.6.cloned.1.call-done = bf16[1024,3072]{1,0:T(8,128)(2,1)} async-done(((bf16[32,3072]{1,0:T(8,128)(2,1)}), bf16[1024,3072]{1,0:T(8,128)(2,1)}) %all-gather.6.cloned.1.call-update) | async-done | bytes 6291472 | tf_op jit(solution)/shard_map/all_gather | solution.py:165
  105.7 40.0 %all-to-all-done = bf16[2,256,3,1024]{1,0,2,3:T(2,128)(2,1)S(1)} async-done(((bf16[2,256,3,1024]{1,0,2,3:T(2,128)(2,1)}), bf16[2,256,3,1024]{1,0,2,3:T(2,128)(2,1)S(1)}, u32[]{:S(2)}, u32[]{:S(2)}) %all-to-all-start) | async-done | bytes 3145760 | tf_op jit(solution)/shard_map/all_to_all | solution.py:183
  154.1 50.3 %while.50 = (s32[]{:T(128)}, bf16[2,1024,256]{2,1,0:T(8,128)(2,1)}, f32[2,2,4,512]{3,2,1,0:T(4,128)S(1)}, bf16[2,1024,3,256]{1,3,2,0:T(8,128)(2,1)}, s32[2,1024]...) while((s32[]{:T(128)}, bf16[2,1024,256]{2,1,0:T(8,128)(2,1)}, ...), condition=%wide.region_7.8_spmd, body=%wide.region_2.7_spmd.sunk | while | flops 563739136 | bytes 37345692 | solution.py:188
  155.7 22.6 %while.53 = (s32[]{:T(128)}, bf16[2,512,256]{2,1,0:T(8,128)(2,1)S(1)}, f32[2,4,512]{2,1,0:T(4,128)S(1)}, s32[2]{0:T(128)S(1)}, s32[1024]{0:T(1024)S(1)}, /*index...) while((s32[]{:T(128)}, ...), condition=%wide.region_6.6_spmd, body=%wide.region_3.5_spmd.sunk | while | flops 563739136 | bytes 29964472 | solution.py:78
  180.9 22.6 %while.53 = (s32[]{:T(128)}, bf16[2,512,256]{2,1,0:T(8,128)(2,1)S(1)}, f32[2,4,512]{2,1,0:T(4,128)S(1)}, s32[2]{0:T(128)S(1)}, s32[1024]{0:T(1024)S(1)}, /*index...) while((s32[]{:T(128)}, ...), condition=%wide.region_6.6_spmd, body=%wide.region_3.5_spmd.sunk | while | flops 563739136 | bytes 29964472 | solution.py:78
  211.4 45.8 %all-gather = bf16[32,1,128]{2,1,0:T(2,128)(2,1)S(1)} all-gather(bf16[1,1,128]{2,1,0:T(2,128)(2,1)S(1)} %convert_bitcast_fusion), channel_id=1, replica_groups=mesh['dp'=8,'seq'=4] {'dp','seq'}, dimensions={0}, use_global_device_ids=true | all-gather | bytes 8448 | tf_op jit(solution)/shard_map/all_gather | solution.py:172
  263.4 10.7 %fusion.50 = f32[2,256,4096]{2,1,0:T(8,128)} fusion(bf16[1024,4096]{1,0:T(8,128)(2,1)} %all-gather.10.cloned.1.call-done, f32[2,256,1024]{2,1,0:T(8,128)S(1)} %get-tuple-element.349, f32[1024]{0:T(1024)S(1)} %convert_element_type.163, f32[1024]{0:T(1024)S(1)} %convert_element_type.161, f32[2,256]{1,0:T(2,128)S(1)} %add_rsqrt_fusion, ...), kind=kOutput, calls=%fused_computation.76 | convolution fusion | flops 4297588736 | bytes 18886656 | tf_op jit(solution)/shard_map/rtk,kn->rtn/dot_general | solution.py:37
  274.1 31.8 %all-gather.12.cloned.1.call-done = bf16[4096,1024]{1,0:T(8,128)(2,1)} async-done(((bf16[128,1024]{1,0:T(8,128)(2,1)}), bf16[4096,1024]{1,0:T(8,128)(2,1)}) %all-gather.12.cloned.1.call-update) | async-done | bytes 8388624 | tf_op jit(solution)/shard_map/all_gather | solution.py:173
  305.8 14.0 %convert_reduce_fusion = (f32[4096]{0:T(1024)}, bf16[2,256,4096]{2,1,0:T(8,128)(2,1)S(1)}) fusion(f32[2,256,4096]{2,1,0:T(8,128)} %fusion.50, f32[4096]{0:T(1024)S(1)} %bitcast.216, bf16[4096,1024]{1,0:T(8,128)(2,1)} %all-gather.12.cloned.1.call-done, bf16[2,256,1024]{2,1,0:T(8,128)(2,1)S(1)} %copy-done.18), kind=kOutput, calls=%fused_computation.78 | convolution fusion | flops 4344770560 | bytes 22052864 | tf_op jit(solution)/shard_map/rtn,kn->rtk/dot_general | solution.py:45
  340.1 11.5 %all-to-all-done.2 = bf16[2,256,1024]{1,0,2:T(2,128)(2,1)S(1)} async-done(((bf16[2,256,1024]{1,0,2:T(2,128)(2,1)}), bf16[2,256,1024]{1,0,2:T(2,128)(2,1)S(1)}, u32[]{:S(2)}, u32[]{:S(2)}) %all-to-all-start.2) | async-done | bytes 1048608 | tf_op jit(solution)/shard_map/all_to_all | solution.py:223
  354.3 106.9 %while.52 = (s32[]{:T(128)}, bf16[2,1024,3,256]{1,3,2,0:T(8,128)(2,1)}, f32[2,2,4,512]{3,2,1,0:T(4,128)S(1)}, bf16[2,1024,3,256]{1,3,2,0:T(8,128)(2,1)}, bf16[2,...) while((s32[]{:T(128)}, ...), condition=%wide.region_16.17_spmd, body=%wide.region_12.16_spmd.sunk | while | flops 1382021632 | bytes 187022096 | solution.py:228
  357.0 47.1 %while.54 = (s32[]{:T(128)}, f32[1024,4,64]{0,2,1:T(8,128)S(1)}, f32[1024,4,64]{0,2,1:T(8,128)}, bf16[2,512,256]{1,2,0:T(8,128)(2,1)}, s32[2]{0:T(128)S(1)}, /*i...) while((s32[]{:T(128)}, f32[1024,4,64]{0,2,1:T(8,128)S(1)}, ...), condition=%wide.region_15.15_spmd.clone, body=%wide.region_13.14_spmd.clone.sunk | while | flops 1376778752 | bytes 164960704 | solution.py:117
  410.4 47.1 %while.54 = (s32[]{:T(128)}, f32[1024,4,64]{0,2,1:T(8,128)S(1)}, f32[1024,4,64]{0,2,1:T(8,128)}, bf16[2,512,256]{1,2,0:T(8,128)(2,1)}, s32[2]{0:T(128)S(1)}, /*i...) while((s32[]{:T(128)}, f32[1024,4,64]{0,2,1:T(8,128)S(1)}, ...), condition=%wide.region_15.15_spmd.clone, body=%wide.region_13.14_spmd.clone.sunk | while | flops 1376778752 | bytes 164960704 | solution.py:117
  468.9 39.6 %all_to_all.69 = bf16[2,1024,3,256]{3,0,2,1:T(2,128)(2,1)S(1)} all-to-all(bf16[2,1024,3,256]{3,0,2,1:T(2,128)(2,1)S(1)} %copy.92), channel_id=1, replica_groups=mesh['dp'=8,'seq'=4] {'seq'}, dimensions={1} | all-to-all | bytes 6291456 | tf_op jit(solution)/shard_map/all_to_all | solution.py:229
  514.5 10.3 convolution_bitcast_fusion.2
  526.4 11.1 %convolution_bitcast_fusion.1 = f32[1024,4096]{1,0:T(8,128)} fusion(bf16[2,256,4096]{2,1,0:T(8,128)(2,1)} %copy-done.51, f32[2,256,1024]{2,1,0:T(8,128)S(1)} %copy-done.14, f32[1024]{0:T(1024)S(1)} %copy-done.43, f32[1024]{0:T(1024)S(1)} %copy-done.30, f32[2,256]{1,0:T(2,128)S(1)} %copy-done.35, f32[2,256]{1,0:T(2,128)S(1)} %copy-done.22), kind=kOutput, calls=%fused_computation.62 | convolution fusion | flops 4297588736 | bytes 23080960 | tf_op jit(solution)/shard_map/rtk,rtn->kn/dot_general | solution.py:41
  538.8 17.1 %convolution_bitcast_fusion = f32[4096,1024]{1,0:T(8,128)} fusion(bf16[2,256,1024]{2,1,0:T(8,128)(2,1)S(1)} %copy-done.19, f32[2,256,4096]{2,1,0:T(8,128)} %fusion.50, f32[4096]{0:T(1024)S(1)} %bitcast.217), kind=kOutput, calls=%fused_computation.61 | convolution fusion | flops 4317511680 | bytes 26230784 | tf_op jit(solution)/shard_map/rtk,rtn->kn/dot_general | solution.py:41
  556.5 13.3 %add_convert_fusion.1 = bf16[2,256,1024]{2,1,0:T(8,128)(2,1)} fusion(f32[2,256,1024]{2,1,0:T(8,128)S(1)} %copy-done.14, bf16[4096,1024]{1,0:T(8,128)(2,1)} %all-gather.12.cloned.1.call-done, f32[1024]{0:T(1024)S(1)} %convert_element_type.171, f32[2,256,4096]{2,1,0:T(8,128)} %fusion.50, f32[4096]{0:T(1024)S(1)} %bitcast.218), kind=kOutput, calls=%fused_computation.119 | convolution fusion | flops 4318035968 | bytes 19943424 | tf_op jit(solution)/shard_map/rtk,kn->rtn/dot_general | solution.py:37
  570.2 8.5 fusion.72
  578.7 44.0 %all-reduce.15 = (f32[1024]{0:T(1024)S(1)}, f32[1024]{0:T(1024)S(1)}, f32[2048]{0:T(1024)S(1)}, f32[1024]{0:T(1024)S(1)}, f32[1024]{0:T(1024)S(1)}, /*index=5*/f...) all-reduce(f32[1024]{0:T(1024)S(1)} %get-tuple-element.250, ...), channel_id=2, replica_groups=mesh['dp'=8,'seq'=4] {'dp','seq'}, use_global_device_ids=true, to_apply=%region_20.21.clone | all-reduce | flops 12288 | bytes 98304
  631.0 49.4 %reduce-scatter.5.cloned.1.call-done = f32[32,3072]{1,0:T(8,128)} async-done(((f32[1024,3072]{1,0:T(8,128)}), f32[32,3072]{1,0:T(8,128)}) %reduce-scatter.5.cloned.1.call-update) | async-done | bytes 393232 | tf_op jit(solution)/shard_map/reduce_scatter | solution.py:258
  680.3 184.8 %reduce-scatter.9.cloned.1.call-done = f32[32,4096]{1,0:T(8,128)} async-done(((f32[1024,4096]{1,0:T(8,128)}), f32[32,4096]{1,0:T(8,128)}) %reduce-scatter.9.cloned.1.call-update) | async-done | bytes 524304 | tf_op jit(solution)/shard_map/reduce_scatter | solution.py:241
  865.2 187.5 %reduce-scatter.11.cloned.1.call-done = f32[128,1024]{1,0:T(8,128)} async-done(((f32[4096,1024]{1,0:T(8,128)}), f32[128,1024]{1,0:T(8,128)}) %reduce-scatter.11.cloned.1.call-update) | async-done | bytes 524304 | tf_op jit(solution)/shard_map/reduce_scatter | solution.py:243
  (385 shorter events, 245.9 us)
Async XLA Ops:
  7.2 55.2 %copy-start.9 = (bf16[2,256,1024]{2,1,0:T(8,128)(2,1)S(1)}, bf16[2,256,1024]{2,1,0:T(8,128)(2,1)}, u32[]{:S(2)}) copy-start(bf16[2,256,1024]{2,1,0:T(8,128)(2,1)} %param.23) | copy-start | bytes 3145732
  7.2 76.5 %all-gather.6.cloned.1.call-start = ((), (), s32[]{:S(2)}) async-start(), calls=%async_computation.8 | async-start | bytes 6488064 | tf_op jit(solution)/shard_map/all_gather | solution.py:165
  9.0 250.6 %all-gather.8.cloned.1.call-start = ((), (), s32[]{:S(2)}) async-start(), calls=%async_computation.9 | async-start | bytes 2162688 | tf_op jit(solution)/shard_map/all_gather | solution.py:167
  10.7 252.7 %all-gather.10.cloned.1.call-start = ((), (), s32[]{:S(2)}) async-start(), calls=%async_computation.10 | async-start | bytes 8650752 | tf_op jit(solution)/shard_map/all_gather | solution.py:171
  60.9 22.8 %copy-start.40 = (f32[1024]{0:T(1024)}, f32[1024]{0:T(1024)S(1)}, u32[]{:S(2)}) copy-start(f32[1024]{0:T(1024)S(1)} %convert_element_type.151) | copy-start | bytes 12292
  60.9 22.8 %copy-start.27 = (f32[1024]{0:T(1024)}, f32[1024]{0:T(1024)S(1)}, u32[]{:S(2)}) copy-start(f32[1024]{0:T(1024)S(1)} %convert_element_type.149) | copy-start | bytes 12292
  62.4 21.3 %copy-start.23 = (f32[2,256]{1,0:T(2,128)}, f32[2,256]{1,0:T(2,128)S(1)}, u32[]{:S(2)}) copy-start(f32[2,256]{1,0:T(2,128)S(1)} %broadcast_multiply_fusion.5) | copy-start | bytes 6148
  99.6 46.1 %all-to-all-start = ((bf16[2,256,3,1024]{1,0,2,3:T(2,128)(2,1)}), bf16[2,256,3,1024]{1,0,2,3:T(2,128)(2,1)S(1)}, u32[]{:S(2)}, u32[]{:S(2)}) async-start(bf16[2,256,3,1024]{1,0,2,3:T(2,128)(2,1)} %copy.83), calls=%async_computation | async-start | bytes 6291456 | tf_op jit(solution)/shard_map/all_to_all | solution.py:183
  103.3 202.6 %all-gather.12.cloned.1.call-start = ((), (), s32[]{:S(2)}) async-start(), calls=%async_computation.11 | async-start | bytes 8650752 | tf_op jit(solution)/shard_map/all_gather | solution.py:173
  207.7 51.9 %copy-start.10 = (bf16[2,256,1024]{2,1,0:T(8,128)(2,1)S(1)}, bf16[2,256,1024]{2,1,0:T(8,128)(2,1)}, u32[]{:S(2)}) copy-start(bf16[2,256,1024]{2,1,0:T(8,128)(2,1)} %param.23) | copy-start | bytes 3145732
  207.7 49.6 %all-to-all-start.1 = ((bf16[2,1024,256]{2,0,1:T(2,128)(2,1)}), bf16[2,1024,256]{2,0,1:T(2,128)(2,1)S(1)}, u32[]{:S(2)}, u32[]{:S(2)}) async-start(bf16[2,1024,256]{2,0,1:T(2,128)(2,1)} %copy.87), calls=%async_computation.1 | async-start | bytes 2097152 | tf_op jit(solution)/shard_map/all_to_all | solution.py:189
  211.4 52.0 %copy-start.42 = (f32[1024]{0:T(1024)}, f32[1024]{0:T(1024)S(1)}, u32[]{:S(2)}) copy-start(f32[1024]{0:T(1024)S(1)} %convert_element_type.163) | copy-start | bytes 12292
  211.4 114.0 %copy-start.29 = (f32[1024]{0:T(1024)}, f32[1024]{0:T(1024)S(1)}, u32[]{:S(2)}) copy-start(f32[1024]{0:T(1024)S(1)} %convert_element_type.161) | copy-start | bytes 12292
  257.2 48.6 %copy-start.32 = (f32[32,1,128]{2,1,0:T(1,128)}, f32[32,1,128]{2,1,0:T(1,128)S(1)}, u32[]{:S(2)}) copy-start(f32[32,1,128]{2,1,0:T(1,128)S(1)} %convert_element_type.183) | copy-start | bytes 49156
  262.9 62.5 %copy-start.13 = (f32[2,256,1024]{2,1,0:T(8,128)}, f32[2,256,1024]{2,1,0:T(8,128)S(1)}, u32[]{:S(2)}) copy-start(f32[2,256,1024]{2,1,0:T(8,128)S(1)} %get-tuple-element.349) | copy-start | bytes 6291460
  263.0 62.5 %copy-start.21 = (f32[2,256]{1,0:T(2,128)}, f32[2,256]{1,0:T(2,128)S(1)}, u32[]{:S(2)}) copy-start(f32[2,256]{1,0:T(2,128)S(1)} %broadcast_multiply_fusion.4) | copy-start | bytes 6148
  263.3 62.1 %copy-start.34 = (f32[2,256]{1,0:T(2,128)}, f32[2,256]{1,0:T(2,128)S(1)}, u32[]{:S(2)}) copy-start(f32[2,256]{1,0:T(2,128)S(1)} %add_rsqrt_fusion) | copy-start | bytes 6148
  263.3 42.5 %copy-start.18 = (bf16[2,256,1024]{2,1,0:T(8,128)(2,1)S(1)}, bf16[2,256,1024]{2,1,0:T(8,128)(2,1)}, u32[]{:S(2)}) copy-start(bf16[2,256,1024]{2,1,0:T(8,128)(2,1)} %param.37) | copy-start | bytes 3145732
  331.8 19.7 %all-to-all-start.2 = ((bf16[2,256,1024]{1,0,2:T(2,128)(2,1)}), bf16[2,256,1024]{1,0,2:T(2,128)(2,1)S(1)}, u32[]{:S(2)}, u32[]{:S(2)}) async-start(bf16[2,256,1024]{1,0,2:T(2,128)(2,1)} %copy.89), calls=%async_computation.2 | async-start | bytes 2097152 | tf_op jit(solution)/shard_map/all_to_all | solution.py:223
  335.4 295.6 %reduce-scatter.7.cloned.1.call-start = ((), (), s32[]{:S(2)}) async-start(), calls=%async_computation.13 | async-start | bytes 4325376 | tf_op jit(solution)/shard_map/reduce_scatter | solution.py:260
  340.0 340.3 %reduce-scatter.5.cloned.1.call-start = ((), (), s32[]{:S(2)}) async-start(), calls=%async_computation.12 | async-start | bytes 12976128 | tf_op jit(solution)/shard_map/reduce_scatter | solution.py:258
  524.9 340.3 %reduce-scatter.9.cloned.1.call-start = ((), (), s32[]{:S(2)}) async-start(), calls=%async_computation.14 | async-start | bytes 17301504 | tf_op jit(solution)/shard_map/reduce_scatter | solution.py:241
  537.5 515.2 %reduce-scatter.11.cloned.1.call-start = ((), (), s32[]{:S(2)}) async-start(), calls=%async_computation.15 | async-start | bytes 17301504 | tf_op jit(solution)/shard_map/reduce_scatter | solution.py:243
  570.2 57.2 %copy-start.17 = (f32[2,256,1024]{2,1,0:T(8,128)S(1)}, f32[2,256,1024]{2,1,0:T(8,128)}, u32[]{:S(2)}) copy-start(f32[2,256,1024]{2,1,0:T(8,128)} %copy-done.15) | copy-start | bytes 6291460
  (62 other events, 276.6 us)
Sparse Core Ops, SparseCore 0:
  11.5 72.1 all-gather.5
  87.1 59.1 all-gather.7
  149.8 76.3 all-gather.9
  229.5 76.2 all-gather.11
  340.1 140.8 reduce-scatter.6
  525.0 155.3 reduce-scatter.4
  683.3 181.8 reduce-scatter.8
  868.1 184.4 reduce-scatter.10
where the time goes:
time: 1070 us; the launch traced here: 1060 us
  waiting for transfers between devices  526 us (49%)
  matrix products  182 us (17%)
  blocking collectives  172 us (16%)
  local copies, waits for them, and re-layouts  77.9 us (7%)
  other arithmetic  59.2 us (6%)
  loops' own time  16.4 us (2%)
  between operations  15 us (1%)
  starting transfers between devices  11.9 us (1%)
    reduce_scatter x1, waiting for transfers between devices, body(): lax.psum_scatter(d_w_down, ('dp', 'seq'), scatter_dimension=0, tiled=True)  187 us
    reduce_scatter x1, waiting for transfers between devices, body(): lax.psum_scatter(d_w_up, ('dp', 'seq'), scatter_dimension=0, tiled=True)  185 us
    unnamed x2, blocking collectives  86.3 us
    reduce_scatter x1, waiting for transfers between devices, body(): lax.psum_scatter(d_w_qkv, ('dp', 'seq'), scatter_dimension=0, tiled=True)  49.4 us
    all_gather x1, blocking collectives, body(): lax.all_gather(half(bias_up), ('dp', 'seq'), axis=0, tiled=True)  45.8 us
    dot_general x4, matrix products, weight_grad(): jnp.einsum('rtk,rtn->kn', left, right, preferred_element_type=jnp.float32)  43.1 us
    all_to_all x1, waiting for transfers between devices, body(): lax.all_to_all(mixed, 'seq', split_axis=3, concat_axis=1, tiled=True)  40 us
    all_to_all x1, blocking collectives, body(): lax.all_to_all(grad_packed, 'seq', split_axis=1, concat_axis=3, tiled=True)  39.6 us
  transfers between devices with their start and end apart: 11, of which 7 were waited for; matrix products, arithmetic and copies ran while one was open for 26% of the time, Pallas kernels for 0%

commit v1 on v0

v1 whole, which is shorter than its diff:
```python
import jax
import jax.numpy as jnp
from jax import lax
from jax.experimental import pallas as pl
from jax.experimental.pallas import tpu as pltpu
from jax.sharding import Mesh, PartitionSpec as P

H = 16
LAYERS = 24
EPSILON = 1e-05
DOC_MAX = 512

BF = jnp.bfloat16
F32 = jnp.float32


def half(values):
    return values.astype(BF)


def norm_parts(values):
    mean = jnp.mean(values, axis=-1, keepdims=True)
    centred = values - mean
    spread = jnp.mean(centred * centred, axis=-1, keepdims=True)
    inverse = lax.rsqrt(spread + EPSILON)
    return (centred * inverse, inverse)


def norm_back(grad_out, normal, inverse, gain):
    scaled = grad_out * gain
    return inverse * (
        scaled
        - jnp.mean(scaled, axis=-1, keepdims=True)
        - normal * jnp.mean(scaled * normal, axis=-1, keepdims=True)
    )


def dot(left, right, contract):
    return lax.dot_general(left, right, ((contract[:1], contract[1:]), ((), ())), preferred_element_type=F32)


def shift(value, axis, step):
    size = lax.axis_size(axis)
    return lax.ppermute(value, axis, [(i, (i + step) % size) for i in range(size)])


def in_order(parts, axis):
    size = len(parts)
    here = lax.axis_index(axis)
    return [lax.select_n(lax.rem(here - place + size, size), *parts) for place in range(size)]


def gather_axis(value, axis, at):
    size = lax.axis_size(axis)
    parts = [value] + [shift(value, axis, k) for k in range(1, size)]
    return jnp.stack(in_order(parts, axis), axis=at)


def swap_axis(value, axis, at):
    size = lax.axis_size(axis)
    here = lax.axis_index(axis)
    parts = []
    for k in range(size):
        block = lax.dynamic_index_in_dim(value, lax.rem(here + k, size), at, keepdims=False)
        parts.append(shift(block, axis, k) if k else block)
    return in_order(parts, axis)


def reduce_axis(value, axis, at):
    size = lax.axis_size(axis)
    here = lax.axis_index(axis)
    total = lax.dynamic_index_in_dim(value, here, at, keepdims=False).astype(F32)
    for k in range(1, size):
        block = lax.dynamic_index_in_dim(value, lax.rem(here + k, size), at, keepdims=False)
        total = total + shift(half(block), axis, k).astype(F32)
    return total


def gather_pair(first, second):
    rows = first.shape[0]
    both = gather_axis(jnp.concatenate([first, second], axis=0), "z", 0)
    first, second = both[:, :rows], both[:, rows:]
    first = gather_axis(gather_axis(first, "g", 1), "y", 1)
    second = gather_axis(gather_axis(second, "y", 1), "g", 2)
    return first, second


def reduce_pair(first, second):
    rows = first.shape[3]
    first = half(reduce_axis(first, "g", 2))
    second = half(reduce_axis(second, "y", 1))
    first = reduce_axis(first, "y", 1)
    second = reduce_axis(second, "g", 1)
    both = reduce_axis(jnp.concatenate([first, second], axis=1), "z", 0)
    return both[:rows], both[rows:]


def spans(length, block):
    for start in range(0, length, block):
        low = max(0, start - DOC_MAX)
        yield start, low, start + block - low


def hidden_part(docs_q, docs_k, start, low, block, width):
    key_pos = low + lax.broadcasted_iota(jnp.int32, (width, block), 0)
    query_pos = start + lax.broadcasted_iota(jnp.int32, (width, block), 1)
    return (docs_k == docs_q) & (key_pos <= query_pos)


def attend_kernel(block, head_dim, q_ref, k_ref, v_ref, docs_row_ref, docs_col_ref, out_ref, log_ref):
    length, lanes = q_ref.shape
    heads = lanes // head_dim
    v_t = v_ref[...].T
    for start, low, width in spans(length, block):
        visible = hidden_part(
            docs_row_ref[:, start : start + block], docs_col_ref[low : low + width], start, low, block, width
        )
        q = q_ref[start : start + block] * (head_dim ** (-0.5))
        lane = lax.broadcasted_iota(jnp.int32, q.shape, 1) // head_dim
        outs = []
        for head in range(heads):
            q_head = jnp.where(lane == head, q, jnp.zeros_like(q))
            scores = dot(k_ref[low : low + width], q_head, (1, 1))
            scores = jnp.where(visible, scores, -1e30)
            top = jnp.max(scores, axis=0, keepdims=True)
            exponent = jnp.exp(scores - top)
            total = jnp.sum(exponent, axis=0, keepdims=True)
            probs = half(exponent * (1.0 / total))
            outs.append(dot(v_t[head * head_dim : (head + 1) * head_dim, low : low + width], probs, (1, 0)))
            log_ref[0, head : head + 1, start : start + block] = top + jnp.log(total)
        out_ref[start : start + block] = half(jnp.concatenate(outs, axis=0).T)


def attend_back_kernel(
    block, head_dim, q_ref, k_ref, v_ref, g_ref, log_ref, docs_row_ref, docs_col_ref, dq_ref, dk_ref, dv_ref, key_sum, value_sum
):
    length, lanes = q_ref.shape
    heads = lanes // head_dim
    scale = head_dim ** (-0.5)
    k_t = k_ref[...].T
    key_sum[...] = jnp.zeros_like(key_sum)
    value_sum[...] = jnp.zeros_like(value_sum)
    for start, low, width in spans(length, block):
        visible = hidden_part(
            docs_row_ref[:, start : start + block], docs_col_ref[low : low + width], start, low, block, width
        )
        q = q_ref[start : start + block] * scale
        g = g_ref[start : start + block]
        lane = lax.broadcasted_iota(jnp.int32, q.shape, 1) // head_dim
        dq, dk, dv = [], 0.0, 0.0
        for head in range(heads):
            q_head = jnp.where(lane == head, q, jnp.zeros_like(q))
            g_head = jnp.where(lane == head, g, jnp.zeros_like(g))
            scores = dot(k_ref[low : low + width], q_head, (1, 1))
            scores = jnp.where(visible, scores, -1e30)
            probs = jnp.exp(scores - log_ref[0, head : head + 1, start : start + block])
            grad_probs = dot(v_ref[low : low + width], g_head, (1, 1))
            delta = jnp.sum(grad_probs * probs, axis=0, keepdims=True)
            grad_scores = half(probs * (grad_probs - delta))
            dq.append(dot(k_t[head * head_dim : (head + 1) * head_dim, low : low + width], grad_scores, (1, 0)))
            dk = dk + dot(grad_scores, q_head, (1, 0))
            dv = dv + dot(half(probs), g_head, (1, 0))
        dq_ref[start : start + block] = half((jnp.concatenate(dq, axis=0) * scale).T)
        key_sum[low : low + width] += dk
        value_sum[low : low + width] += dv
    dk_ref[...] = half(key_sum[...])
    dv_ref[...] = half(value_sum[...])


def attend_specs(length, lanes, steps):
    def column(offset):
        return pl.BlockSpec((length, lanes), lambda i: (0, offset * steps + i))

    whole_row = pl.BlockSpec((1, length), lambda i: (0, 0))
    whole_col = pl.BlockSpec((length, 1), lambda i: (0, 0))
    return column, whole_row, whole_col


def attend(qk, value, docs, head_dim):
    length, width = value.shape
    block = min(256, length)
    lanes = min(128, width)
    steps = width // lanes
    column, whole_row, whole_col = attend_specs(length, lanes, steps)
    logs = pl.BlockSpec((1, lanes // head_dim, length), lambda i: (i, 0, 0))

    def kernel(*refs):
        attend_kernel(block, head_dim, *refs)

    return pl.pallas_call(
        kernel,
        grid=(steps,),
        in_specs=[column(0), column(1), column(0), whole_row, whole_col],
        out_specs=[column(0), logs],
        out_shape=[
            jax.ShapeDtypeStruct((length, width), BF),
            jax.ShapeDtypeStruct((steps, lanes // head_dim, length), F32),
        ],
        compiler_params=pltpu.CompilerParams(vmem_limit_bytes=48 << 20),
        name="attend",
    )(qk, qk, value, docs[None], docs[:, None])


def attend_back(qk, value, grad_out, logs, docs, head_dim):
    length, width = value.shape
    block = min(256, length)
    lanes = min(128, width)
    steps = width // lanes
    column, whole_row, whole_col = attend_specs(length, lanes, steps)
    logs_spec = pl.BlockSpec((1, lanes // head_dim, length), lambda i: (i, 0, 0))

    def kernel(*refs):
        attend_back_kernel(block, head_dim, *refs)

    shape = jax.ShapeDtypeStruct((length, width), BF)
    return pl.pallas_call(
        kernel,
        grid=(steps,),
        in_specs=[column(0), column(1), column(0), column(0), logs_spec, whole_row, whole_col],
        out_specs=[column(0), column(0), column(0)],
        out_shape=[shape, shape, shape],
        scratch_shapes=[pltpu.VMEM((length, lanes), F32), pltpu.VMEM((length, lanes), F32)],
        compiler_params=pltpu.CompilerParams(vmem_limit_bytes=48 << 20),
        name="attend_back",
    )(qk, qk, value, grad_out, logs, docs[None], docs[:, None])


def gelu_parts(u):
    c = 0.7978845608028654
    inner = jnp.tanh(c * (u + 0.044715 * (u * u * u)))
    value = 0.5 * u * (1.0 + inner)
    slope = 0.5 * (1.0 + inner) + 0.5 * u * (1.0 - inner * inner) * (c * (1.0 + 3 * 0.044715 * (u * u)))
    return value, slope


def body(
    block_input,
    doc_ids,
    gain_attn,
    shift_attn,
    w_qkv,
    bias_qv,
    w_proj,
    bias_proj,
    gain_mlp,
    shift_mlp,
    w_up,
    bias_up,
    w_down,
    bias_down,
    out_grad,
):
    zs, ys, gs, ts = (lax.axis_size(a) for a in ("z", "y", "g", "t"))
    blocks = zs * ys * gs
    t = lax.axis_index("t")
    g = lax.axis_index("g")
    depth = LAYERS ** (-0.5)
    rows, local, width = block_input.shape
    length = doc_ids.shape[1]
    shard = w_qkv.shape[0]
    part = width // ts
    head_dim = width // H
    hidden_width = w_up.shape[1]
    ff_shard = w_down.shape[0]
    ff_half = ff_shard // 2
    ff_part = hidden_width // ts // 2
    own = gs * local

    docs = lax.dynamic_index_in_dim(doc_ids, g, 0, keepdims=False)

    x_own = jnp.stack(swap_axis(block_input, "g", 0), axis=0)
    x_all = gather_axis(x_own, "t", 1).reshape(length, width)
    grad_own = jnp.stack(swap_axis(out_grad, "g", 0), axis=0).astype(F32)
    grad_down_own = half(depth * grad_own)
    grad_down = gather_axis(grad_down_own, "t", 1).reshape(length, width)

    vectors = [gain_attn, shift_attn, bias_qv, bias_proj, gain_mlp, shift_mlp, bias_up, bias_down]
    sizes = [v.shape[0] for v in vectors]
    packed = half(jnp.concatenate(vectors))
    count = packed.shape[0]
    w_q, w_k, w_v = (w.reshape(shard, ts, part) for w in jnp.split(half(w_qkv), 3, axis=1))
    w_o = half(w_proj).reshape(shard, ts, part)
    w_u = half(w_up).reshape(shard, blocks, ts, 2, ff_half)
    w_u = [w_u[:, :, :, i].transpose(0, 2, 1, 3).reshape(shard, ts, ff_part) for i in range(2)]
    columns = jnp.concatenate([w_q, w_k, w_v, w_o, *w_u], axis=2)
    columns = jnp.concatenate(swap_axis(columns, "t", 1), axis=0)
    packed_all = jnp.concatenate([gather_axis(packed, "t", 0).reshape(-1), jnp.zeros((2 * part - ts * count,), BF)])
    extra = 8
    shard_qk = jnp.concatenate(
        [columns[:, : 2 * part], jnp.broadcast_to(packed_all[None], (extra, 2 * part))], axis=0
    )
    shard_vo = columns[:, 2 * part : 4 * part]
    shard_u1 = columns[:, 4 * part : 4 * part + ff_part]
    shard_u2 = columns[:, 4 * part + ff_part :]
    shard_d = half(w_down)

    full_qk, full_vo = gather_pair(shard_qk, shard_vo)
    full_u1, full_u2 = gather_pair(shard_u1, shard_u2)
    full_d1, full_d2 = gather_pair(shard_d[:ff_half], shard_d[ff_half:])

    vector_rows = full_qk[:, :, :, ts * shard, : ts * count].reshape(blocks, ts, count)
    offsets = [0]
    for size in sizes:
        offsets.append(offsets[-1] + size)
    pieces = [vector_rows[:, :, offsets[i] : offsets[i + 1]] for i in range(len(sizes))]
    h_gain_attn, h_shift_attn, h_bias_qv, h_bias_proj, h_gain_mlp, h_shift_mlp = (
        p.reshape(-1).astype(F32) for p in pieces[:6]
    )
    h_bias_down = pieces[7].reshape(-1).astype(F32)
    h_bias_up = lax.dynamic_index_in_dim(pieces[6], t, 1, keepdims=False).astype(F32)
    h_bias_up = h_bias_up.reshape(blocks, 2, ff_half)
    h_bias_up = [h_bias_up[:, i].reshape(-1) for i in range(2)]
    bias_q = lax.dynamic_slice_in_dim(h_bias_qv, t * part, part)
    bias_v = lax.dynamic_slice_in_dim(h_bias_qv, width + t * part, part)
    wqk = full_qk[:, :, :, : ts * shard].reshape(width, 2 * part)
    wvo = full_vo.reshape(width, 2 * part)
    wv = wvo[:, :part]
    wo = jnp.concatenate(
        in_order(
            [wvo[:, part:]] + [shift(wvo[:, part:], "t", k) for k in range(1, ts)],
            "t",
        ),
        axis=1,
    )
    wu = [full_u1.reshape(width, ff_part), full_u2.reshape(width, ff_part)]
    wd = [full_d1.reshape(ff_part, width), full_d2.reshape(ff_part, width)]

    normal_all, _ = norm_parts(x_all.astype(F32))
    normed_attn = half(normal_all * h_gain_attn + h_shift_attn)
    qk = half(dot(normed_attn, wqk, (1, 0)) + jnp.concatenate([bias_q, jnp.zeros((part,), F32)]))
    value = half(dot(normed_attn, wv, (1, 0)) + bias_v)
    attended_heads, logs = attend(qk, value, docs, head_dim)
    attended = jnp.concatenate(swap_axis(attended_heads.reshape(gs, ts, local, part), "t", 1), axis=-1)
    attended = attended.reshape(own, width)
    x_flat = x_own.reshape(own, width).astype(F32)
    hidden = x_flat + depth * (dot(attended, wo, (1, 0)) + h_bias_proj)
    normal_two, inverse_two = norm_parts(hidden)
    normed_own = half(normal_two * h_gain_mlp + h_shift_mlp)
    normed_mlp = gather_axis(normed_own.reshape(gs, local, width), "t", 1).reshape(length, width)
    lowered = 0.0
    grad_up, d_down, d_bias_up = [], [], []
    actives, slopes = [], []
    for i in range(2):
        upward = dot(normed_mlp, wu[i], (1, 0)) + h_bias_up[i]
        active, slope = gelu_parts(upward)
        active = half(active)
        actives.append(active)
        slopes.append(slope)
        d_down.append(half(dot(active, grad_down, (0, 0))).reshape(zs, ys, gs, ff_half, width))
    sum_d1, sum_d2 = reduce_pair(*d_down)
    for i in range(2):
        grad_up.append(half(dot(grad_down, wd[i], (1, 1)) * slopes[i]))
        d_bias_up.append(jnp.sum(grad_up[i], axis=0, dtype=F32))
    d_up = [half(dot(normed_mlp, grad_up[i], (0, 0))).reshape(zs, ys, gs, ts * shard, ff_part) for i in range(2)]
    sum_u = reduce_pair(*d_up)
    e2 = dot(grad_up[0], wu[0], (1, 1)) + dot(grad_up[1], wu[1], (1, 1))
    e2 = reduce_axis(e2.reshape(gs, ts, local, width), "t", 1).reshape(own, width)
    lowered = dot(actives[0], wd[0], (1, 0)) + dot(actives[1], wd[1], (1, 0))
    lowered = reduce_axis(lowered.reshape(gs, ts, local, width), "t", 1).reshape(own, width)
    block_out = half(hidden + depth * (lowered + h_bias_down)).reshape(gs, local, width)
    block_out = jnp.stack(swap_axis(block_out, "g", 0), axis=0)

    d_gain_mlp = jnp.sum(e2 * normal_two, axis=0)
    d_shift_mlp = jnp.sum(e2, axis=0)
    grad_hidden = grad_own.reshape(own, width) + norm_back(e2, normal_two, inverse_two, h_gain_mlp)
    grad_branch = half(depth * grad_hidden)
    d_bias_proj = jnp.sum(grad_branch, axis=0, dtype=F32)
    d_proj = dot(attended, grad_branch, (0, 0))
    d_proj = reduce_axis(d_proj.reshape(width, ts, part), "t", 1)
    grad_attended = half(dot(grad_branch, wo, (1, 1))).reshape(own, ts, part)
    grad_attended = jnp.stack(
        [p.reshape(gs, local, part) for p in swap_axis(grad_attended, "t", 1)], axis=1
    ).reshape(length, part)
    dq, dk, dv = attend_back(qk, value, grad_attended, logs, docs, head_dim)
    d_qk = jnp.concatenate([dq, dk], axis=1)
    e1 = dot(d_qk, wqk, (1, 1)) + dot(dv, wv, (1, 1))
    e1 = reduce_axis(e1.reshape(gs, ts, local, width), "t", 1).reshape(own, width)
    normal_one, inverse_one = norm_parts(x_flat)
    d_gain_attn = jnp.sum(e1 * normal_one, axis=0)
    d_shift_attn = jnp.sum(e1, axis=0)
    grad_input = grad_hidden + norm_back(e1, normal_one, inverse_one, h_gain_attn)
    grad_input = half(grad_input).reshape(gs, local, width)
    grad_input = jnp.stack(swap_axis(grad_input, "g", 0), axis=0).astype(F32)

    def by_owner(full):
        return full.reshape(blocks, ts, -1)

    d_bias_q = jnp.sum(dq, axis=0, dtype=F32)
    d_bias_v = jnp.sum(dv, axis=0, dtype=F32)
    d_bias_qv = jnp.zeros((2 * width,), F32)
    d_bias_qv = lax.dynamic_update_slice_in_dim(d_bias_qv, d_bias_q, t * part, 0)
    d_bias_qv = lax.dynamic_update_slice_in_dim(d_bias_qv, d_bias_v, width + t * part, 0)
    d_bias_up = jnp.stack([d.reshape(blocks, ff_half) for d in d_bias_up], axis=1).reshape(blocks, 1, ff_shard)
    d_bias_up = jnp.where(lax.broadcasted_iota(jnp.int32, (blocks, ts, 1), 1) == t, d_bias_up, 0.0)
    d_bias_down = jnp.sum(grad_down_own, axis=(0, 1), dtype=F32)
    vector_sums = jnp.concatenate(
        [
            by_owner(d_gain_attn),
            by_owner(d_shift_attn),
            by_owner(d_bias_qv),
            by_owner(d_bias_proj),
            by_owner(d_gain_mlp),
            by_owner(d_shift_mlp),
            d_bias_up,
            by_owner(d_bias_down),
        ],
        axis=2,
    )
    vector_sums = reduce_axis(vector_sums, "t", 1)
    vector_sums = jnp.pad(half(vector_sums), ((0, 0), (0, 2 * part - count)))
    vector_sums = jnp.broadcast_to(vector_sums[:, None], (blocks, extra, 2 * part))
    d_wqk = half(dot(normed_attn, d_qk, (0, 0))).reshape(blocks, ts * shard, 2 * part)
    d_wqk = jnp.concatenate([d_wqk, vector_sums], axis=1).reshape(zs, ys, gs, ts * shard + extra, 2 * part)
    d_wv = half(dot(normed_attn, dv, (0, 0)))
    d_wvo = jnp.concatenate([d_wv, half(d_proj)], axis=1).reshape(zs, ys, gs, ts * shard, 2 * part)
    sum_qk, sum_vo = reduce_pair(d_wqk, d_wvo)
    vector_sums = sum_qk[ts * shard, :count]
    out_vectors = [vector_sums[offsets[i] : offsets[i + 1]] for i in range(len(sizes))]

    up = jnp.stack(sum_u, axis=0).reshape(2, ts, shard, blocks, ff_half)
    up = jnp.stack(swap_axis(up, "t", 1), axis=0)
    sum_up = up.transpose(2, 3, 0, 1, 4).reshape(shard, hidden_width)
    rest = jnp.concatenate([sum_qk[: ts * shard], sum_vo], axis=1).reshape(ts, shard, 4, part)
    rest = jnp.stack(swap_axis(rest, "t", 0), axis=2)
    sum_qkv = rest[:, :3].reshape(shard, 3 * width)
    sum_proj = rest[:, 3].reshape(shard, width)
    sum_down = jnp.concatenate([sum_d1, sum_d2], axis=0)
    return (
        block_out,
        grad_input,
        out_vectors[0],
        out_vectors[1],
        sum_qkv,
        out_vectors[2],
        sum_proj,
        out_vectors[3],
        out_vectors[4],
        out_vectors[5],
        sum_up,
        out_vectors[6],
        sum_down,
        out_vectors[7],
    )


def solution(mesh):
    rows = 2
    dp, seq = mesh.shape["dp"], mesh.shape["seq"]
    high = 4
    split = Mesh(mesh.devices.reshape(high, dp // high, rows, seq // rows), ("z", "y", "g", "t"))
    everything = ("z", "y", "g", "t")
    tokens = P(("z", "y"), ("g", "t"), None)
    vector = P(everything)
    matrix = P(everything, None)
    return jax.shard_map(
        body,
        mesh=split,
        in_specs=(
            tokens,
            P(("z", "y"), None),
            vector,
            vector,
            matrix,
            vector,
            matrix,
            vector,
            vector,
            vector,
            matrix,
            vector,
            matrix,
            vector,
            tokens,
        ),
        out_specs=(
            tokens,
            tokens,
            vector,
            vector,
            matrix,
            vector,
            matrix,
            vector,
            vector,
            vector,
            matrix,
            vector,
            matrix,
            vector,
        ),
        check_vma=False,
    )
```

time: 1070 us -> 474 us (0.44)
  waiting for transfers between devices: 526 us -> 112 us
  blocking collectives: 172 us -> 0 us
  matrix products: 182 us -> 54.3 us
  starting transfers between devices: 11.9 us -> 87.2 us
  Pallas kernels: 0 us -> 40.4 us
  other arithmetic: 59.2 us -> 90.4 us
  loops' own time: 16.4 us -> 0 us
  between operations: 15 us -> 3.43 us
    reduce_scatter x4 -> x0, waiting for transfers between devices: 422 us -> none  [the longest x1 187 us: body(): lax.psum_scatter(d_w_down, ('dp', 'seq'), scatter_dimension=0, tiled=True)]
    dot_general x40 -> x21, matrix products: 182 us -> 54.3 us  [dot(): lax.dot_general(left, right, ((contract[:1], contract[1:]), ((), ())), pr...]
    ppermute x0 -> x61, waiting for transfers between devices: none -> 112 us  [shift(): lax.ppermute(value, axis, [(i, (i + step) % size) for i in range(size)])]
    ppermute x0 -> x61, starting transfers between devices: none -> 87.2 us  [shift(): lax.ppermute(value, axis, [(i, (i + step) % size) for i in range(size)])]
    unnamed x2 -> x0, blocking collectives: 86.3 us -> none
    all_gather x4 -> x0, waiting for transfers between devices: 52.6 us -> none  [the longest x1 31.8 us: body(): lax.all_gather(half(w_down), ('dp', 'seq'), axis=0, tiled=True)]
    all_to_all x3 -> x0, waiting for transfers between devices: 51.5 us -> none  [the longest x1 40 us: body(): lax.all_to_all(mixed, 'seq', split_axis=3, concat_axis=1, tiled=True)]
    all_gather x1 -> x0, blocking collectives: 45.8 us -> none  [body(): lax.all_gather(half(bias_up), ('dp', 'seq'), axis=0, tiled=True)]
  transfers between devices with their start and end apart: 11 -> 61, of which waited for: 7 -> 14; matrix products, arithmetic and copies ran while one was open for 26% -> 38% of each run, Pallas kernels for 0% -> 9%
where the time goes in v1:
time: 474 us; the launch traced here: 466 us
  waiting for transfers between devices  112 us (24%)
  other arithmetic  90.4 us (19%)
  starting transfers between devices  87.2 us (18%)
  local copies, waits for them, and re-layouts  78.1 us (16%)
  matrix products  54.3 us (11%)
  Pallas kernels  40.4 us (9%)
    ppermute x61, waiting for transfers between devices, shift(): lax.ppermute(value, axis, [(i, (i + step) % size) for i in range(size)])  112 us
    ppermute x61, starting transfers between devices, shift(): lax.ppermute(value, axis, [(i, (i + step) % size) for i in range(size)])  87.2 us
    dot_general x21, matrix products, dot(): lax.dot_general(left, right, ((contract[:1], contract[1:]), ((), ())), pr...  54.3 us
    another operation x34, other arithmetic, gather_axis(): return jnp.stack(in_order(parts, axis), axis=at)  25.3 us
    pallas_call x1, Pallas kernels, attend_back(): pl.pallas_call(kernel, grid=(steps,), in_specs=[column(0), column(1), col...  21.4 us
    convert_element_type x18, other arithmetic, half(): return values.astype(BF)  21.4 us
    pallas_call x1, Pallas kernels, attend(): pl.pallas_call(kernel, grid=(steps,), in_specs=[column(0), column(1), col...  18.9 us
    unnamed x242, local copies, waits for them, and re-layouts  16.4 us
  transfers between devices with their start and end apart: 61, of which 14 were waited for; matrix products, arithmetic and copies ran while one was open for 38% of the time, Pallas kernels for 9%

profile of v1, /device:TPU:0, one launch (start us, length us, event | category | flops | bytes accessed | tf_op | source)
XLA Modules:
  0.0 465.5 jit_solution(10753053358660744400)
XLA Ops:
  21.3 4.0 collective-permute-start.14
  27.3 14.9 %collective-permute-start.16 = (bf16[128,1024]{1,0:T(8,128)(2,1)S(1)}, bf16[128,1024]{1,0:T(8,128)(2,1)S(1)}, u32[]{:S(2)}, u32[]{:S(2)}) collective-permute-start(bf16[128,1024]{1,0:T(8,128)(2,1)S(1)} %fusion.106), channel_id=1, source_target_pairs={{0,24},{8,0},{16,8},{24,16},{1,25},{9,1},{17,9},{25,17},{2,26},{10... | collective-permute-start | bytes 786440 | tf_op jit(solution)/shard_map/ppermute | solution.py:44
  62.2 9.4 %collective-permute-done.5 = bf16[136,1024]{1,0:T(8,128)(2,1)} collective-permute-done((bf16[136,1024]{1,0:T(8,128)(2,1)}, bf16[136,1024]{1,0:T(8,128)(2,1)}, u32[]{:S(2)}, u32[]{:S(2)}) %collective-permute-start.5) | collective-permute-done | bytes 278560 | tf_op jit(solution)/shard_map/ppermute | solution.py:44
  83.3 3.1 collective-permute-done.24
  90.4 7.2 %collective-permute-done.9 = bf16[4,64,1024]{2,1,0:T(8,128)(2,1)S(1)} collective-permute-done((bf16[4,64,1024]{2,1,0:T(8,128)(2,1)S(1)}, bf16[4,64,1024]{2,1,0:T(8,128)(2,1)S(1)}, u32[]{:S(2)}, u32[]{:S(2)}) %collective-permute-start.9) | collective-permute-done | bytes 524320 | tf_op jit(solution)/shard_map/ppermute | solution.py:44
  108.1 38.3 %collective-permute-done.10 = bf16[4,2,64,1024]{3,2,0,1:T(8,128)(2,1)S(1)} collective-permute-done((bf16[4,2,64,1024]{3,2,0,1:T(8,128)(2,1)S(1)}, bf16[4,2,64,1024]{3,2,0,1:T(8,128)(2,1)S(1)}, u32[]{:S(2)}, u32[]{:S(2)}) %collective-permute-start.10) | collective-permute-done | bytes 1048608 | tf_op jit(solution)/shard_map/ppermute | solution.py:44
  152.6 3.1 pad_maximum_fusion
  164.7 18.9 %attend.1 = (bf16[1024,512]{1,0:T(8,128)(2,1)S(1)}, f32[4,2,1024]{2,1,0:T(2,128)S(1)}) custom-call(bf16[1024,1024]{1,0:T(8,128)(2,1)S(1)} %add_convert_fusion.refs_0_.refs_1_, bf16[1024,1024]{1,0:T(8,128)(2,1)S(1)} %add_convert_fusion.refs_0_.refs_1_, bf16[1024,512]{1,0:T(8,128)(2,1)S(1)} %add_convert_fusion.3.refs_2_, ...), custom_call_target="tpu_custom_call" | custom-call | tf_op jit(solution)/shard_map/attend/pallas_call | solution.py:190
  209.3 3.1 convolution_convert_fusion.1
  212.4 4.9 %convert_reduce_fusion.1 = (f32[1024]{0:T(1024)S(1)}, bf16[1024,1024]{1,0:T(8,128)(2,1)S(1)}) fusion(f32[1024,1024]{1,0:T(8,128)S(1)} %fusion.138, f32[1024]{0:T(1024)S(1)} %add.525, bf16[1024,1024]{1,0:T(8,128)(2,1)S(1)} %bitcast.559, bf16[1024,1024]{1,0:T(8,128)(2,1)S(1)} %bitcast.564), kind=kOutput, calls=%fused_computation.30 | convolution fusion | flops 2169502720 | bytes 10493952 | tf_op jit(solution)/shard_map/dot_general | solution.py:39
  227.3 3.1 convolution_convert_fusion
  236.9 4.9 %convert_reduce_fusion = (f32[1024]{0:T(1024)S(1)}, bf16[1024,1024]{1,0:T(8,128)(2,1)S(1)}) fusion(f32[1024,1024]{1,0:T(8,128)S(1)} %fusion.139, f32[1024]{0:T(1024)S(1)} %add.530, bf16[1024,1024]{1,0:T(8,128)(2,1)S(1)} %bitcast.561, bf16[1024,1024]{1,0:T(8,128)(2,1)S(1)} %bitcast.562), kind=kOutput, calls=%fused_computation.29 | convolution fusion | flops 2169502720 | bytes 10493952 | tf_op jit(solution)/shard_map/dot_general | solution.py:39
  254.3 4.5 convolution_add_fusion.1
  267.9 12.9 %collective-permute-done.48 = bf16[4,2,64,1024]{3,2,0,1:T(8,128)(2,1)} collective-permute-done((bf16[4,2,64,1024]{3,2,0,1:T(8,128)(2,1)}, bf16[4,2,64,1024]{3,2,0,1:T(8,128)(2,1)}, u32[]{:S(2)}, u32[]{:S(2)}) %collective-permute-start.48) | collective-permute-done | bytes 1048608 | tf_op jit(solution)/shard_map/ppermute | solution.py:44
  294.5 3.0 fusion.127
  315.5 5.9 %collective-permute-start.50 = (bf16[128,1024]{1,0:T(8,128)(2,1)}, bf16[128,1024]{1,0:T(8,128)(2,1)S(1)}, u32[]{:S(2)}, u32[]{:S(2)}) collective-permute-start(bf16[128,1024]{1,0:T(8,128)(2,1)} %get-tuple-element.52), channel_id=1, source_target_pairs={{0,8},{8,16},{16,24},{24,0},{1,9},{9,17},{17,25},{25,1},{2,10},{10... | collective-permute-start | bytes 786440 | tf_op jit(solution)/shard_map/ppermute | solution.py:44
  322.7 21.4 %attend_back.1 = (bf16[1024,512]{1,0:T(8,128)(2,1)S(1)}, bf16[1024,512]{1,0:T(8,128)(2,1)S(1)}, bf16[1024,512]{1,0:T(8,128)(2,1)S(1)}) custom-call(bf16[1024,1024]{1,0:T(8,128)(2,1)} %copy-done.2, bf16[1024,1024]{1,0:T(8,128)(2,1)} %copy-done.2, bf16[1024,512]{1,0:T(8,128)(2,1)S(1)} %copy-done.4, bf16[1024,512]{1,0:T(8,128)(2,1)S(1)} %bitcast.527, ...), custom_call_target="tpu_custom_call" | custom-call | tf_op jit(solution)/shard_map/attend_back/pallas_call | solution.py:216
  362.1 3.8 convolution_convert_fusion.4
  375.8 4.0 copy.175
  379.9 3.3 fusion.45
  397.4 16.9 %collective-permute-done.40 = bf16[4,2,64,1024]{3,2,1,0:T(8,128)(2,1)} collective-permute-done((bf16[4,2,64,1024]{3,2,1,0:T(8,128)(2,1)}, bf16[4,2,64,1024]{3,2,1,0:T(8,128)(2,1)}, u32[]{:S(2)}, u32[]{:S(2)}) %collective-permute-start.40) | collective-permute-done | bytes 1048608 | tf_op jit(solution)/shard_map/ppermute | solution.py:44
  433.2 4.2 collective-permute-done.38
  445.0 5.3 %collective-permute-done.42 = bf16[136,1024]{1,0:T(8,128)(2,1)S(1)} collective-permute-done((bf16[136,1024]{1,0:T(8,128)(2,1)S(1)}, bf16[136,1024]{1,0:T(8,128)(2,1)S(1)}, u32[]{:S(2)}, u32[]{:S(2)}) %collective-permute-start.42) | collective-permute-done | bytes 278560 | tf_op jit(solution)/shard_map/ppermute | solution.py:44
  450.3 9.1 %collective-permute-done.43 = bf16[136,1024]{1,0:T(8,128)(2,1)S(1)} collective-permute-done((bf16[136,1024]{1,0:T(8,128)(2,1)S(1)}, bf16[136,1024]{1,0:T(8,128)(2,1)S(1)}, u32[]{:S(2)}, u32[]{:S(2)}) %collective-permute-start.43) | collective-permute-done | bytes 278560 | tf_op jit(solution)/shard_map/ppermute | solution.py:44
  (605 shorter events, 252.6 us)
Async XLA Ops:
  21.3 31.3 %collective-permute-start.14 = (bf16[128,1024]{1,0:T(8,128)(2,1)S(1)}, bf16[128,1024]{1,0:T(8,128)(2,1)S(1)}, u32[]{:S(2)}, u32[]{:S(2)}) collective-permute-start(bf16[128,1024]{1,0:T(8,128)(2,1)S(1)} %fusion.106), channel_id=1, source_target_pairs={{0,8},{8,16},{16,24},{24,0},{1,9},{9,17},{17,25},{25,1},{2,10},{10... | collective-permute-start | bytes 786440 | tf_op jit(solution)/shard_map/ppermute | solution.py:44
  25.6 30.0 %collective-permute-start.15 = (bf16[128,1024]{1,0:T(8,128)(2,1)S(1)}, bf16[128,1024]{1,0:T(8,128)(2,1)S(1)}, u32[]{:S(2)}, u32[]{:S(2)}) collective-permute-start(bf16[128,1024]{1,0:T(8,128)(2,1)S(1)} %fusion.106), channel_id=1, source_target_pairs={{0,16},{8,24},{16,0},{24,8},{1,17},{9,25},{17,1},{25,9},{2,18},{10... | collective-permute-start | bytes 786440 | tf_op jit(solution)/shard_map/ppermute | solution.py:44
  27.3 29.8 %collective-permute-start.16 = (bf16[128,1024]{1,0:T(8,128)(2,1)S(1)}, bf16[128,1024]{1,0:T(8,128)(2,1)S(1)}, u32[]{:S(2)}, u32[]{:S(2)}) collective-permute-start(bf16[128,1024]{1,0:T(8,128)(2,1)S(1)} %fusion.106), channel_id=1, source_target_pairs={{0,24},{8,0},{16,8},{24,16},{1,25},{9,1},{17,9},{25,17},{2,26},{10... | collective-permute-start | bytes 786440 | tf_op jit(solution)/shard_map/ppermute | solution.py:44
  86.4 97.4 %collective-permute-start.23 = (bf16[4,2,64,1024]{3,2,0,1:T(8,128)(2,1)}, bf16[4,2,64,1024]{3,2,0,1:T(8,128)(2,1)}, u32[]{:S(2)}, u32[]{:S(2)}) collective-permute-start(bf16[4,2,64,1024]{3,2,0,1:T(8,128)(2,1)} %pad_maximum_fusion.21), channel_id=1, source_target_pairs={{0,4},{4,0},{1,5},{5,1},{2,6},{6,2},{3,7},{7,3},{8,12},{12,8},{9,1... | collective-permute-start | bytes 3145736 | tf_op jit(solution)/shard_map/ppermute | solution.py:44
  97.6 86.7 %collective-permute-start.27 = (bf16[4,2,64,1024]{3,2,0,1:T(8,128)(2,1)}, bf16[4,2,64,1024]{3,2,0,1:T(8,128)(2,1)}, u32[]{:S(2)}, u32[]{:S(2)}) collective-permute-start(bf16[4,2,64,1024]{3,2,0,1:T(8,128)(2,1)} %pad_maximum_fusion.23), channel_id=1, source_target_pairs={{0,2},{2,0},{1,3},{3,1},{4,6},{6,4},{5,7},{7,5},{8,10},{10,8},{9,1... | collective-permute-start | bytes 3145736 | tf_op jit(solution)/shard_map/ppermute | solution.py:44
  99.5 46.9 %collective-permute-start.10 = (bf16[4,2,64,1024]{3,2,0,1:T(8,128)(2,1)S(1)}, bf16[4,2,64,1024]{3,2,0,1:T(8,128)(2,1)S(1)}, u32[]{:S(2)}, u32[]{:S(2)}) collective-permute-start(bf16[4,2,64,1024]{3,2,0,1:T(8,128)(2,1)S(1)} %pad_maximum_fusion.16), channel_id=1, source_target_pairs={{0,2},{2,0},{1,3},{3,1},{4,6},{6,4},{5,7},{7,5},{8,10},{10,8},{9,1... | collective-permute-start | bytes 3145736 | tf_op jit(solution)/shard_map/ppermute | solution.py:44
  100.3 49.4 %collective-permute-start.8 = (bf16[4,2,72,1024]{3,2,0,1:T(8,128)(2,1)S(1)}, bf16[4,2,72,1024]{3,2,0,1:T(8,128)(2,1)S(1)}, u32[]{:S(2)}, u32[]{:S(2)}) collective-permute-start(bf16[4,2,72,1024]{3,2,0,1:T(8,128)(2,1)S(1)} %pad_maximum_fusion.13), channel_id=1, source_target_pairs={{0,4},{4,0},{1,5},{5,1},{2,6},{6,2},{3,7},{7,3},{8,12},{12,8},{9,1... | collective-permute-start | bytes 3538952 | tf_op jit(solution)/shard_map/ppermute | solution.py:44
  103.2 93.6 %collective-permute-start.25 = (bf16[4,2,64,1024]{3,2,0,1:T(8,128)(2,1)}, bf16[4,2,64,1024]{3,2,0,1:T(8,128)(2,1)}, u32[]{:S(2)}, u32[]{:S(2)}) collective-permute-start(bf16[4,2,64,1024]{3,2,0,1:T(8,128)(2,1)} %pad_maximum_fusion.22), channel_id=1, source_target_pairs={{0,2},{2,0},{1,3},{3,1},{4,6},{6,4},{5,7},{7,5},{8,10},{10,8},{9,1... | collective-permute-start | bytes 3145736 | tf_op jit(solution)/shard_map/ppermute | solution.py:44
  146.4 53.5 %collective-permute-start.18 = (bf16[4,2,64,1024]{3,2,0,1:T(8,128)(2,1)}, bf16[4,2,64,1024]{3,2,0,1:T(8,128)(2,1)}, u32[]{:S(2)}, u32[]{:S(2)}) collective-permute-start(bf16[4,2,64,1024]{3,2,0,1:T(8,128)(2,1)} %pad_maximum_fusion.19), channel_id=1, source_target_pairs={{0,4},{4,0},{1,5},{5,1},{2,6},{6,2},{3,7},{7,3},{8,12},{12,8},{9,1... | collective-permute-start | bytes 3145736 | tf_op jit(solution)/shard_map/ppermute | solution.py:44
  149.7 40.6 %collective-permute-start.12 = (bf16[1024,512]{1,0:T(8,128)(2,1)}, bf16[1024,512]{1,0:T(8,128)(2,1)}, u32[]{:S(2)}, u32[]{:S(2)}) collective-permute-start(bf16[1024,512]{1,0:T(8,128)(2,1)} %slice.222), channel_id=1, source_target_pairs={{0,1},{1,0},{2,3},{3,2},{4,5},{5,4},{6,7},{7,6},{8,9},{9,8},{10,11... | collective-permute-start | bytes 3145736 | tf_op jit(solution)/shard_map/ppermute | solution.py:44
  232.6 28.3 %collective-permute-start.56 = (bf16[4,2,64,1024]{3,2,0,1:T(8,128)(2,1)}, bf16[4,2,64,1024]{3,2,0,1:T(8,128)(2,1)}, u32[]{:S(2)}, u32[]{:S(2)}) collective-permute-start(bf16[4,2,64,1024]{3,2,0,1:T(8,128)(2,1)} %bitcast.521), channel_id=1, source_target_pairs={{0,4},{4,0},{1,5},{5,1},{2,6},{6,2},{3,7},{7,3},{8,12},{12,8},{9,1... | collective-permute-start | bytes 3145736 | tf_op jit(solution)/shard_map/ppermute | solution.py:44
  235.4 28.8 %collective-permute-start.54 = (bf16[4,2,64,1024]{3,2,0,1:T(8,128)(2,1)}, bf16[4,2,64,1024]{3,2,0,1:T(8,128)(2,1)}, u32[]{:S(2)}, u32[]{:S(2)}) collective-permute-start(bf16[4,2,64,1024]{3,2,0,1:T(8,128)(2,1)} %bitcast.522), channel_id=1, source_target_pairs={{0,2},{2,0},{1,3},{3,1},{4,6},{6,4},{5,7},{7,5},{8,10},{10,8},{9,1... | collective-permute-start | bytes 3145736 | tf_op jit(solution)/shard_map/ppermute | solution.py:44
  246.5 34.2 %collective-permute-start.48 = (bf16[4,2,64,1024]{3,2,0,1:T(8,128)(2,1)}, bf16[4,2,64,1024]{3,2,0,1:T(8,128)(2,1)}, u32[]{:S(2)}, u32[]{:S(2)}) collective-permute-start(bf16[4,2,64,1024]{3,2,0,1:T(8,128)(2,1)} %bitcast.523), channel_id=1, source_target_pairs={{0,4},{4,0},{1,5},{5,1},{2,6},{6,2},{3,7},{7,3},{8,12},{12,8},{9,1... | collective-permute-start | bytes 3145736 | tf_op jit(solution)/shard_map/ppermute | solution.py:44
  249.2 35.0 %collective-permute-start.46 = (bf16[4,2,64,1024]{3,2,1,0:T(8,128)(2,1)}, bf16[4,2,64,1024]{3,2,1,0:T(8,128)(2,1)}, u32[]{:S(2)}, u32[]{:S(2)}) collective-permute-start(bf16[4,2,64,1024]{3,2,1,0:T(8,128)(2,1)} %dynamic-slice_bitcast_fusion), channel_id=1, source_target_pairs={{0,2},{2,0},{1,3},{3,1},{4,6},{6,4},{5,7},{7,5},{8,10},{10,8},{9,1... | collective-permute-start | bytes 3145736 | tf_op jit(solution)/shard_map/ppermute | solution.py:44
  254.3 37.1 %collective-permute-start.28 = (bf16[2,256,1024]{2,1,0:T(8,128)(2,1)}, bf16[2,256,1024]{2,1,0:T(8,128)(2,1)}, u32[]{:S(2)}, u32[]{:S(2)}) collective-permute-start(bf16[2,256,1024]{2,1,0:T(8,128)(2,1)} %fusion.55), channel_id=1, source_target_pairs={{0,1},{1,0},{2,3},{3,2},{4,5},{5,4},{6,7},{7,6},{8,9},{9,8},{10,11... | collective-permute-start | bytes 3145736 | tf_op jit(solution)/shard_map/ppermute | solution.py:44
  264.1 82.3 %collective-permute-start.57 = (bf16[4,64,1024]{2,1,0:T(8,128)(2,1)}, bf16[4,64,1024]{2,1,0:T(8,128)(2,1)}, u32[]{:S(2)}, u32[]{:S(2)}) collective-permute-start(bf16[4,64,1024]{2,1,0:T(8,128)(2,1)} %dynamic-slice_bitcast_fusion.3), channel_id=1, source_target_pairs={{0,2},{2,0},{1,3},{3,1},{4,6},{6,4},{5,7},{7,5},{8,10},{10,8},{9,1... | collective-permute-start | bytes 1572872 | tf_op jit(solution)/shard_map/ppermute | solution.py:44
  280.8 72.1 %collective-permute-start.55 = (bf16[4,64,1024]{2,1,0:T(8,128)(2,1)}, bf16[4,64,1024]{2,1,0:T(8,128)(2,1)}, u32[]{:S(2)}, u32[]{:S(2)}) collective-permute-start(bf16[4,64,1024]{2,1,0:T(8,128)(2,1)} %dynamic-slice_bitcast_fusion.4), channel_id=1, source_target_pairs={{0,4},{4,0},{1,5},{5,1},{2,6},{6,2},{3,7},{7,3},{8,12},{12,8},{9,1... | collective-permute-start | bytes 1572872 | tf_op jit(solution)/shard_map/ppermute | solution.py:44
  284.2 27.9 %collective-permute-start.49 = (bf16[4,64,1024]{2,1,0:T(8,128)(2,1)}, bf16[4,64,1024]{2,1,0:T(8,128)(2,1)S(1)}, u32[]{:S(2)}, u32[]{:S(2)}) collective-permute-start(bf16[4,64,1024]{2,1,0:T(8,128)(2,1)} %dynamic-slice_bitcast_fusion.5), channel_id=1, source_target_pairs={{0,2},{2,0},{1,3},{3,1},{4,6},{6,4},{5,7},{7,5},{8,10},{10,8},{9,1... | collective-permute-start | bytes 1572872 | tf_op jit(solution)/shard_map/ppermute | solution.py:44
  303.9 68.7 %collective-permute-start.39 = (bf16[1024,512]{0,1:T(8,128)(2,1)}, bf16[1024,512]{0,1:T(8,128)(2,1)}, u32[]{:S(2)}, u32[]{:S(2)}) collective-permute-start(bf16[1024,512]{0,1:T(8,128)(2,1)} %fusion.53), channel_id=1, source_target_pairs={{0,1},{1,0},{2,3},{3,2},{4,5},{5,4},{6,7},{7,6},{8,9},{9,8},{10,11... | collective-permute-start | bytes 3145736 | tf_op jit(solution)/shard_map/ppermute | solution.py:44
  312.3 46.0 %collective-permute-start.29 = (bf16[256,1024]{1,0:T(8,128)(2,1)}, bf16[256,1024]{1,0:T(8,128)(2,1)}, u32[]{:S(2)}, u32[]{:S(2)}) collective-permute-start(bf16[256,1024]{1,0:T(8,128)(2,1)} %dynamic-slice_bitcast_fusion.10), channel_id=1, source_target_pairs={{0,2},{2,0},{1,3},{3,1},{4,6},{6,4},{5,7},{7,5},{8,10},{10,8},{9,1... | collective-permute-start | bytes 1572872 | tf_op jit(solution)/shard_map/ppermute | solution.py:44
  315.5 51.7 %collective-permute-start.50 = (bf16[128,1024]{1,0:T(8,128)(2,1)}, bf16[128,1024]{1,0:T(8,128)(2,1)S(1)}, u32[]{:S(2)}, u32[]{:S(2)}) collective-permute-start(bf16[128,1024]{1,0:T(8,128)(2,1)} %get-tuple-element.52), channel_id=1, source_target_pairs={{0,8},{8,16},{16,24},{24,0},{1,9},{9,17},{17,25},{25,1},{2,10},{10... | collective-permute-start | bytes 786440 | tf_op jit(solution)/shard_map/ppermute | solution.py:44
  367.2 27.9 %collective-permute-start.58 = (bf16[128,1024]{1,0:T(8,128)(2,1)}, bf16[128,1024]{1,0:T(8,128)(2,1)}, u32[]{:S(2)}, u32[]{:S(2)}) collective-permute-start(bf16[128,1024]{1,0:T(8,128)(2,1)} %get-tuple-element.45), channel_id=1, source_target_pairs={{0,8},{8,16},{16,24},{24,0},{1,9},{9,17},{17,25},{25,1},{2,10},{10... | collective-permute-start | bytes 786440 | tf_op jit(solution)/shard_map/ppermute | solution.py:44
  391.4 28.7 %collective-permute-start.37 = (bf16[4,2,72,1024]{3,2,0,1:T(8,128)(2,1)}, bf16[4,2,72,1024]{3,2,0,1:T(8,128)(2,1)}, u32[]{:S(2)}, u32[]{:S(2)}) collective-permute-start(bf16[4,2,72,1024]{3,2,0,1:T(8,128)(2,1)} %fusion.50), channel_id=1, source_target_pairs={{0,2},{2,0},{1,3},{3,1},{4,6},{6,4},{5,7},{7,5},{8,10},{10,8},{9,1... | collective-permute-start | bytes 3538952 | tf_op jit(solution)/shard_map/ppermute | solution.py:44
  395.2 29.5 %collective-permute-start.53 = (f32[2,32,16,64]{3,0,2,1:T(2,128)S(1)}, f32[2,32,16,64]{3,0,2,1:T(2,128)S(1)}, u32[]{:S(2)}, u32[]{:S(2)}) collective-permute-start(f32[2,32,16,64]{3,0,2,1:T(2,128)S(1)} %bitcast.579), channel_id=1, source_target_pairs={{0,1},{1,0},{2,3},{3,2},{4,5},{5,4},{6,7},{7,6},{8,9},{9,8},{10,11... | collective-permute-start | bytes 786440 | tf_op jit(solution)/shard_map/ppermute | solution.py:44
  (150 other events, 1257.6 us)

commit v2 on v1

v2 whole, which is shorter than its diff:
```python
import jax
import jax.numpy as jnp
from jax import lax
from jax.experimental import pallas as pl
from jax.experimental.pallas import tpu as pltpu
from jax.sharding import Mesh, PartitionSpec as P

H = 16
LAYERS = 24
EPSILON = 1e-05
DOC_MAX = 512

BF = jnp.bfloat16
F32 = jnp.float32


def half(values):
    return values.astype(BF)


def norm_parts(values):
    mean = jnp.mean(values, axis=-1, keepdims=True)
    centred = values - mean
    spread = jnp.mean(centred * centred, axis=-1, keepdims=True)
    inverse = lax.rsqrt(spread + EPSILON)
    return (centred * inverse, inverse)


def norm_back(grad_out, normal, inverse, gain):
    scaled = grad_out * gain
    return inverse * (
        scaled
        - jnp.mean(scaled, axis=-1, keepdims=True)
        - normal * jnp.mean(scaled * normal, axis=-1, keepdims=True)
    )


def dot(left, right, contract):
    return lax.dot_general(left, right, ((contract[:1], contract[1:]), ((), ())), preferred_element_type=F32)


def cost(microseconds):
    return pl.CostEstimate(flops=int(microseconds * 9e8), bytes_accessed=int(microseconds * 3e6), transcendentals=0)


def after(value, *others):
    return lax.optimization_barrier((value, *others))[0]


def shift(value, axis, step):
    size = lax.axis_size(axis)
    return lax.ppermute(value, axis, [(i, (i + step) % size) for i in range(size)])


def gather_relative(value, axis):
    return [value] + [shift(value, axis, k) for k in range(1, lax.axis_size(axis))]


def return_relative(blocks, axis):
    return [blocks[0]] + [shift(block, axis, -k) for k, block in enumerate(blocks) if k]


def by_place(parts, axis, sign):
    size = len(parts)
    here = lax.axis_index(axis)
    return [lax.select_n(lax.rem(sign * (place - here) + size, size), *parts) for place in range(size)]


def swap_axis(value, axis, at):
    size = lax.axis_size(axis)
    here = lax.axis_index(axis)
    parts = []
    for k in range(size):
        block = lax.dynamic_index_in_dim(value, lax.rem(here + k, size), at, keepdims=False)
        parts.append(shift(block, axis, k) if k else block)
    return by_place(parts, axis, -1)


def reduce_axis(value, axis, at):
    size = lax.axis_size(axis)
    here = lax.axis_index(axis)
    total = lax.dynamic_index_in_dim(value, here, at, keepdims=False)
    for k in range(1, size):
        block = lax.dynamic_index_in_dim(value, lax.rem(here + k, size), at, keepdims=False)
        total = total + shift(block, axis, k)
    return total


def whole(memory_space=pltpu.VMEM):
    return pl.BlockSpec(memory_space=memory_space)


def assemble(place, firsts, seconds, wanted, shapes):
    ny, ng = len(firsts), len(seconds)
    nz, high, wide = firsts[0].shape[1:]

    def kernel(place_ref, *refs):
        ins, outs = (refs[:ny], refs[ny : ny + ng]), refs[ny + ng :]
        y, g = place_ref[1], place_ref[2]
        for pieces, out in zip(wanted, outs):
            for which, row, rows, column, columns, into in pieces:
                for ky in range(ny):
                    for kg in range(ng):
                        source = ins[0][ky].at[kg, 0] if which == 0 else ins[1][kg].at[ky, 0]
                        at = (0, lax.rem(y - ky + ny, ny), lax.rem(g - kg + ng, ng))
                        out[(*at, slice(None), pl.ds(into, columns))] = source[row : row + rows, column : column + columns]

    def out_spec(shape):
        return pl.BlockSpec((1, ny, ng, *shape), lambda i, place_ref: (lax.rem(place_ref[0] - i + nz, nz), 0, 0, 0, 0))

    return pl.pallas_call(
        kernel,
        grid_spec=pltpu.PrefetchScalarGridSpec(
            num_scalar_prefetch=1,
            grid=(nz,),
            in_specs=[pl.BlockSpec((ng, 1, high, wide), lambda i, place_ref: (0, i, 0, 0))] * ny
            + [pl.BlockSpec((ny, 1, high, wide), lambda i, place_ref: (0, i, 0, 0))] * ng,
            out_specs=[out_spec(shape) for shape in shapes],
        ),
        out_shape=[jax.ShapeDtypeStruct((nz, ny, ng, *shape), BF) for shape in shapes],
        compiler_params=pltpu.CompilerParams(vmem_limit_bytes=16 << 20),
        cost_estimate=cost(4),
        name="assemble",
    )(place, *firsts, *seconds)


def gather_over_z(shard):
    parts = gather_relative(shard, "z")
    middle = shard.shape[1] // 2
    return jnp.stack([p[:, :middle] for p in parts]), jnp.stack([p[:, middle:] for p in parts])


def gather_once(first, second):
    return jnp.stack(gather_relative(first, "g")), jnp.stack(gather_relative(second, "y"))


def gather_twice(first, second):
    return gather_relative(first, "y"), gather_relative(second, "g")


def weight_grad_kernel(sizes, place_ref, left_ref, right_ref, *refs):
    nz, ny, ng = sizes
    middle = (len(refs) - 1) - (ny + ng)
    kept, outs, total = refs[:middle], refs[middle:-1], refs[-1]
    y, g = place_ref[1], place_ref[2]
    width = right_ref.shape[1]
    total[:, :width] = dot(left_ref[...], right_ref[...], (0, 0))
    if kept:
        total[:, width:] = kept[0][...].astype(F32)
    columns = total.shape[1] // 2
    rows = total.shape[0] // (ny * ng)
    for k in range(ng):
        at = lax.rem(g + k, ng)
        for i in range(ny):
            start = pl.multiple_of((i * ng + at) * rows, rows)
            outs[k][0, i] = half(total[pl.ds(start, rows), :columns])
    for k in range(ny):
        at = lax.rem(y + k, ny)
        for i in range(ng):
            start = pl.multiple_of((at * ng + i) * rows, rows)
            outs[ng + k][0, i] = half(total[pl.ds(start, rows), columns:])


def weight_grad(place, sizes, left, right, more=None):
    nz, ny, ng = sizes
    tokens, height = left.shape
    width = right.shape[1] + (more.shape[1] if more is not None else 0)
    rows, columns = height // (nz * ny * ng), width // 2

    def kernel(*refs):
        weight_grad_kernel(sizes, *refs)

    first = jax.ShapeDtypeStruct((nz, ny, rows, columns), BF)
    second = jax.ShapeDtypeStruct((nz, ng, rows, columns), BF)
    step = height // nz
    extra = [] if more is None else [more]
    outs = pl.pallas_call(
        kernel,
        grid=(nz,),
        in_specs=[
            whole(pltpu.SMEM),
            pl.BlockSpec((tokens, step), lambda i: (0, i)),
            pl.BlockSpec((tokens, right.shape[1]), lambda i: (0, 0)),
        ]
        + [pl.BlockSpec((step, m.shape[1]), lambda i: (i, 0)) for m in extra],
        out_specs=[pl.BlockSpec((1, ny, rows, columns), lambda i: (i, 0, 0, 0))] * ng
        + [pl.BlockSpec((1, ng, rows, columns), lambda i: (i, 0, 0, 0))] * ny,
        out_shape=[first] * ng + [second] * ny,
        scratch_shapes=[pltpu.VMEM((step, width), F32)],
        compiler_params=pltpu.CompilerParams(vmem_limit_bytes=20 << 20),
        cost_estimate=cost(7),
        name="weight_grad",
    )(place, left, right, *extra)
    return outs[:ng], outs[ng:]


def total_of(refs, at):
    value = refs[0][at].astype(F32)
    for ref in refs[1:]:
        value = value + ref[at].astype(F32)
    return value


def add_split(place, sizes, first, second):
    nz, ny, ng = sizes
    rows, columns = first[0].shape[2:]

    def kernel(place_ref, *refs):
        firsts, seconds, outs = refs[:ng], refs[ng : ng + ny], refs[ng + ny :]
        y, g = place_ref[1], place_ref[2]
        for k in range(ny):
            outs[k][0] = half(total_of(firsts, (0, lax.rem(y + k, ny))))
        for k in range(ng):
            outs[ny + k][0] = half(total_of(seconds, (0, lax.rem(g + k, ng))))

    shape = jax.ShapeDtypeStruct((nz, rows, columns), BF)
    outs = pl.pallas_call(
        kernel,
        grid=(nz,),
        in_specs=[whole(pltpu.SMEM)]
        + [pl.BlockSpec((1, ny, rows, columns), lambda i: (i, 0, 0, 0))] * ng
        + [pl.BlockSpec((1, ng, rows, columns), lambda i: (i, 0, 0, 0))] * ny,
        out_specs=[pl.BlockSpec((1, rows, columns), lambda i: (i, 0, 0))] * (ny + ng),
        out_shape=[shape] * (ny + ng),
        compiler_params=pltpu.CompilerParams(vmem_limit_bytes=12 << 20),
        cost_estimate=cost(3.5),
        name="add_split",
    )(place, *first, *second)
    return outs[:ny], outs[ny:]


def split_over_z(place, first, second):
    ny, ng = len(first), len(second)
    nz, rows, columns = first[0].shape

    def kernel(place_ref, *refs):
        firsts, seconds, outs = refs[:ny], refs[ny : ny + ng], refs[ny + ng :]
        z = place_ref[0]
        for k in range(nz):
            at = lax.rem(z + k, nz)
            outs[k][:, :columns] = total_of(firsts, at).astype(outs[k].dtype)
            outs[k][:, columns:] = total_of(seconds, at).astype(outs[k].dtype)

    return pl.pallas_call(
        kernel,
        in_specs=[whole(pltpu.SMEM)] + [whole()] * (ny + ng),
        out_specs=[whole()] * nz,
        out_shape=[jax.ShapeDtypeStruct((rows, 2 * columns), BF if k else F32) for k in range(nz)],
        compiler_params=pltpu.CompilerParams(vmem_limit_bytes=12 << 20),
        cost_estimate=cost(2.5),
        name="split_over_z",
    )(place, *first, *second)


def send_parts(first, second, axis_first, axis_second):
    first = [first[0]] + [shift(b, axis_first, k) for k, b in enumerate(first) if k]
    second = [second[0]] + [shift(b, axis_second, k) for k, b in enumerate(second) if k]
    return first, second


def reduce_in_layer(place, sizes, parts, *others):
    first, second = parts
    first = [after(first[0], *others)] + first[1:]
    return send_parts(*add_split(place, sizes, first, second), "y", "g")


def reduce_over_z(place, parts, *others):
    first, second = parts
    first = [after(first[0], *others)] + first[1:]
    blocks = split_over_z(place, first, second)
    return [blocks[0]] + [shift(block, "z", k) for k, block in enumerate(blocks) if k]


def total_sum(blocks):
    total = blocks[0]
    for block in blocks[1:]:
        total = total + block.astype(F32)
    return total


def key_blocks(start, block):
    return range(max(0, start - DOC_MAX), start + block, block)


def visible_part(first_ref, low, start, block, rows, row):
    key_pos = low + row + lax.broadcasted_iota(jnp.int32, (rows, block), 0)
    visible = key_pos >= first_ref[:, start : start + block]
    if low == start:
        visible &= key_pos <= start + lax.broadcasted_iota(jnp.int32, (rows, block), 1)
    return visible


def fold(values, op):
    rows, lanes = values.shape
    return op(values.reshape(rows // 8, 8, lanes), axis=0)


def for_heads(values, head_dim):
    lane = lax.broadcasted_iota(jnp.int32, values.shape, 1) // head_dim
    heads = values.shape[1] // head_dim
    return jnp.concatenate([jnp.where(lane == h, values, jnp.zeros_like(values)) for h in range(heads)], axis=0)


def heads_of(values, head_dim, block):
    heads = values.shape[0] // head_dim
    return jnp.concatenate(
        [values[h * head_dim : (h + 1) * head_dim, h * block : (h + 1) * block] for h in range(heads)], axis=0
    )


def load_in_order(order_ref, source, into, local, columns):
    for n in range(into.shape[0] // local):
        rows = pl.ds(pl.multiple_of(order_ref[n] * local, local), local)
        into[n * local : (n + 1) * local] = source[rows, columns]


def store_in_order(order_ref, source, into, local, columns):
    for n in range(source.shape[0] // local):
        rows = pl.ds(pl.multiple_of(order_ref[n] * local, local), local)
        into[rows, columns] = half(source[n * local : (n + 1) * local])


def attend_kernel(block, sub, head_dim, local, order_ref, qkv_ref, first_ref, out_ref, log_ref, q_s, k_s, v_s, o_s, s_s):
    length, lanes = q_s.shape
    heads = lanes // head_dim
    for i, into in enumerate((q_s, k_s, v_s)):
        load_in_order(order_ref, qkv_ref, into, local, slice(i * lanes, (i + 1) * lanes))
    v_t = v_s[...].T
    for start in range(0, length, block):
        q_heads = for_heads(q_s[start : start + block] * (head_dim ** (-0.5)), head_dim)
        lows = list(key_blocks(start, block))
        top8 = [jnp.full((8, block), -1e30, F32)] * heads
        for n, low in enumerate(lows):
            scores = dot(k_s[low : low + block], q_heads, (1, 1))
            for r in range(0, block, sub):
                visible = visible_part(first_ref, low, start, block, sub, r)
                rows = slice(n * block + r, n * block + r + sub)
                for h in range(heads):
                    columns = slice(h * block, (h + 1) * block)
                    piece = jnp.where(visible, scores[r : r + sub, columns], -1e30)
                    top8[h] = jnp.maximum(top8[h], fold(piece, jnp.max))
                    s_s[rows, columns] = piece
        width = len(lows) * block
        top = jnp.concatenate([jnp.max(v, axis=0, keepdims=True) for v in top8], axis=1)
        total8 = jnp.zeros((8, heads * block), F32)
        for r in range(0, width, sub):
            exponent = jnp.exp(s_s[r : r + sub] - top)
            total8 = total8 + fold(exponent, jnp.sum)
            s_s[r : r + sub] = exponent
        total = jnp.sum(total8, axis=0, keepdims=True)
        probs = half(s_s[:width] * (1.0 / total))
        out = dot(v_t[:, lows[0] : lows[0] + width], probs, (1, 0))
        log = top + jnp.log(total)
        for h in range(heads):
            log_ref[0, h : h + 1, start : start + block] = log[:, h * block : (h + 1) * block]
        o_s[start : start + block] = half(heads_of(out, head_dim, block).T)
    store_in_order(order_ref, o_s, out_ref, local, slice(None))


def attend_back_kernel(
    block,
    sub,
    head_dim,
    local,
    order_ref,
    qkv_ref,
    g_ref,
    log_ref,
    first_ref,
    out_ref,
    q_s,
    k_s,
    v_s,
    g_s,
    query_grad,
    key_sum,
    value_sum,
    p_s,
    d_s,
):
    length, lanes = q_s.shape
    heads = lanes // head_dim
    scale = head_dim ** (-0.5)
    for i, into in enumerate((q_s, k_s, v_s)):
        load_in_order(order_ref, qkv_ref, into, local, slice(i * lanes, (i + 1) * lanes))
    load_in_order(order_ref, g_ref, g_s, local, slice(None))
    k_t = k_s[...].T
    for start in range(0, length, block):
        q_heads = for_heads(q_s[start : start + block] * scale, head_dim)
        g_heads = for_heads(g_s[start : start + block], head_dim)
        lows = list(key_blocks(start, block))
        delta8 = [jnp.zeros((8, block), F32)] * heads
        for n, low in enumerate(lows):
            scores = dot(k_s[low : low + block], q_heads, (1, 1))
            grads = dot(v_s[low : low + block], g_heads, (1, 1))
            for r in range(0, block, sub):
                visible = visible_part(first_ref, low, start, block, sub, r)
                rows = slice(n * block + r, n * block + r + sub)
                for h in range(heads):
                    columns = slice(h * block, (h + 1) * block)
                    p = jnp.where(visible, scores[r : r + sub, columns], -1e30)
                    p = jnp.exp(p - log_ref[0, h : h + 1, start : start + block])
                    d = grads[r : r + sub, columns]
                    delta8[h] = delta8[h] + fold(p * d, jnp.sum)
                    p_s[rows, columns] = p
                    d_s[rows, columns] = d
        delta = jnp.concatenate([jnp.sum(v, axis=0, keepdims=True) for v in delta8], axis=1)
        width = len(lows) * block
        p = p_s[:width]
        grad_scores = half(p * (d_s[:width] - delta))
        dq = dot(k_t[:, lows[0] : lows[0] + width], grad_scores, (1, 0))
        dk = dot(grad_scores, q_heads, (1, 0))
        dv = dot(half(p), g_heads, (1, 0))
        for n, low in enumerate(lows):
            rows = slice(n * block, (n + 1) * block)
            if low == start:
                key_sum[low : low + block] = dk[rows]
                value_sum[low : low + block] = dv[rows]
            else:
                key_sum[low : low + block] += dk[rows]
                value_sum[low : low + block] += dv[rows]
        query_grad[start : start + block] = (heads_of(dq, head_dim, block) * scale).T
    for i, source in enumerate((query_grad, key_sum, value_sum)):
        store_in_order(order_ref, source, out_ref, local, slice(i * lanes, (i + 1) * lanes))


def attend(qkv, first, order, local, head_dim):
    length, width = qkv.shape
    block = min(256, length)
    window = min(length, DOC_MAX + block)
    lanes = 2 * head_dim
    steps = width // (3 * lanes)

    def kernel(*refs):
        attend_kernel(block, 64, head_dim, local, *refs)

    return pl.pallas_call(
        kernel,
        grid=(steps,),
        in_specs=[
            whole(pltpu.SMEM),
            pl.BlockSpec((length, 3 * lanes), lambda i: (0, i)),
            pl.BlockSpec((1, length), lambda i: (0, 0)),
        ],
        out_specs=[
            pl.BlockSpec((length, lanes), lambda i: (0, i)),
            pl.BlockSpec((1, 2, length), lambda i: (i, 0, 0)),
        ],
        out_shape=[
            jax.ShapeDtypeStruct((length, width // 3), BF),
            jax.ShapeDtypeStruct((steps, 2, length), F32),
        ],
        scratch_shapes=[pltpu.VMEM((length, lanes), BF)] * 4 + [pltpu.VMEM((window, 2 * block), F32)],
        compiler_params=pltpu.CompilerParams(vmem_limit_bytes=16 << 20),
        cost_estimate=cost(11.5 * steps / 4),
        name="attend",
    )(order, qkv, first[None])


def attend_back(qkv, grad_out, logs, first, order, local, head_dim):
    length, width = qkv.shape
    block = min(256, length)
    window = min(length, DOC_MAX + block)
    lanes = 2 * head_dim
    steps = width // (3 * lanes)

    def kernel(*refs):
        attend_back_kernel(block, 64, head_dim, local, *refs)

    return pl.pallas_call(
        kernel,
        grid=(steps,),
        in_specs=[
            whole(pltpu.SMEM),
            pl.BlockSpec((length, 3 * lanes), lambda i: (0, i)),
            pl.BlockSpec((length, lanes), lambda i: (0, i)),
            pl.BlockSpec((1, 2, length), lambda i: (i, 0, 0)),
            pl.BlockSpec((1, length), lambda i: (0, 0)),
        ],
        out_specs=pl.BlockSpec((length, 3 * lanes), lambda i: (0, i)),
        out_shape=jax.ShapeDtypeStruct((length, width), BF),
        scratch_shapes=[pltpu.VMEM((length, lanes), BF)] * 4
        + [pltpu.VMEM((length, lanes), F32)] * 3
        + [pltpu.VMEM((window, 2 * block), F32)] * 2,
        compiler_params=pltpu.CompilerParams(vmem_limit_bytes=20 << 20),
        cost_estimate=cost(18 * steps / 4),
        name="attend_back",
    )(order, qkv, grad_out, logs, first[None])


def gelu_parts(u):
    c = 0.7978845608028654
    square = u * u
    h = 0.5 + 0.5 * jnp.tanh(u * (c + (c * 0.044715) * square))
    value = u * h
    return value, h + value * (1.0 - h) * (2 * c + (6 * c * 0.044715) * square)


def up_part(normed, weight, bias):
    tokens, width = normed.shape
    ff = weight.shape[1]
    block = min(256, ff)
    rows = min(256, tokens)

    def kernel(x_ref, w_ref, b_ref, active_ref, slope_ref):
        for r in range(0, tokens, rows):
            u = dot(x_ref[r : r + rows], w_ref[...], (1, 0)) + b_ref[...]
            value, slope = gelu_parts(u)
            active_ref[r : r + rows] = half(value)
            slope_ref[r : r + rows] = slope

    column = pl.BlockSpec((tokens, block), lambda i: (0, i))
    return pl.pallas_call(
        kernel,
        grid=(ff // block,),
        in_specs=[
            pl.BlockSpec((tokens, width), lambda i: (0, 0)),
            pl.BlockSpec((width, block), lambda i: (0, i)),
            pl.BlockSpec((1, block), lambda i: (0, i)),
        ],
        out_specs=[column, column],
        out_shape=[jax.ShapeDtypeStruct((tokens, ff), BF), jax.ShapeDtypeStruct((tokens, ff), F32)],
        compiler_params=pltpu.CompilerParams(vmem_limit_bytes=16 << 20),
        cost_estimate=cost(7),
        name="up_part",
    )(normed, weight, bias[None])


def up_back(grad_down, weight, slope):
    tokens, width = grad_down.shape
    ff = weight.shape[0]
    block = min(256, ff)
    rows = min(256, tokens)

    def kernel(g_ref, w_ref, slope_ref, out_ref, sum_ref):
        total = jnp.zeros((8, block), F32)
        for r in range(0, tokens, rows):
            grad = half(dot(g_ref[r : r + rows], w_ref[...], (1, 1)) * slope_ref[r : r + rows])
            out_ref[r : r + rows] = grad
            total = total + fold(grad.astype(F32), jnp.sum)
        sum_ref[...] = jnp.sum(total, axis=0, keepdims=True)

    column = pl.BlockSpec((tokens, block), lambda i: (0, i))
    return pl.pallas_call(
        kernel,
        grid=(ff // block,),
        in_specs=[
            pl.BlockSpec((tokens, width), lambda i: (0, 0)),
            pl.BlockSpec((block, width), lambda i: (i, 0)),
            column,
        ],
        out_specs=[column, pl.BlockSpec((1, block), lambda i: (0, i))],
        out_shape=[jax.ShapeDtypeStruct((tokens, ff), BF), jax.ShapeDtypeStruct((1, ff), F32)],
        compiler_params=pltpu.CompilerParams(vmem_limit_bytes=16 << 20),
        cost_estimate=cost(6.5),
        name="up_back",
    )(grad_down, weight, slope)


def body(
    block_input,
    doc_ids,
    gain_attn,
    shift_attn,
    w_qkv,
    bias_qv,
    w_proj,
    bias_proj,
    gain_mlp,
    shift_mlp,
    w_up,
    bias_up,
    w_down,
    bias_down,
    out_grad,
):
    nz, ny, ng, nt = (lax.axis_size(a) for a in ("z", "y", "g", "t"))
    sizes = (nz, ny, ng)
    z, y, g, t = (lax.axis_index(a) for a in ("z", "y", "g", "t"))
    place = jnp.stack([z, y, g]).astype(jnp.int32)
    chips = nz * ny * ng
    depth = LAYERS ** (-0.5)
    _, local, width = block_input.shape
    length = doc_ids.shape[1]
    shard = w_qkv.shape[0]
    part = width // nt
    head_dim = width // H
    lanes = 2 * head_dim
    pairs = part // lanes
    hidden_width = w_up.shape[1]
    ff_shard = w_down.shape[0]
    ff_part = hidden_width // nt
    own = ng * local
    block_rows = nt * shard

    natural = jnp.arange(ng * nt, dtype=jnp.int32)
    order = lax.rem(t - natural % nt + nt, nt) * ng + lax.rem(g - natural // nt + ng, ng)
    docs = lax.dynamic_index_in_dim(doc_ids, g, 0, keepdims=False)
    first_token = jnp.sum((docs[None, :] < docs[:, None]).astype(jnp.int32), axis=1)

    both = jnp.stack([block_input, out_grad], axis=1)
    parts = []
    for k in range(ng):
        block = lax.dynamic_index_in_dim(both, lax.rem(g + k, ng), 0, keepdims=False)
        parts.append(shift(block, "g", k) if k else block)
    both_own = jnp.concatenate(parts, axis=1)
    x_own, grad_own = both_own[0].astype(F32), both_own[1].astype(F32)
    both_all = jnp.concatenate(gather_relative(both_own, "t"), axis=1)

    vectors = [gain_attn, shift_attn, bias_qv, bias_proj, gain_mlp, shift_mlp, bias_up, bias_down]
    counts = [v.shape[0] for v in vectors]
    packed = half(lax.optimization_barrier(jnp.concatenate(vectors)))
    count = packed.shape[0]
    columns_a = half(w_qkv).reshape(shard, 3, nt, pairs, lanes).transpose(2, 0, 3, 1, 4).reshape(nt, shard, 3 * part)
    columns_o = half(w_proj).reshape(shard, nt, part).transpose(1, 0, 2)
    columns_u = half(w_up).reshape(shard, chips, nt, ff_shard).transpose(2, 0, 1, 3).reshape(nt, shard, ff_part)
    columns = jnp.concatenate([columns_a, columns_o, columns_u], axis=2)
    wide = columns.shape[2]
    packed = jnp.broadcast_to(jnp.pad(packed, (0, wide - count)), (nt, 8, wide))
    columns = swap_axis(jnp.concatenate([columns, packed], axis=1), "t", 0)
    packed = jnp.concatenate([c[shard : shard + 1, :count] for c in columns], axis=1)
    columns = jnp.concatenate([c[:shard] for c in columns], axis=0)
    packed = jnp.broadcast_to(jnp.pad(packed, ((0, 0), (0, 4 * part - nt * count))), (8, 4 * part))
    shard_a = jnp.concatenate([columns[:, : 4 * part], packed], axis=0)
    shard_u = columns[:, 4 * part :]
    shard_d = half(w_down)
    middle_d = width // 2

    first_a, second_a = gather_over_z(shard_a)
    first_d, second_d = gather_once(shard_d[:, :middle_d], shard_d[:, middle_d:])
    first_u, second_u = gather_over_z(after(shard_u, first_a, second_a))
    first_a, second_a = gather_once(first_a, second_a)
    first_a, second_a = gather_twice(first_a, second_a)
    side = 3 * part - 2 * part
    wqkv, wo, vector_rows = assemble(
        place,
        first_a,
        second_a,
        [
            [(0, 0, block_rows, 0, 2 * part, 0), (1, 0, block_rows, 0, side, 2 * part)],
            [(1, 0, block_rows, side, part, 0)],
            [(0, block_rows, 8, 0, 2 * part, 0)],
        ],
        [(block_rows, 3 * part), (block_rows, part), (8, 2 * part)],
    )
    wqkv = wqkv.reshape(width, 3 * part)
    wo = wo.reshape(width, part)
    first_u, second_u = gather_once(after(first_u, *first_a, *second_a), after(second_u, *first_a, *second_a))

    vector_rows = vector_rows.reshape(chips, 8, 2 * part)[:, 0, : nt * count].reshape(chips, nt, count)
    offsets = [0]
    for size in counts:
        offsets.append(offsets[-1] + size)
    pieces = [vector_rows[:, :, offsets[i] : offsets[i + 1]] for i in range(len(counts))]
    h_gain_attn, h_shift_attn, h_bias_qv, h_bias_proj, h_gain_mlp, h_shift_mlp = (
        p.reshape(-1).astype(F32) for p in pieces[:6]
    )
    h_bias_down = pieces[7].reshape(-1).astype(F32)
    h_bias_up = lax.dynamic_index_in_dim(pieces[6], t, 1, keepdims=False).astype(F32).reshape(-1)
    bias_q = lax.dynamic_slice_in_dim(h_bias_qv, t * part, part).reshape(pairs, lanes)
    bias_v = lax.dynamic_slice_in_dim(h_bias_qv, width + t * part, part).reshape(pairs, lanes)
    bias_qkv = jnp.stack([bias_q, jnp.zeros_like(bias_q), bias_v], axis=1).reshape(-1)

    normal_all, _ = norm_parts(both_all[0].astype(F32))
    normed_attn = half(normal_all * h_gain_attn + h_shift_attn)
    grad_down = half(depth * both_all[1].astype(F32))
    qkv = half(dot(normed_attn, wqkv, (1, 0)) + bias_qkv)
    both_d = gather_relative(after(jnp.concatenate([first_d, second_d], axis=0), first_u), "z")
    attended_heads, logs = attend(qkv, first_token, order, local, head_dim)
    first_u, second_u = gather_twice(first_u, second_u)
    wo = jnp.concatenate(by_place(gather_relative(wo, "t"), "t", -1), axis=1)
    attended = return_relative([attended_heads[k * own : (k + 1) * own] for k in range(nt)], "t")
    attended = jnp.concatenate(by_place(attended, "t", 1), axis=1)
    hidden = x_own + depth * (dot(attended, wo, (1, 0)) + h_bias_proj)
    normal_two, inverse_two = norm_parts(hidden)
    normed_own = half(normal_two * h_gain_mlp + h_shift_mlp)
    normed_mlp = jnp.concatenate(gather_relative(normed_own, "t"), axis=0)
    (wu,) = assemble(
        place,
        first_u,
        second_u,
        [[(0, 0, block_rows, 0, ff_part // 2, 0), (1, 0, block_rows, 0, ff_part // 2, ff_part // 2)]],
        [(block_rows, ff_part)],
    )
    wu = wu.reshape(width, ff_part)
    first_d = jnp.stack([b[:ng] for b in both_d], axis=1)
    second_d = jnp.stack([b[ng:] for b in both_d], axis=1)
    first_d, second_d = gather_twice(after(first_d, *first_u, *second_u), after(second_d, *first_u, *second_u))
    active, slope = up_part(normed_mlp, wu, h_bias_up)

    def own_sum(left, right):
        blocks = [half(dot(left[k * own : (k + 1) * own], right, (1, 1))) for k in range(1, nt)]
        mine = dot(after(left[:own], *blocks), right, (1, 1))
        return total_sum([mine] + [shift(block, "t", -k - 1) for k, block in enumerate(blocks)])

    down_parts = send_parts(*weight_grad(place, sizes, active, grad_down), "g", "y")
    (wd,) = assemble(
        place,
        first_d,
        second_d,
        [[(0, 0, ff_shard, 0, middle_d, 0), (1, 0, ff_shard, 0, middle_d, middle_d)]],
        [(ff_shard, width)],
    )
    wd = wd.reshape(ff_part, width)
    grad_up, d_bias_up = up_back(grad_down, wd, slope)
    up_blocks = weight_grad(place, sizes, normed_mlp, grad_up)
    down_parts = reduce_in_layer(place, sizes, down_parts, *up_blocks[0])
    up_parts = send_parts(*up_blocks, "g", "y")
    e2 = own_sum(grad_up, wu)

    d_gain_mlp = jnp.sum(e2 * normal_two, axis=0)
    d_shift_mlp = jnp.sum(e2, axis=0)
    grad_hidden = grad_own + norm_back(e2, normal_two, inverse_two, h_gain_mlp)
    grad_branch = half(depth * grad_hidden)
    d_bias_proj = jnp.sum(grad_branch, axis=0, dtype=F32)

    attended_back, d_proj = [], []
    for k in range(nt):
        at = lax.rem(t + k, nt) * part
        attended_back.append(half(dot(grad_branch, lax.dynamic_slice_in_dim(wo, at, part, 0), (1, 1))))
        d_proj.append(half(dot(attended, lax.dynamic_slice_in_dim(grad_branch, at, part, 1), (0, 0))))
    grad_attended = jnp.concatenate(
        [attended_back[0]] + [shift(b, "t", k) for k, b in enumerate(attended_back) if k], axis=0
    )
    d_proj = total_sum([d_proj[0].astype(F32)] + [shift(b, "t", k) for k, b in enumerate(d_proj) if k])

    def to_rows(blocks):
        return jnp.stack(by_place(return_relative([blocks[k] for k in range(ng)], "g"), "g", 1), axis=0)

    up_parts = reduce_in_layer(place, sizes, up_parts, grad_attended)
    down_parts = reduce_over_z(place, down_parts, grad_attended)
    grad_attended = after(grad_attended, up_parts[0][0], down_parts[0])
    d_qkv = attend_back(qkv, grad_attended, logs, first_token, order, local, head_dim)
    sum_down = total_sum(down_parts)
    a_blocks = weight_grad(place, sizes, normed_attn, d_qkv, half(d_proj))
    a_parts = send_parts(*a_blocks, "g", "y")
    up_parts = reduce_over_z(place, up_parts, *a_blocks[0])
    e1 = own_sum(d_qkv, wqkv)
    lowered = dot(after(active, e1), wd, (1, 0))
    lowered = total_sum(
        [lowered[:own]] + [shift(half(lowered[k * own : (k + 1) * own]), "t", -k) for k in range(1, nt)]
    )
    block_out = to_rows(half(hidden + depth * (lowered + h_bias_down)).reshape(ng, local, width))
    normal_one, inverse_one = norm_parts(x_own)
    d_gain_attn = jnp.sum(e1 * normal_one, axis=0)
    d_shift_attn = jnp.sum(e1, axis=0)
    grad_input = grad_hidden + norm_back(e1, normal_one, inverse_one, h_gain_attn)
    grad_input = to_rows(half(grad_input).reshape(ng, local, width)).astype(F32)
    a_parts = reduce_in_layer(place, sizes, a_parts, e1)
    sum_up = total_sum(up_parts)
    sum_a = total_sum(reduce_over_z(place, a_parts))

    def by_owner(full):
        return full.reshape(chips, nt, -1)

    d_bias_qkv = jnp.sum(d_qkv, axis=0, dtype=F32).reshape(pairs, 3, lanes)
    d_bias_qv = jnp.zeros((2 * width,), F32)
    d_bias_qv = lax.dynamic_update_slice_in_dim(d_bias_qv, d_bias_qkv[:, 0].reshape(-1), t * part, 0)
    d_bias_qv = lax.dynamic_update_slice_in_dim(d_bias_qv, d_bias_qkv[:, 2].reshape(-1), width + t * part, 0)
    d_bias_up = d_bias_up.reshape(chips, 1, ff_shard)
    d_bias_up = jnp.where(lax.broadcasted_iota(jnp.int32, (chips, nt, 1), 1) == t, d_bias_up, 0.0)
    d_bias_down = jnp.sum(grad_down[:own], axis=0, dtype=F32)
    sums = jnp.concatenate(
        [
            by_owner(d_gain_attn),
            by_owner(d_shift_attn),
            by_owner(d_bias_qv),
            by_owner(d_bias_proj),
            by_owner(d_gain_mlp),
            by_owner(d_shift_mlp),
            d_bias_up,
            by_owner(d_bias_down),
        ],
        axis=2,
    )
    sums = reduce_axis(sums, "t", 1).reshape(nz, ny, ng, count)
    for axis, at in (("g", 2), ("y", 1), ("z", 0)):
        sums = reduce_axis(sums, axis, at)
    out_vectors = [sums[offsets[i] : offsets[i + 1]] for i in range(len(counts))]

    up = swap_axis(sum_up.reshape(nt, shard, ff_part), "t", 0)
    sum_up = jnp.stack([u.reshape(shard, chips, ff_shard) for u in up], axis=2).reshape(shard, hidden_width)
    rest = swap_axis(sum_a.reshape(nt, shard, 4 * part), "t", 0)
    sum_qkv = jnp.stack([r[:, : 3 * part].reshape(shard, pairs, 3, lanes) for r in rest], axis=1)
    sum_qkv = sum_qkv.transpose(0, 3, 1, 2, 4).reshape(shard, 3 * width)
    sum_proj = jnp.concatenate([r[:, 3 * part :] for r in rest], axis=1)
    return (
        block_out,
        grad_input,
        out_vectors[0],
        out_vectors[1],
        sum_qkv,
        out_vectors[2],
        sum_proj,
        out_vectors[3],
        out_vectors[4],
        out_vectors[5],
        sum_up,
        out_vectors[6],
        sum_down,
        out_vectors[7],
    )


def solution(mesh):
    rows = 2
    dp, seq = mesh.shape["dp"], mesh.shape["seq"]
    high = 4
    split = Mesh(mesh.devices.reshape(high, dp // high, rows, seq // rows), ("z", "y", "g", "t"))
    everything = ("z", "y", "g", "t")
    tokens = P(("z", "y"), ("g", "t"), None)
    vector = P(everything)
    matrix = P(everything, None)
    return jax.shard_map(
        body,
        mesh=split,
        in_specs=(
            tokens,
            P(("z", "y"), None),
            vector,
            vector,
            matrix,
            vector,
            matrix,
            vector,
            vector,
            vector,
            matrix,
            vector,
            matrix,
            vector,
            tokens,
        ),
        out_specs=(
            tokens,
            tokens,
            vector,
            vector,
            matrix,
            vector,
            matrix,
            vector,
            vector,
            vector,
            matrix,
            vector,
            matrix,
            vector,
        ),
        check_vma=False,
    )
```

time: 474 us -> 420 us (0.89)
  other arithmetic: 90.4 us -> 41.4 us
  Pallas kernels: 40.4 us -> 85.9 us
  local copies, waits for them, and re-layouts: 78.1 us -> 39 us
  waiting for transfers between devices: 112 us -> 137 us
  matrix products: 54.3 us -> 30.8 us
  starting transfers between devices: 87.2 us -> 75.8 us
    pallas_call x2 -> x16, Pallas kernels: 40.4 us -> 85.9 us  [the longest x3 21.6 us: weight_grad(): pl.pallas_call(kernel, grid=(nz,), in_specs=[whole(pltpu.SMEM), pl.BlockS...]
    ppermute x61 -> x63, waiting for transfers between devices: 112 us -> 137 us  [shift(): lax.ppermute(value, axis, [(i, (i + step) % size) for i in range(size)])]
    another operation x52 -> x16, other arithmetic: 32.1 us -> 8.03 us  [the longest x3 2.49 us: gather_once(): jnp.stack(gather_relative(first, 'g'))]
    dot_general x21 -> x11, matrix products: 54.3 us -> 30.8 us  [dot(): lax.dot_general(left, right, ((contract[:1], contract[1:]), ((), ())), pr...]
    ppermute x61 -> x63, starting transfers between devices: 87.2 us -> 75.8 us  [shift(): lax.ppermute(value, axis, [(i, (i + step) % size) for i in range(size)])]
    add x10 -> x8, other arithmetic: 11.3 us -> 1.21 us  [the longest x3 1.17 us: total_sum(): total = total + block.astype(F32)]
    convert_element_type x18 -> x10, other arithmetic: 21.4 us -> 12.2 us  [half(): return values.astype(BF)]
    squeeze x8 -> x0, local copies, waits for them, and re-layouts: 8.81 us -> none  [reduce_axis(): lax.dynamic_index_in_dim(value, lax.rem(here + k, size), at, keepdims=False)]
  transfers between devices with their start and end apart: 61 -> 63, of which waited for: 14 -> 24; matrix products, arithmetic and copies ran while one was open for 38% -> 22% of each run, Pallas kernels for 9% -> 21%
where the time goes in v2:
time: 420 us; the launch traced here: 413 us
  waiting for transfers between devices  137 us (33%)
  Pallas kernels  85.9 us (20%)
  starting transfers between devices  75.8 us (18%)
  other arithmetic  41.4 us (10%)
  local copies, waits for them, and re-layouts  39 us (9%)
  matrix products  30.8 us (7%)
    ppermute x63, waiting for transfers between devices, shift(): lax.ppermute(value, axis, [(i, (i + step) % size) for i in range(size)])  137 us
    ppermute x63, starting transfers between devices, shift(): lax.ppermute(value, axis, [(i, (i + step) % size) for i in range(size)])  75.8 us
    dot_general x11, matrix products, dot(): lax.dot_general(left, right, ((contract[:1], contract[1:]), ((), ())), pr...  30.8 us
    pallas_call x3, Pallas kernels, weight_grad(): pl.pallas_call(kernel, grid=(nz,), in_specs=[whole(pltpu.SMEM), pl.BlockS...  21.6 us
    pallas_call x1, Pallas kernels, attend_back(): pl.pallas_call(kernel, grid=(steps,), in_specs=[whole(pltpu.SMEM), pl.Blo...  17.8 us
    unnamed x159, local copies, waits for them, and re-layouts  16.2 us
    convert_element_type x10, other arithmetic, half(): return values.astype(BF)  12.2 us
    pallas_call x1, Pallas kernels, attend(): pl.pallas_call(kernel, grid=(steps,), in_specs=[whole(pltpu.SMEM), pl.Blo...  11.2 us
  transfers between devices with their start and end apart: 63, of which 24 were waited for; matrix products, arithmetic and copies ran while one was open for 22% of the time, Pallas kernels for 21%

profile of v2, /device:TPU:0, one launch (start us, length us, event | category | flops | bytes accessed | tf_op | source)
XLA Modules:
  0.0 413.1 jit_solution(5794909426891225987)
XLA Ops:
  19.8 17.7 %collective-permute-done.4 = bf16[72,2048]{1,0:T(8,128)(2,1)S(1)} collective-permute-done((bf16[72,2048]{1,0:T(8,128)(2,1)S(1)}, bf16[72,2048]{1,0:T(8,128)(2,1)S(1)}, u32[]{:S(2)}, u32[]{:S(2)}) %collective-permute-start.4) | collective-permute-done | bytes 294944 | tf_op jit(solution)/shard_map/ppermute | solution.py:52
  37.6 7.2 %collective-permute-done.5 = bf16[72,2048]{1,0:T(8,128)(2,1)S(1)} collective-permute-done((bf16[72,2048]{1,0:T(8,128)(2,1)S(1)}, bf16[72,2048]{1,0:T(8,128)(2,1)S(1)}, u32[]{:S(2)}, u32[]{:S(2)}) %collective-permute-start.5) | collective-permute-done | bytes 294944 | tf_op jit(solution)/shard_map/ppermute | solution.py:52
  54.0 13.3 %collective-permute-done.14 = bf16[64,2048]{1,0:T(8,128)(2,1)S(1)} collective-permute-done((bf16[64,2048]{1,0:T(8,128)(2,1)S(1)}, bf16[64,2048]{1,0:T(8,128)(2,1)S(1)}, u32[]{:S(2)}, u32[]{:S(2)}) %collective-permute-start.14) | collective-permute-done | bytes 262176 | tf_op jit(solution)/shard_map/ppermute | solution.py:52
  73.5 20.8 %collective-permute-done.7.refs_1_ = bf16[2,4,72,1024]{3,2,1,0:T(8,128)(2,1)S(1)} collective-permute-done((bf16[2,4,72,1024]{3,2,1,0:T(8,128)(2,1)S(1)}, bf16[2,4,72,1024]{3,2,1,0:T(8,128)(2,1)S(1)}, u32[]{:S(2)}, u32[]{:S(2)}) %collective-permute-start.7) | collective-permute-done | bytes 1179680 | tf_op jit(solution)/shard_map/ppermute | solution.py:52
  102.6 5.2 %collective-permute-done.16 = bf16[4,64,1024]{2,1,0:T(8,128)(2,1)} collective-permute-done((bf16[4,64,1024]{2,1,0:T(8,128)(2,1)}, bf16[4,64,1024]{2,1,0:T(8,128)(2,1)}, u32[]{:S(2)}, u32[]{:S(2)}) %collective-permute-start.16) | collective-permute-done | bytes 524320 | tf_op jit(solution)/shard_map/ppermute | solution.py:52
  122.0 4.0 add_convert_fusion.refs_1_
  126.0 11.2 %attend.1 = (bf16[1024,512]{1,0:T(8,128)(2,1)S(1)}, f32[4,2,1024]{2,1,0:T(2,128)S(1)}) custom-call(s32[4]{0:T(128)S(1)} %fusion.83.refs_0_, bf16[1024,1536]{1,0:T(8,128)(2,1)S(1)} %add_convert_fusion.refs_1_, s32[1,1024]{1,0:T(1,128)S(1)} %bitcast.241), custom_call_target="tpu_custom_call" | custom-call | flops 10350000128 | bytes 34500000 | tf_op jit(solution)/shard_map/attend/pallas_call | solution.py:437
  139.6 3.8 fusion.10.refs_1_
  155.4 14.8 %collective-permute-done.19.refs_3_ = bf16[2,4,64,1024]{3,2,1,0:T(8,128)(2,1)S(1)} collective-permute-done((bf16[2,4,64,1024]{3,2,1,0:T(8,128)(2,1)S(1)}, bf16[2,4,64,1024]{3,2,1,0:T(8,128)(2,1)S(1)}, u32[]{:S(2)}, u32[]{:S(2)}) %collective-permute-start.19) | collective-permute-done | bytes 1048608 | tf_op jit(solution)/shard_map/ppermute | solution.py:52
  176.5 11.0 %up_part.1 = (bf16[1024,2048]{1,0:T(8,128)(2,1)S(1)}, f32[1024,2048]{1,0:T(8,128)S(1)}) custom-call(bf16[1024,1024]{1,0:T(8,128)(2,1)S(1)} %pad_maximum_fusion.4.x_ref.refs_1_, bf16[1024,2048]{1,0:T(8,128)(2,1)S(1)} %bitcast.245, f32[1,2048]{1,0:T(1,128)S(1)} %bitcast_convert_fusion.b_ref), custom_call_target="tpu_custom_call" | custom-call | flops 6300000256 | bytes 21000000 | tf_op jit(solution)/shard_map/up_part/pallas_call | solution.py:513
  187.5 7.1 %weight_grad.4 = (bf16[4,2,128,512]{3,2,1,0:T(8,128)(2,1)S(1)}, bf16[4,2,128,512]{3,2,1,0:T(8,128)(2,1)S(1)}, bf16[4,2,128,512]{3,2,1,0:T(8,128)(2,1)S(1)}, bf16[4,2,128,512]{3,2,1,0:T(8,128)(2,1)S(1)}) custom-call(s32[3]{0:T(128)S(1)} %pad_add_fusion.place_ref.refs_0_, bf16[1024,2048]{1,0:T(8,128)(2,1)S(1)} %get-tuple-element.108.refs_1_, ...), custom_call_target="tpu_custom_call" | custom-call | flops 6300000256 | bytes 21000000 | tf_op jit(solution)/shard_map/weight_grad/pallas_call | solution.py:177
  197.7 7.4 %up_back.1 = (bf16[1024,2048]{1,0:T(8,128)(2,1)S(1)}, f32[1,2048]{1,0:T(1,128)S(1)}) custom-call(bf16[1024,1024]{1,0:T(8,128)(2,1)S(1)} %get-tuple-element.152.g_ref.refs_2_, bf16[2048,1024]{1,0:T(8,128)(2,1)S(1)} %bitcast.243, f32[1024,2048]{1,0:T(8,128)S(1)} %get-tuple-element.85.slope_ref), custom_call_target="tpu_custom_call" | custom-call | flops 5849999872 | bytes 19500000 | tf_op jit(solution)/shard_map/up_back/pallas_call | solution.py:544
  207.9 7.9 %weight_grad.3 = (bf16[4,2,64,1024]{3,2,1,0:T(8,128)(2,1)S(1)}, bf16[4,2,64,1024]{3,2,1,0:T(8,128)(2,1)S(1)}, bf16[4,2,64,1024]{3,2,1,0:T(8,128)(2,1)S(1)}, bf16[4,2,64,1024]{3,2,1,0:T(8,128)(2,1)}) custom-call(s32[3]{0:T(128)S(1)} %pad_add_fusion.place_ref.refs_0_, bf16[1024,1024]{1,0:T(8,128)(2,1)S(1)} %pad_maximum_fusion.4.x_ref.refs_1_, ...), custom_call_target="tpu_custom_call" | custom-call | flops 6300000256 | bytes 21000000 | tf_op jit(solution)/shard_map/weight_grad/pallas_call | solution.py:177
  238.9 4.1 collective-permute-done.30.refs_3_
  249.2 5.1 %collective-permute-done.33.refs_1_ = bf16[4,128,512]{2,1,0:T(8,128)(2,1)} collective-permute-done((bf16[4,128,512]{2,1,0:T(8,128)(2,1)}, bf16[4,128,512]{2,1,0:T(8,128)(2,1)}, u32[]{:S(2)}, u32[]{:S(2)}) %collective-permute-start.33) | collective-permute-done | bytes 524320 | tf_op jit(solution)/shard_map/ppermute | solution.py:52
  259.0 17.8 %attend_back.1.refs_2_ = bf16[1024,1536]{1,0:T(8,128)(2,1)S(1)} custom-call(s32[4]{0:T(128)S(1)} %fusion.83.refs_0_, bf16[1024,1536]{1,0:T(8,128)(2,1)S(1)} %copy-done.39, bf16[1024,512]{1,0:T(8,128)(2,1)S(1)} %pad_maximum_fusion.14.refs_2_, f32[4,2,1024]{2,1,0:T(2,128)S(1)} %get-tuple-element.106.refs_3_, s32[1,1024]{1,0:T(1,128)S(1)} %bitcast.242), custom_call_target="tpu_custom_call" | custom-call | flops 16199999488 | bytes 54000000 | tf_op jit(solution)/shard_map/attend_back/pallas_call | solution.py:470
  289.8 6.6 %weight_grad.5 = (bf16[4,2,64,1024]{3,2,1,0:T(8,128)(2,1)S(1)}, bf16[4,2,64,1024]{3,2,1,0:T(8,128)(2,1)}, bf16[4,2,64,1024]{3,2,1,0:T(8,128)(2,1)S(1)}, bf16[4,2,64,1024]{3,2,1,0:T(8,128)(2,1)}) custom-call(s32[3]{0:T(128)S(1)} %pad_add_fusion.place_ref.refs_0_, bf16[1024,1024]{1,0:T(8,128)(2,1)S(1)} %copy-done.3, ...), custom_call_target="tpu_custom_call" | custom-call | flops 6300000256 | bytes 21000000 | tf_op jit(solution)/shard_map/weight_grad/pallas_call | solution.py:177
  302.2 7.2 %collective-permute-start.58 = (bf16[64,2048]{1,0:T(8,128)(2,1)S(1)}, bf16[64,2048]{1,0:T(8,128)(2,1)S(1)}, u32[]{:S(2)}, u32[]{:S(2)}) collective-permute-start(bf16[64,2048]{1,0:T(8,128)(2,1)S(1)} %get-tuple-element.130), channel_id=1, source_target_pairs={{0,24},{8,0},{16,8},{24,16},{1,25},{9,1},{17,9},{25,17},{2,26},{10... | collective-permute-start | bytes 786440 | tf_op jit(solution)/shard_map/ppermute | solution.py:52
  313.5 7.8 %collective-permute-done.57 = bf16[64,2048]{1,0:T(8,128)(2,1)S(1)} collective-permute-done((bf16[64,2048]{1,0:T(8,128)(2,1)S(1)}, bf16[64,2048]{1,0:T(8,128)(2,1)S(1)}, u32[]{:S(2)}, u32[]{:S(2)}) %collective-permute-start.57) | collective-permute-done | bytes 262176 | tf_op jit(solution)/shard_map/ppermute | solution.py:52
  326.6 6.1 %fusion.98 = f32[1024,1024]{1,0:T(8,128)} fusion(bf16[1024,2048]{1,0:T(8,128)(2,1)S(1)} %copy-done.25, bf16[2048,1024]{1,0:T(8,128)(2,1)S(1)} %bitcast.244), kind=kOutput, calls=%fused_computation.259 | convolution fusion | flops 4294967296 | bytes 12582912 | tf_op jit(solution)/shard_map/dot_general | solution.py:39
  349.0 6.1 %collective-permute-start.42 = (f32[384]{0:T(512)S(1)}, f32[384]{0:T(512)S(1)}, u32[]{:S(2)}, u32[]{:S(2)}) collective-permute-start(f32[384]{0:T(512)S(1)} %get-tuple-element.142), channel_id=1, source_target_pairs={{0,8},{8,16},{16,24},{24,0},{1,9},{9,17},{17,25},{25,1},{2,10},{10... | collective-permute-start | bytes 4616 | tf_op jit(solution)/shard_map/ppermute | solution.py:52
  367.7 5.7 %collective-permute-done.48.refs_1_ = bf16[4,64,1024]{2,1,0:T(8,128)(2,1)S(1)} collective-permute-done((bf16[4,64,1024]{2,1,0:T(8,128)(2,1)}, bf16[4,64,1024]{2,1,0:T(8,128)(2,1)S(1)}, u32[]{:S(2)}, u32[]{:S(2)}) %collective-permute-start.48) | collective-permute-done | bytes 524320 | tf_op jit(solution)/shard_map/ppermute | solution.py:52
  388.9 7.3 %collective-permute-done.51 = bf16[64,2048]{1,0:T(8,128)(2,1)S(1)} collective-permute-done((bf16[64,2048]{1,0:T(8,128)(2,1)S(1)}, bf16[64,2048]{1,0:T(8,128)(2,1)S(1)}, u32[]{:S(2)}, u32[]{:S(2)}) %collective-permute-start.51) | collective-permute-done | bytes 262176 | tf_op jit(solution)/shard_map/ppermute | solution.py:52
  400.2 11.3 %collective-permute-done.37 = bf16[256,1024]{1,0:T(8,128)(2,1)S(1)} collective-permute-done((bf16[256,1024]{1,0:T(8,128)(2,1)S(1)}, bf16[256,1024]{1,0:T(8,128)(2,1)S(1)}, u32[]{:S(2)}, u32[]{:S(2)}) %collective-permute-start.37) | collective-permute-done | bytes 524320 | tf_op jit(solution)/shard_map/ppermute | solution.py:52
  (446 shorter events, 193.4 us)
Async XLA Ops:
  2.6 44.5 %collective-permute-start.21 = (bf16[128,512]{1,0:T(8,128)(2,1)}, bf16[128,512]{1,0:T(8,128)(2,1)}, u32[]{:S(2)}, u32[]{:S(2)}) collective-permute-start(bf16[128,512]{1,0:T(8,128)(2,1)} %get-tuple-element.194), channel_id=1, source_target_pairs={{0,4},{4,0},{1,5},{5,1},{2,6},{6,2},{3,7},{7,3},{8,12},{12,8},{9,1... | collective-permute-start | bytes 393224 | tf_op jit(solution)/shard_map/ppermute | solution.py:52
  5.6 41.6 %collective-permute-start.20 = (bf16[128,512]{1,0:T(8,128)(2,1)}, bf16[128,512]{1,0:T(8,128)(2,1)}, u32[]{:S(2)}, u32[]{:S(2)}) collective-permute-start(bf16[128,512]{1,0:T(8,128)(2,1)} %get-tuple-element.195), channel_id=1, source_target_pairs={{0,2},{2,0},{1,3},{3,1},{4,6},{6,4},{5,7},{7,5},{8,10},{10,8},{9,1... | collective-permute-start | bytes 393224 | tf_op jit(solution)/shard_map/ppermute | solution.py:52
  12.9 58.2 %collective-permute-start = (bf16[2,256,1024]{2,1,0:T(8,128)(2,1)}, bf16[2,256,1024]{2,1,0:T(8,128)(2,1)S(1)}, u32[]{:S(2)}, u32[]{:S(2)}) collective-permute-start(bf16[2,256,1024]{2,1,0:T(8,128)(2,1)} %get-tuple-element.157), channel_id=1, source_target_pairs={{0,2},{2,0},{1,3},{3,1},{4,6},{6,4},{5,7},{7,5},{8,10},{10,8},{9,1... | collective-permute-start | bytes 3145736 | tf_op jit(solution)/shard_map/ppermute | solution.py:52
  67.4 26.9 %collective-permute-start.7 = (bf16[2,4,72,1024]{3,2,1,0:T(8,128)(2,1)S(1)}, bf16[2,4,72,1024]{3,2,1,0:T(8,128)(2,1)S(1)}, u32[]{:S(2)}, u32[]{:S(2)}) collective-permute-start(bf16[2,4,72,1024]{3,2,1,0:T(8,128)(2,1)S(1)} %pad_maximum_fusion.7.refs_0_), channel_id=1, source_target_pairs={{0,4},{4,0},{1,5},{5,1},{2,6},{6,2},{3,7},{7,3},{8,12},{12,8},{9,1... | collective-permute-start | bytes 3538952 | tf_op jit(solution)/shard_map/ppermute | solution.py:52
  68.6 27.0 %collective-permute-start.9 = (bf16[2,4,72,1024]{3,2,1,0:T(8,128)(2,1)S(1)}, bf16[2,4,72,1024]{3,2,1,0:T(8,128)(2,1)S(1)}, u32[]{:S(2)}, u32[]{:S(2)}) collective-permute-start(bf16[2,4,72,1024]{3,2,1,0:T(8,128)(2,1)S(1)} %pad_maximum_fusion.8.refs_2_), channel_id=1, source_target_pairs={{0,2},{2,0},{1,3},{3,1},{4,6},{6,4},{5,7},{7,5},{8,10},{10,8},{9,1... | collective-permute-start | bytes 3538952 | tf_op jit(solution)/shard_map/ppermute | solution.py:52
  72.8 43.6 %collective-permute-start.1 = (bf16[2,512,1024]{2,1,0:T(8,128)(2,1)}, bf16[2,512,1024]{2,1,0:T(8,128)(2,1)}, u32[]{:S(2)}, u32[]{:S(2)}) collective-permute-start(bf16[2,512,1024]{2,1,0:T(8,128)(2,1)} %pad_maximum_fusion.1), channel_id=1, source_target_pairs={{0,1},{1,0},{2,3},{3,2},{4,5},{5,4},{6,7},{7,6},{8,9},{9,8},{10,11... | collective-permute-start | bytes 6291464 | tf_op jit(solution)/shard_map/ppermute | solution.py:52
  102.6 41.9 %collective-permute-start.11 = (bf16[1024,512]{1,0:T(8,128)(2,1)S(1)}, bf16[1024,512]{1,0:T(8,128)(2,1)}, u32[]{:S(2)}, u32[]{:S(2)}) collective-permute-start(bf16[1024,512]{1,0:T(8,128)(2,1)S(1)} %bitcast.238), channel_id=1, source_target_pairs={{0,1},{1,0},{2,3},{3,2},{4,5},{5,4},{6,7},{7,6},{8,9},{9,8},{10,11... | collective-permute-start | bytes 3145736 | tf_op jit(solution)/shard_map/ppermute | solution.py:52
  110.1 33.3 %collective-permute-start.24 = (bf16[4,128,512]{2,1,0:T(8,128)(2,1)}, bf16[4,128,512]{2,1,0:T(8,128)(2,1)}, u32[]{:S(2)}, u32[]{:S(2)}) collective-permute-start(bf16[4,128,512]{2,1,0:T(8,128)(2,1)} %pad_maximum_fusion.21), channel_id=1, source_target_pairs={{0,24},{8,0},{16,8},{24,16},{1,25},{9,1},{17,9},{25,17},{2,26},{10... | collective-permute-start | bytes 1572872 | tf_op jit(solution)/shard_map/ppermute | solution.py:52
  110.1 42.8 %collective-permute-start.23 = (bf16[4,128,512]{2,1,0:T(8,128)(2,1)}, bf16[4,128,512]{2,1,0:T(8,128)(2,1)}, u32[]{:S(2)}, u32[]{:S(2)}) collective-permute-start(bf16[4,128,512]{2,1,0:T(8,128)(2,1)} %pad_maximum_fusion.21), channel_id=1, source_target_pairs={{0,16},{8,24},{16,0},{24,8},{1,17},{9,25},{17,1},{25,9},{2,18},{10... | collective-permute-start | bytes 1572872 | tf_op jit(solution)/shard_map/ppermute | solution.py:52
  110.1 43.9 %collective-permute-start.22 = (bf16[4,128,512]{2,1,0:T(8,128)(2,1)}, bf16[4,128,512]{2,1,0:T(8,128)(2,1)}, u32[]{:S(2)}, u32[]{:S(2)}) collective-permute-start(bf16[4,128,512]{2,1,0:T(8,128)(2,1)} %pad_maximum_fusion.21), channel_id=1, source_target_pairs={{0,8},{8,16},{16,24},{24,0},{1,9},{9,17},{17,25},{25,1},{2,10},{10... | collective-permute-start | bytes 1572872 | tf_op jit(solution)/shard_map/ppermute | solution.py:52
  116.4 53.7 %collective-permute-start.17 = (bf16[2,4,64,1024]{3,2,1,0:T(8,128)(2,1)}, bf16[2,4,64,1024]{3,2,1,0:T(8,128)(2,1)}, u32[]{:S(2)}, u32[]{:S(2)}) collective-permute-start(bf16[2,4,64,1024]{3,2,1,0:T(8,128)(2,1)} %pad_maximum_fusion.10.refs_0_), channel_id=1, source_target_pairs={{0,4},{4,0},{1,5},{5,1},{2,6},{6,2},{3,7},{7,3},{8,12},{12,8},{9,1... | collective-permute-start | bytes 3145736 | tf_op jit(solution)/shard_map/ppermute | solution.py:52
  144.5 25.6 %collective-permute-start.19 = (bf16[2,4,64,1024]{3,2,1,0:T(8,128)(2,1)S(1)}, bf16[2,4,64,1024]{3,2,1,0:T(8,128)(2,1)S(1)}, u32[]{:S(2)}, u32[]{:S(2)}) collective-permute-start(bf16[2,4,64,1024]{3,2,1,0:T(8,128)(2,1)S(1)} %copy-done.4), channel_id=1, source_target_pairs={{0,2},{2,0},{1,3},{3,1},{4,6},{6,4},{5,7},{7,5},{8,10},{10,8},{9,1... | collective-permute-start | bytes 3145736 | tf_op jit(solution)/shard_map/ppermute | solution.py:52
  170.2 25.5 %collective-permute-start.25 = (bf16[2,4,128,512]{3,2,0,1:T(8,128)(2,1)S(1)}, bf16[2,4,128,512]{3,2,0,1:T(8,128)(2,1)S(1)}, u32[]{:S(2)}, u32[]{:S(2)}) collective-permute-start(bf16[2,4,128,512]{3,2,0,1:T(8,128)(2,1)S(1)} %pad_maximum_fusion.12), channel_id=1, source_target_pairs={{0,4},{4,0},{1,5},{5,1},{2,6},{6,2},{3,7},{7,3},{8,12},{12,8},{9,1... | collective-permute-start | bytes 3145736 | tf_op jit(solution)/shard_map/ppermute | solution.py:52
  216.8 26.2 %collective-permute-start.30 = (bf16[4,2,64,1024]{3,2,1,0:T(8,128)(2,1)}, bf16[4,2,64,1024]{3,2,1,0:T(8,128)(2,1)S(1)}, u32[]{:S(2)}, u32[]{:S(2)}) collective-permute-start(bf16[4,2,64,1024]{3,2,1,0:T(8,128)(2,1)} %get-tuple-element.92), channel_id=1, source_target_pairs={{0,4},{4,0},{1,5},{5,1},{2,6},{6,2},{3,7},{7,3},{8,12},{12,8},{9,1... | collective-permute-start | bytes 3145736 | tf_op jit(solution)/shard_map/ppermute | solution.py:52
  217.8 26.0 %collective-permute-start.29 = (bf16[4,2,64,1024]{3,2,1,0:T(8,128)(2,1)S(1)}, bf16[4,2,64,1024]{3,2,1,0:T(8,128)(2,1)S(1)}, u32[]{:S(2)}, u32[]{:S(2)}) collective-permute-start(bf16[4,2,64,1024]{3,2,1,0:T(8,128)(2,1)S(1)} %get-tuple-element.90), channel_id=1, source_target_pairs={{0,2},{2,0},{1,3},{3,1},{4,6},{6,4},{5,7},{7,5},{8,10},{10,8},{9,1... | collective-permute-start | bytes 3145736 | tf_op jit(solution)/shard_map/ppermute | solution.py:52
  223.9 30.4 %collective-permute-start.33 = (bf16[4,128,512]{2,1,0:T(8,128)(2,1)}, bf16[4,128,512]{2,1,0:T(8,128)(2,1)}, u32[]{:S(2)}, u32[]{:S(2)}) collective-permute-start(bf16[4,128,512]{2,1,0:T(8,128)(2,1)} %get-tuple-element.101), channel_id=1, source_target_pairs={{0,4},{4,0},{1,5},{5,1},{2,6},{6,2},{3,7},{7,3},{8,12},{12,8},{9,1... | collective-permute-start | bytes 1572872 | tf_op jit(solution)/shard_map/ppermute | solution.py:52
  225.5 29.7 %collective-permute-start.34 = (bf16[4,128,512]{2,1,0:T(8,128)(2,1)}, bf16[4,128,512]{2,1,0:T(8,128)(2,1)}, u32[]{:S(2)}, u32[]{:S(2)}) collective-permute-start(bf16[4,128,512]{2,1,0:T(8,128)(2,1)} %get-tuple-element.103), channel_id=1, source_target_pairs={{0,2},{2,0},{1,3},{3,1},{4,6},{6,4},{5,7},{7,5},{8,10},{10,8},{9,1... | collective-permute-start | bytes 1572872 | tf_op jit(solution)/shard_map/ppermute | solution.py:52
  238.3 46.9 %collective-permute-start.45 = (bf16[1024,512]{1,0:T(8,128)(2,1)}, bf16[1024,512]{1,0:T(8,128)(2,1)}, u32[]{:S(2)}, u32[]{:S(2)}) collective-permute-start(bf16[1024,512]{1,0:T(8,128)(2,1)} %convolution_convert_fusion), channel_id=1, source_target_pairs={{0,1},{1,0},{2,3},{3,2},{4,5},{5,4},{6,7},{7,6},{8,9},{9,8},{10,11... | collective-permute-start | bytes 3145736 | tf_op jit(solution)/shard_map/ppermute | solution.py:52
  246.1 50.3 %collective-permute-start.54 = (bf16[4,64,1024]{2,1,0:T(8,128)(2,1)}, bf16[4,64,1024]{2,1,0:T(8,128)(2,1)}, u32[]{:S(2)}, u32[]{:S(2)}) collective-permute-start(bf16[4,64,1024]{2,1,0:T(8,128)(2,1)} %get-tuple-element.124), channel_id=1, source_target_pairs={{0,4},{4,0},{1,5},{5,1},{2,6},{6,2},{3,7},{7,3},{8,12},{12,8},{9,1... | collective-permute-start | bytes 1572872 | tf_op jit(solution)/shard_map/ppermute | solution.py:52
  247.1 49.3 %collective-permute-start.55 = (bf16[4,64,1024]{2,1,0:T(8,128)(2,1)}, bf16[4,64,1024]{2,1,0:T(8,128)(2,1)}, u32[]{:S(2)}, u32[]{:S(2)}) collective-permute-start(bf16[4,64,1024]{2,1,0:T(8,128)(2,1)} %get-tuple-element.126), channel_id=1, source_target_pairs={{0,2},{2,0},{1,3},{3,1},{4,6},{6,4},{5,7},{7,5},{8,10},{10,8},{9,1... | collective-permute-start | bytes 1572872 | tf_op jit(solution)/shard_map/ppermute | solution.py:52
  296.4 26.6 %collective-permute-start.35 = (bf16[512,1024]{1,0:T(8,128)(2,1)S(1)}, bf16[512,1024]{1,0:T(8,128)(2,1)S(1)}, u32[]{:S(2)}, u32[]{:S(2)}) collective-permute-start(bf16[512,1024]{1,0:T(8,128)(2,1)S(1)} %fusion.40), channel_id=1, source_target_pairs={{0,1},{1,0},{2,3},{3,2},{4,5},{5,4},{6,7},{7,6},{8,9},{9,8},{10,11... | collective-permute-start | bytes 3145736 | tf_op jit(solution)/shard_map/ppermute | solution.py:52
  310.4 46.8 %collective-permute-start.46 = (bf16[4,2,64,1024]{3,2,1,0:T(8,128)(2,1)}, bf16[4,2,64,1024]{3,2,1,0:T(8,128)(2,1)S(1)}, u32[]{:S(2)}, u32[]{:S(2)}) collective-permute-start(bf16[4,2,64,1024]{3,2,1,0:T(8,128)(2,1)} %get-tuple-element.112), channel_id=1, source_target_pairs={{0,2},{2,0},{1,3},{3,1},{4,6},{6,4},{5,7},{7,5},{8,10},{10,8},{9,1... | collective-permute-start | bytes 3145736 | tf_op jit(solution)/shard_map/ppermute | solution.py:52
  312.0 45.2 %collective-permute-start.47 = (bf16[4,2,64,1024]{3,2,1,0:T(8,128)(2,1)}, bf16[4,2,64,1024]{3,2,1,0:T(8,128)(2,1)S(1)}, u32[]{:S(2)}, u32[]{:S(2)}) collective-permute-start(bf16[4,2,64,1024]{3,2,1,0:T(8,128)(2,1)} %get-tuple-element.114), channel_id=1, source_target_pairs={{0,4},{4,0},{1,5},{5,1},{2,6},{6,2},{3,7},{7,3},{8,12},{12,8},{9,1... | collective-permute-start | bytes 3145736 | tf_op jit(solution)/shard_map/ppermute | solution.py:52
  365.9 30.6 %collective-permute-start.36 = (bf16[512,1024]{1,0:T(8,128)(2,1)}, bf16[512,1024]{1,0:T(8,128)(2,1)S(1)}, u32[]{:S(2)}, u32[]{:S(2)}) collective-permute-start(bf16[512,1024]{1,0:T(8,128)(2,1)} %slice.459), channel_id=1, source_target_pairs={{0,1},{1,0},{2,3},{3,2},{4,5},{5,4},{6,7},{7,6},{8,9},{9,8},{10,11... | collective-permute-start | bytes 3145736 | tf_op jit(solution)/shard_map/ppermute | solution.py:52
  (117 other events, 1886.3 us)

commit v3 on v2

--- a/solution.py
+++ b/solution.py
@@ -40,7 +40,7 @@
 
 
 def cost(microseconds):
-    return pl.CostEstimate(flops=int(microseconds * 9e8), bytes_accessed=int(microseconds * 3e6), transcendentals=0)
+    return pl.CostEstimate(flops=int(microseconds * 2.70e8), bytes_accessed=int(microseconds * 0.90e6), transcendentals=0)
 
 
 def after(value, *others):
@@ -106,7 +106,7 @@
                         out[(*at, slice(None), pl.ds(into, columns))] = source[row : row + rows, column : column + columns]
 
     def out_spec(shape):
-        return pl.BlockSpec((1, ny, ng, *shape), lambda i, place_ref: (lax.rem(place_ref[0] - i + nz, nz), 0, 0, 0, 0))
+        return pl.BlockSpec((1, ny, ng, *shape), lambda i, place_ref: (i, 0, 0, 0, 0))
 
     return pl.pallas_call(
         kernel,
@@ -121,13 +121,17 @@
         compiler_params=pltpu.CompilerParams(vmem_limit_bytes=16 << 20),
         cost_estimate=cost(4),
         name="assemble",
-    )(place, *firsts, *seconds)
-
-
-def gather_over_z(shard):
-    parts = gather_relative(shard, "z")
-    middle = shard.shape[1] // 2
-    return jnp.stack([p[:, :middle] for p in parts]), jnp.stack([p[:, middle:] for p in parts])
+    )(place, *[*firsts, *seconds])
+
+
+def gather_over_z(value):
+    copies = jnp.broadcast_to(value[None], (lax.axis_size("z"), *value.shape))
+    return lax.all_to_all(copies, "z", 0, 0, tiled=True)
+
+
+def halves(values):
+    middle = values.shape[-1] // 2
+    return values[..., :middle], values[..., middle:]
 
 
 def gather_once(first, second):
@@ -190,7 +194,7 @@
         compiler_params=pltpu.CompilerParams(vmem_limit_bytes=20 << 20),
         cost_estimate=cost(7),
         name="weight_grad",
-    )(place, left, right, *extra)
+    )(place, *[left, right, *extra])
     return outs[:ng], outs[ng:]
 
 
@@ -225,31 +229,35 @@
         compiler_params=pltpu.CompilerParams(vmem_limit_bytes=12 << 20),
         cost_estimate=cost(3.5),
         name="add_split",
-    )(place, *first, *second)
+    )(place, *[*first, *second])
     return outs[:ny], outs[ny:]
 
 
-def split_over_z(place, first, second):
+def split_over_z(first, second, more):
     ny, ng = len(first), len(second)
     nz, rows, columns = first[0].shape
-
-    def kernel(place_ref, *refs):
-        firsts, seconds, outs = refs[:ny], refs[ny : ny + ng], refs[ny + ng :]
-        z = place_ref[0]
-        for k in range(nz):
-            at = lax.rem(z + k, nz)
-            outs[k][:, :columns] = total_of(firsts, at).astype(outs[k].dtype)
-            outs[k][:, columns:] = total_of(seconds, at).astype(outs[k].dtype)
+    extra = [] if more is None else [more]
+    count = 0 if more is None else more.shape[1]
+    n_in = ny + ng + len(extra)
+
+    def kernel(*refs):
+        out = refs[n_in]
+        out[0, :rows, :columns] = half(total_of(refs[:ny], 0))
+        out[0, :rows, columns:] = half(total_of(refs[ny : ny + ng], 0))
+        if extra:
+            out[0, rows:] = half(refs[n_in - 1][0])
 
     return pl.pallas_call(
         kernel,
-        in_specs=[whole(pltpu.SMEM)] + [whole()] * (ny + ng),
-        out_specs=[whole()] * nz,
-        out_shape=[jax.ShapeDtypeStruct((rows, 2 * columns), BF if k else F32) for k in range(nz)],
+        grid=(nz,),
+        in_specs=[pl.BlockSpec((1, rows, columns), lambda i: (i, 0, 0))] * (ny + ng)
+        + [pl.BlockSpec((1, *m.shape[1:]), lambda i: (i, 0, 0)) for m in extra],
+        out_specs=pl.BlockSpec((1, rows + count, 2 * columns), lambda i: (i, 0, 0)),
+        out_shape=jax.ShapeDtypeStruct((nz, rows + count, 2 * columns), BF),
         compiler_params=pltpu.CompilerParams(vmem_limit_bytes=12 << 20),
         cost_estimate=cost(2.5),
         name="split_over_z",
-    )(place, *first, *second)
+    )(*first, *second, *extra)
 
 
 def send_parts(first, second, axis_first, axis_second):
@@ -264,11 +272,8 @@
     return send_parts(*add_split(place, sizes, first, second), "y", "g")
 
 
-def reduce_over_z(place, parts, *others):
-    first, second = parts
-    first = [after(first[0], *others)] + first[1:]
-    blocks = split_over_z(place, first, second)
-    return [blocks[0]] + [shift(block, "z", k) for k, block in enumerate(blocks) if k]
+def sum_over_z(blocks):
+    return jnp.sum(lax.all_to_all(blocks, "z", 0, 0, tiled=True).astype(F32), axis=0)
 
 
 def total_sum(blocks):
@@ -523,7 +528,7 @@
         compiler_params=pltpu.CompilerParams(vmem_limit_bytes=16 << 20),
         cost_estimate=cost(7),
         name="up_part",
-    )(normed, weight, bias[None])
+    )(*[normed, weight], bias[None])
 
 
 def up_back(grad_down, weight, slope):
@@ -554,7 +559,7 @@
         compiler_params=pltpu.CompilerParams(vmem_limit_bytes=16 << 20),
         cost_estimate=cost(6.5),
         name="up_back",
-    )(grad_down, weight, slope)
+    )(*[grad_down, weight, slope])
 
 
 def body(
@@ -626,10 +631,12 @@
     shard_d = half(w_down)
     middle_d = width // 2
 
-    first_a, second_a = gather_over_z(shard_a)
     first_d, second_d = gather_once(shard_d[:, :middle_d], shard_d[:, middle_d:])
-    first_u, second_u = gather_over_z(after(shard_u, first_a, second_a))
+    first_a, second_a = halves(gather_over_z(after(shard_a, first_d, second_d)))
+    first_u, second_u = halves(gather_over_z(after(shard_u, first_a, second_a)))
     first_a, second_a = gather_once(first_a, second_a)
+    both_d = jnp.concatenate([first_d, second_d], axis=0)
+    both_d = gather_over_z(after(both_d, first_u, second_u, first_a, second_a))
     first_a, second_a = gather_twice(first_a, second_a)
     side = 3 * part - 2 * part
     wqkv, wo, vector_rows = assemble(
@@ -664,8 +671,7 @@
     normal_all, _ = norm_parts(both_all[0].astype(F32))
     normed_attn = half(normal_all * h_gain_attn + h_shift_attn)
     grad_down = half(depth * both_all[1].astype(F32))
-    qkv = half(dot(normed_attn, wqkv, (1, 0)) + bias_qkv)
-    both_d = gather_relative(after(jnp.concatenate([first_d, second_d], axis=0), first_u), "z")
+    qkv = half(dot(after(normed_attn, first_u, second_u), wqkv, (1, 0)) + bias_qkv)
     attended_heads, logs = attend(qkv, first_token, order, local, head_dim)
     first_u, second_u = gather_twice(first_u, second_u)
     wo = jnp.concatenate(by_place(gather_relative(wo, "t"), "t", -1), axis=1)
@@ -683,8 +689,7 @@
         [(block_rows, ff_part)],
     )
     wu = wu.reshape(width, ff_part)
-    first_d = jnp.stack([b[:ng] for b in both_d], axis=1)
-    second_d = jnp.stack([b[ng:] for b in both_d], axis=1)
+    first_d, second_d = both_d[:, :ng].swapaxes(0, 1), both_d[:, ng:].swapaxes(0, 1)
     first_d, second_d = gather_twice(after(first_d, *first_u, *second_u), after(second_d, *first_u, *second_u))
     active, slope = up_part(normed_mlp, wu, h_bias_up)
 
@@ -693,7 +698,8 @@
         mine = dot(after(left[:own], *blocks), right, (1, 1))
         return total_sum([mine] + [shift(block, "t", -k - 1) for k, block in enumerate(blocks)])
 
-    down_parts = send_parts(*weight_grad(place, sizes, active, grad_down), "g", "y")
+    down_blocks = weight_grad(place, sizes, active, grad_down)
+    down_parts = send_parts(*down_blocks, "g", "y")
     (wd,) = assemble(
         place,
         first_d,
@@ -702,7 +708,7 @@
         [(ff_shard, width)],
     )
     wd = wd.reshape(ff_part, width)
-    grad_up, d_bias_up = up_back(grad_down, wd, slope)
+    grad_up, d_bias_up = up_back(after(grad_down, *down_blocks[0]), wd, slope)
     up_blocks = weight_grad(place, sizes, normed_mlp, grad_up)
     down_parts = reduce_in_layer(place, sizes, down_parts, *up_blocks[0])
     up_parts = send_parts(*up_blocks, "g", "y")
@@ -728,27 +734,26 @@
         return jnp.stack(by_place(return_relative([blocks[k] for k in range(ng)], "g"), "g", 1), axis=0)
 
     up_parts = reduce_in_layer(place, sizes, up_parts, grad_attended)
-    down_parts = reduce_over_z(place, down_parts, grad_attended)
-    grad_attended = after(grad_attended, up_parts[0][0], down_parts[0])
+    down_blocks = split_over_z(*down_parts, None)
+    sum_down = sum_over_z(down_blocks)
+    grad_attended = after(grad_attended, up_parts[0][0], down_blocks)
     d_qkv = attend_back(qkv, grad_attended, logs, first_token, order, local, head_dim)
-    sum_down = total_sum(down_parts)
     a_blocks = weight_grad(place, sizes, normed_attn, d_qkv, half(d_proj))
     a_parts = send_parts(*a_blocks, "g", "y")
-    up_parts = reduce_over_z(place, up_parts, *a_blocks[0])
-    e1 = own_sum(d_qkv, wqkv)
-    lowered = dot(after(active, e1), wd, (1, 0))
-    lowered = total_sum(
-        [lowered[:own]] + [shift(half(lowered[k * own : (k + 1) * own]), "t", -k) for k in range(1, nt)]
-    )
-    block_out = to_rows(half(hidden + depth * (lowered + h_bias_down)).reshape(ng, local, width))
+    up_blocks = split_over_z([after(up_parts[0][0], *a_blocks[0])] + up_parts[0][1:], up_parts[1], None)
+    sum_up = sum_over_z(up_blocks)
+    e1 = own_sum(after(d_qkv, up_blocks), wqkv)
     normal_one, inverse_one = norm_parts(x_own)
     d_gain_attn = jnp.sum(e1 * normal_one, axis=0)
     d_shift_attn = jnp.sum(e1, axis=0)
     grad_input = grad_hidden + norm_back(e1, normal_one, inverse_one, h_gain_attn)
+    a_parts = reduce_in_layer(place, sizes, a_parts, e1)
+    lowered = dot(after(active, a_parts[0][0]), wd, (1, 0))
+    lowered = total_sum(
+        [lowered[:own]] + [shift(half(lowered[k * own : (k + 1) * own]), "t", -k) for k in range(1, nt)]
+    )
+    block_out = to_rows(half(hidden + depth * (lowered + h_bias_down)).reshape(ng, local, width))
     grad_input = to_rows(half(grad_input).reshape(ng, local, width)).astype(F32)
-    a_parts = reduce_in_layer(place, sizes, a_parts, e1)
-    sum_up = total_sum(up_parts)
-    sum_a = total_sum(reduce_over_z(place, a_parts))
 
     def by_owner(full):
         return full.reshape(chips, nt, -1)
@@ -774,8 +779,13 @@
         axis=2,
     )
     sums = reduce_axis(sums, "t", 1).reshape(nz, ny, ng, count)
-    for axis, at in (("g", 2), ("y", 1), ("z", 0)):
-        sums = reduce_axis(sums, axis, at)
+    sums = reduce_axis(reduce_axis(sums, "g", 2), "y", 1)
+    high = half(sums)
+    more = jnp.stack([high.astype(F32), sums - high.astype(F32)], axis=1)
+    more = jnp.pad(more, ((0, 0), (0, 6), (0, 4 * part - count)))
+    sum_a = sum_over_z(split_over_z(*a_parts, more))
+    sums = sum_a[block_rows, :count] + sum_a[block_rows + 1, :count]
+    sum_a = sum_a[:block_rows]
     out_vectors = [sums[offsets[i] : offsets[i + 1]] for i in range(len(counts))]
 
     up = swap_axis(sum_up.reshape(nt, shard, ff_part), "t", 0)

time: 420 us -> 386 us (0.919)
  waiting for transfers between devices: 137 us -> 103 us
  starting transfers between devices: 75.8 us -> 59 us
  other arithmetic: 41.4 us -> 53.7 us
    ppermute x63 -> x42, waiting for transfers between devices: 137 us -> 82.6 us  [shift(): lax.ppermute(value, axis, [(i, (i + step) % size) for i in range(size)])]
    ppermute x63 -> x42, starting transfers between devices: 75.8 us -> 32.3 us  [shift(): lax.ppermute(value, axis, [(i, (i + step) % size) for i in range(size)])]
    all_to_all x0 -> x6, starting transfers between devices: none -> 26.7 us  [the longest x3 13.8 us: gather_over_z(): return lax.all_to_all(copies, 'z', 0, 0, tiled=True)]
    all_to_all x0 -> x6, waiting for transfers between devices: none -> 20.6 us  [the longest x3 14.1 us: gather_over_z(): return lax.all_to_all(copies, 'z', 0, 0, tiled=True)]
    pallas_call x3, Pallas kernels: 5.65 us -> 10 us  [assemble(): pl.pallas_call(kernel, grid_spec=pltpu.PrefetchScalarGridSpec(num_scalar_...]
    unnamed x159 -> x118, local copies, waits for them, and re-layouts: 16.2 us -> 14.7 us
  transfers between devices with their start and end apart: 63 -> 48, of which waited for: 24 -> 18; matrix products, arithmetic and copies ran while one was open for 22% -> 28% of each run, Pallas kernels for 21% -> 23%
where the time goes in v3:
time: 386 us; the launch traced here: 380 us
  waiting for transfers between devices  103 us (27%)
  Pallas kernels  89 us (23%)
  starting transfers between devices  59 us (15%)
  other arithmetic  53.7 us (14%)
  local copies, waits for them, and re-layouts  39.4 us (10%)
  matrix products  33.2 us (9%)
    ppermute x42, waiting for transfers between devices, shift(): lax.ppermute(value, axis, [(i, (i + step) % size) for i in range(size)])  82.6 us
    dot_general x11, matrix products, dot(): lax.dot_general(left, right, ((contract[:1], contract[1:]), ((), ())), pr...  33.2 us
    ppermute x42, starting transfers between devices, shift(): lax.ppermute(value, axis, [(i, (i + step) % size) for i in range(size)])  32.3 us
    pallas_call x3, Pallas kernels, weight_grad(): pl.pallas_call(kernel, grid=(nz,), in_specs=[whole(pltpu.SMEM), pl.BlockS...  20.6 us
    pallas_call x1, Pallas kernels, attend_back(): pl.pallas_call(kernel, grid=(steps,), in_specs=[whole(pltpu.SMEM), pl.Blo...  17.8 us
    unnamed x118, local copies, waits for them, and re-layouts  14.7 us
    convert_element_type x10, other arithmetic, half(): return values.astype(BF)  14.4 us
    all_to_all x3, waiting for transfers between devices, gather_over_z(): return lax.all_to_all(copies, 'z', 0, 0, tiled=True)  14.1 us
  transfers between devices with their start and end apart: 48, of which 18 were waited for; matrix products, arithmetic and copies ran while one was open for 28% of the time, Pallas kernels for 23%

profile of v3, /device:TPU:0, one launch (start us, length us, event | category | flops | bytes accessed | tf_op | source)
XLA Modules:
  0.0 379.8 jit_solution(2497818618656586789)
XLA Ops:
  12.0 4.9 %all-to-all-start = ((bf16[4,72,2048]{2,1,0:T(8,128)(2,1)}), bf16[4,72,2048]{2,1,0:T(8,128)(2,1)S(1)}, u32[]{:S(2)}, u32[]{:S(2)}) async-start(bf16[4,72,2048]{2,1,0:T(8,128)(2,1)} %broadcast_in_dim.34), calls=%async_computation | async-start | bytes 2359296 | tf_op jit(solution)/shard_map/all_to_all | solution.py:129
  16.8 17.1 %collective-permute-done = bf16[2,256,1024]{2,1,0:T(8,128)(2,1)S(1)} collective-permute-done((bf16[2,256,1024]{2,1,0:T(8,128)(2,1)}, bf16[2,256,1024]{2,1,0:T(8,128)(2,1)S(1)}, u32[]{:S(2)}, u32[]{:S(2)}) %collective-permute-start) | collective-permute-done | bytes 1048608 | tf_op jit(solution)/shard_map/ppermute | solution.py:52
  39.7 5.4 %all-to-all-done = bf16[4,72,2048]{2,1,0:T(8,128)(2,1)S(1)} async-done(((bf16[4,72,2048]{2,1,0:T(8,128)(2,1)}), bf16[4,72,2048]{2,1,0:T(8,128)(2,1)S(1)}, u32[]{:S(2)}, u32[]{:S(2)}) %all-to-all-start) | async-done | bytes 1179680 | tf_op jit(solution)/shard_map/all_to_all | solution.py:129
  56.8 4.3 %collective-permute-done.3 = bf16[4,72,1024]{2,1,0:T(8,128)(2,1)S(1)} collective-permute-done((bf16[4,72,1024]{2,1,0:T(8,128)(2,1)}, bf16[4,72,1024]{2,1,0:T(8,128)(2,1)S(1)}, u32[]{:S(2)}, u32[]{:S(2)}) %collective-permute-start.3) | collective-permute-done | bytes 589856 | tf_op jit(solution)/shard_map/ppermute | solution.py:52
  72.8 8.7 %all-to-all-done.1 = bf16[4,64,2048]{2,1,0:T(8,128)(2,1)} async-done(((bf16[4,64,2048]{2,1,0:T(8,128)(2,1)}), bf16[4,64,2048]{2,1,0:T(8,128)(2,1)}, u32[]{:S(2)}, u32[]{:S(2)}) %all-to-all-start.1) | async-done | bytes 1048608 | tf_op jit(solution)/shard_map/all_to_all | solution.py:129
  85.4 4.7 %all-to-all-start.2 = ((bf16[4,4,128,512]{3,2,1,0:T(8,128)(2,1)}), bf16[4,4,128,512]{3,2,1,0:T(8,128)(2,1)}, u32[]{:S(2)}, u32[]{:S(2)}) async-start(bf16[4,4,128,512]{3,2,1,0:T(8,128)(2,1)} %broadcast_in_dim.37), calls=%async_computation.2 | async-start | bytes 4194304 | tf_op jit(solution)/shard_map/all_to_all | solution.py:129
  103.6 7.1 %collective-permute-done.7 = bf16[4,64,1024]{2,1,0:T(8,128)(2,1)S(1)} collective-permute-done((bf16[4,64,1024]{2,1,0:T(8,128)(2,1)}, bf16[4,64,1024]{2,1,0:T(8,128)(2,1)S(1)}, u32[]{:S(2)}, u32[]{:S(2)}) %collective-permute-start.7) | collective-permute-done | bytes 524320 | tf_op jit(solution)/shard_map/ppermute | solution.py:52
  118.7 11.2 %attend.1 = (bf16[1024,512]{1,0:T(8,128)(2,1)S(1)}, f32[4,2,1024]{2,1,0:T(2,128)S(1)}) custom-call(s32[4]{0:T(128)S(1)} %fusion.64.refs_0_, bf16[1024,1536]{1,0:T(8,128)(2,1)S(1)} %add_convert_fusion.refs_1_, s32[1,1024]{1,0:T(1,128)S(1)} %bitcast.211), custom_call_target="tpu_custom_call" | custom-call | flops 3104999936 | bytes 10350000 | tf_op jit(solution)/shard_map/attend/pallas_call | solution.py:442
  145.1 15.1 %collective-permute-done.13.refs_3_ = bf16[2,4,64,1024]{3,2,1,0:T(8,128)(2,1)} collective-permute-done((bf16[2,4,64,1024]{3,2,1,0:T(8,128)(2,1)}, bf16[2,4,64,1024]{3,2,1,0:T(8,128)(2,1)}, u32[]{:S(2)}, u32[]{:S(2)}) %collective-permute-start.13) | collective-permute-done | bytes 1048608 | tf_op jit(solution)/shard_map/ppermute | solution.py:52
  169.9 11.0 %up_part.1 = (bf16[1024,2048]{1,0:T(8,128)(2,1)S(1)}, f32[1024,2048]{1,0:T(8,128)S(1)}) custom-call(bf16[1024,1024]{1,0:T(8,128)(2,1)S(1)} %pad_maximum_fusion.4.x_ref.refs_1_, bf16[1024,2048]{1,0:T(8,128)(2,1)S(1)} %bitcast.205, f32[1,2048]{1,0:T(1,128)S(1)} %bitcast_convert_fusion.b_ref), custom_call_target="tpu_custom_call" | custom-call | flops 1890000000 | bytes 6300000 | tf_op jit(solution)/shard_map/up_part/pallas_call | solution.py:518
  180.9 6.9 %weight_grad.3 = (bf16[4,2,128,512]{3,2,1,0:T(8,128)(2,1)S(1)}, bf16[4,2,128,512]{3,2,1,0:T(8,128)(2,1)S(1)}, bf16[4,2,128,512]{3,2,1,0:T(8,128)(2,1)S(1)}, bf16[4,2,128,512]{3,2,1,0:T(8,128)(2,1)S(1)}) custom-call(s32[3]{0:T(128)S(1)} %pad_add_fusion.place_ref.refs_0_, bf16[1024,2048]{1,0:T(8,128)(2,1)S(1)} %get-tuple-element.109.refs_1_, ...), custom_call_target="tpu_custom_call" | custom-call | flops 1890000000 | bytes 6300000 | tf_op jit(solution)/shard_map/weight_grad/pallas_call | solution.py:181
  193.5 7.9 %up_back.1 = (bf16[1024,2048]{1,0:T(8,128)(2,1)S(1)}, f32[1,2048]{1,0:T(1,128)S(1)}) custom-call(bf16[1024,1024]{1,0:T(8,128)(2,1)S(1)} %get-tuple-element.75.refs_2_.g_ref, bf16[2048,1024]{1,0:T(8,128)(2,1)S(1)} %bitcast.203, f32[1024,2048]{1,0:T(8,128)S(1)} %get-tuple-element.79.slope_ref), custom_call_target="tpu_custom_call" | custom-call | flops 1755000064 | bytes 5850000 | tf_op jit(solution)/shard_map/up_back/pallas_call | solution.py:549
  204.8 7.9 %weight_grad.4 = (bf16[4,2,64,1024]{3,2,1,0:T(8,128)(2,1)S(1)}, bf16[4,2,64,1024]{3,2,1,0:T(8,128)(2,1)}, bf16[4,2,64,1024]{3,2,1,0:T(8,128)(2,1)S(1)}, bf16[4,2,64,1024]{3,2,1,0:T(8,128)(2,1)}) custom-call(s32[3]{0:T(128)S(1)} %pad_add_fusion.place_ref.refs_0_, bf16[1024,1024]{1,0:T(8,128)(2,1)S(1)} %pad_maximum_fusion.4.x_ref.refs_1_, ...), custom_call_target="tpu_custom_call" | custom-call | flops 1890000000 | bytes 6300000 | tf_op jit(solution)/shard_map/weight_grad/pallas_call | solution.py:181
  219.9 8.7 %collective-permute-done.24.refs_1_ = bf16[4,128,512]{2,1,0:T(8,128)(2,1)S(1)} collective-permute-done((bf16[4,128,512]{2,1,0:T(8,128)(2,1)S(1)}, bf16[4,128,512]{2,1,0:T(8,128)(2,1)S(1)}, u32[]{:S(2)}, u32[]{:S(2)}) %collective-permute-start.24) | collective-permute-done | bytes 524320 | tf_op jit(solution)/shard_map/ppermute | solution.py:52
  235.9 6.8 %multiply_reduce_fusion = (f32[1024]{0:T(1024)S(1)}, f32[512]{0:T(512)S(1)}, f32[512]{0:T(512)S(1)}, f32[1024]{0:T(1024)S(1)}, f32[512,1024]{1,0:T(8,128)S(1)}) fusion(f32[512,1024]{1,0:T(8,128)} %copy-done.26, f32[512]{0:T(512)S(1)} %add_rsqrt_fusion.2, f32[512]{0:T(512)S(1)} %broadcast_multiply_fusion.6, f32[1024]{0:T(1024)S(1)} %reshape.276, ...), kind=kOutput, calls=%fused_computation.57 | convolution fusion | flops 2153247744 | bytes 11554816 | tf_op jit(solution)/shard_map/dot_general | solution.py:39
  256.5 17.8 %attend_back.1.refs_2_ = bf16[1024,1536]{1,0:T(8,128)(2,1)S(1)} custom-call(s32[4]{0:T(128)S(1)} %fusion.64.refs_0_, bf16[1024,1536]{1,0:T(8,128)(2,1)S(1)} %copy-done.24, bf16[1024,512]{1,0:T(8,128)(2,1)S(1)} %pad_maximum_fusion.12.refs_2_, f32[4,2,1024]{2,1,0:T(2,128)S(1)} %get-tuple-element.96.refs_3_, s32[1,1024]{1,0:T(1,128)S(1)} %bitcast.212), custom_call_target="tpu_custom_call" | custom-call | flops 4860000256 | bytes 16200000 | tf_op jit(solution)/shard_map/attend_back/pallas_call | solution.py:475
  277.1 5.8 %weight_grad.5 = (bf16[4,2,64,1024]{3,2,1,0:T(8,128)(2,1)S(1)}, bf16[4,2,64,1024]{3,2,1,0:T(8,128)(2,1)S(1)}, bf16[4,2,64,1024]{3,2,1,0:T(8,128)(2,1)S(1)}, bf16[4,2,64,1024]{3,2,1,0:T(8,128)(2,1)S(1)}) custom-call(s32[3]{0:T(128)S(1)} %pad_add_fusion.place_ref.refs_0_, bf16[1024,1024]{1,0:T(8,128)(2,1)S(1)} %copy-done.9, ...), custom_call_target="tpu_custom_call" | custom-call | flops 1890000000 | bytes 6300000 | tf_op jit(solution)/shard_map/weight_grad/pallas_call | solution.py:181
  293.2 4.7 %all-to-all-start.4 = ((bf16[4,64,2048]{2,1,0:T(8,128)(2,1)}), bf16[4,64,2048]{2,1,0:T(8,128)(2,1)}, u32[]{:S(2)}, u32[]{:S(2)}) async-start(bf16[4,64,2048]{2,1,0:T(8,128)(2,1)} %copy-done.5), calls=%async_computation.4 | async-start | bytes 2097152 | tf_op jit(solution)/shard_map/all_to_all | solution.py:276
  300.2 5.8 %fusion.19 = (f32[1024]{0:T(1024)S(1)}, f32[512]{0:T(512)S(1)}, f32[512]{0:T(512)S(1)}, f32[1024]{0:T(1024)S(1)}, f32[512,1024]{1,0:T(8,128)}) fusion(bf16[1,512,1024]{2,1,0:T(8,128)(2,1)S(1)} %copy-done.36, f32[512]{0:T(512)S(1)} %add_rsqrt_fusion.1, f32[512]{0:T(512)S(1)} %broadcast_multiply_fusion.3, f32[1024]{0:T(1024)S(1)} %reshape.272, ...), kind=kOutput, calls=%fused_computation.43 | convolution fusion | flops 1616901120 | bytes 8933376 | tf_op jit(solution)/shard_map/dot_general | solution.py:39
  313.5 4.8 %collective-permute-done.31.refs_3_ = bf16[4,2,64,1024]{3,2,1,0:T(8,128)(2,1)} collective-permute-done((bf16[4,2,64,1024]{3,2,1,0:T(8,128)(2,1)}, bf16[4,2,64,1024]{3,2,1,0:T(8,128)(2,1)}, u32[]{:S(2)}, u32[]{:S(2)}) %collective-permute-start.31) | collective-permute-done | bytes 1048608 | tf_op jit(solution)/shard_map/ppermute | solution.py:52
  323.3 6.5 %collective-permute-done.38 = f32[4,2,384]{2,1,0:T(2,128)S(1)} collective-permute-done((f32[4,2,384]{2,1,0:T(2,128)S(1)}, f32[4,2,384]{2,1,0:T(2,128)S(1)}, u32[]{:S(2)}, u32[]{:S(2)}) %collective-permute-start.38) | collective-permute-done | bytes 12320 | tf_op jit(solution)/shard_map/ppermute | solution.py:52
  330.4 6.4 %fusion.78 = f32[1024,1024]{1,0:T(8,128)S(1)} fusion(bf16[1024,2048]{1,0:T(8,128)(2,1)} %copy-done.22, bf16[2048,1024]{1,0:T(8,128)(2,1)S(1)} %bitcast.204), kind=kOutput, calls=%fused_computation.218 | convolution fusion | flops 4294967296 | bytes 12582912 | tf_op jit(solution)/shard_map/dot_general | solution.py:39
  356.6 9.6 %collective-permute-done.33 = bf16[256,1024]{1,0:T(8,128)(2,1)} collective-permute-done((bf16[256,1024]{1,0:T(8,128)(2,1)S(1)}, bf16[256,1024]{1,0:T(8,128)(2,1)}, u32[]{:S(2)}, u32[]{:S(2)}) %collective-permute-start.33) | collective-permute-done | bytes 524320 | tf_op jit(solution)/shard_map/ppermute | solution.py:52
  368.4 6.5 %all-to-all-done.3 = bf16[4,72,2048]{2,1,0:T(8,128)(2,1)S(1)} async-done(((bf16[4,72,2048]{2,1,0:T(8,128)(2,1)}), bf16[4,72,2048]{2,1,0:T(8,128)(2,1)S(1)}, u32[]{:S(2)}, u32[]{:S(2)}) %all-to-all-start.3) | async-done | bytes 1179680 | tf_op jit(solution)/shard_map/all_to_all | solution.py:276
  (374 shorter events, 182.0 us)
Async XLA Ops:
  7.6 26.3 %collective-permute-start = (bf16[2,256,1024]{2,1,0:T(8,128)(2,1)}, bf16[2,256,1024]{2,1,0:T(8,128)(2,1)S(1)}, u32[]{:S(2)}, u32[]{:S(2)}) collective-permute-start(bf16[2,256,1024]{2,1,0:T(8,128)(2,1)} %get-tuple-element.135), channel_id=1, source_target_pairs={{0,2},{2,0},{1,3},{3,1},{4,6},{6,4},{5,7},{7,5},{8,10},{10,8},{9,1... | collective-permute-start | bytes 3145736 | tf_op jit(solution)/shard_map/ppermute | solution.py:52
  12.0 33.2 %all-to-all-start = ((bf16[4,72,2048]{2,1,0:T(8,128)(2,1)}), bf16[4,72,2048]{2,1,0:T(8,128)(2,1)S(1)}, u32[]{:S(2)}, u32[]{:S(2)}) async-start(bf16[4,72,2048]{2,1,0:T(8,128)(2,1)} %broadcast_in_dim.34), calls=%async_computation | async-start | bytes 2359296 | tf_op jit(solution)/shard_map/all_to_all | solution.py:129
  35.6 32.0 %collective-permute-start.1 = (bf16[2,512,1024]{2,1,0:T(8,128)(2,1)}, bf16[2,512,1024]{2,1,0:T(8,128)(2,1)}, u32[]{:S(2)}, u32[]{:S(2)}) collective-permute-start(bf16[2,512,1024]{2,1,0:T(8,128)(2,1)} %pad_maximum_fusion.1), channel_id=1, source_target_pairs={{0,1},{1,0},{2,3},{3,2},{4,5},{5,4},{6,7},{7,6},{8,9},{9,8},{10,11... | collective-permute-start | bytes 6291464 | tf_op jit(solution)/shard_map/ppermute | solution.py:52
  52.5 29.0 %all-to-all-start.1 = ((bf16[4,64,2048]{2,1,0:T(8,128)(2,1)}), bf16[4,64,2048]{2,1,0:T(8,128)(2,1)}, u32[]{:S(2)}, u32[]{:S(2)}) async-start(bf16[4,64,2048]{2,1,0:T(8,128)(2,1)} %broadcast_in_dim.35), calls=%async_computation.1 | async-start | bytes 2097152 | tf_op jit(solution)/shard_map/all_to_all | solution.py:129
  63.3 26.7 %collective-permute-start.4 = (bf16[2,4,72,1024]{3,2,1,0:T(8,128)(2,1)S(1)}, bf16[2,4,72,1024]{3,2,1,0:T(8,128)(2,1)}, u32[]{:S(2)}, u32[]{:S(2)}) collective-permute-start(bf16[2,4,72,1024]{3,2,1,0:T(8,128)(2,1)S(1)} %pad_maximum_fusion.7.refs_0_), channel_id=1, source_target_pairs={{0,4},{4,0},{1,5},{5,1},{2,6},{6,2},{3,7},{7,3},{8,12},{12,8},{9,1... | collective-permute-start | bytes 3538952 | tf_op jit(solution)/shard_map/ppermute | solution.py:52
  67.1 26.1 %collective-permute-start.6 = (bf16[2,4,72,1024]{3,2,1,0:T(8,128)(2,1)}, bf16[2,4,72,1024]{3,2,1,0:T(8,128)(2,1)}, u32[]{:S(2)}, u32[]{:S(2)}) collective-permute-start(bf16[2,4,72,1024]{3,2,1,0:T(8,128)(2,1)} %pad_maximum_fusion.8.refs_2_), channel_id=1, source_target_pairs={{0,2},{2,0},{1,3},{3,1},{4,6},{6,4},{5,7},{7,5},{8,10},{10,8},{9,1... | collective-permute-start | bytes 3538952 | tf_op jit(solution)/shard_map/ppermute | solution.py:52
  85.4 56.4 %all-to-all-start.2 = ((bf16[4,4,128,512]{3,2,1,0:T(8,128)(2,1)}), bf16[4,4,128,512]{3,2,1,0:T(8,128)(2,1)}, u32[]{:S(2)}, u32[]{:S(2)}) async-start(bf16[4,4,128,512]{3,2,1,0:T(8,128)(2,1)} %broadcast_in_dim.37), calls=%async_computation.2 | async-start | bytes 4194304 | tf_op jit(solution)/shard_map/all_to_all | solution.py:129
  101.1 35.6 %collective-permute-start.10 = (bf16[1024,512]{1,0:T(8,128)(2,1)}, bf16[1024,512]{1,0:T(8,128)(2,1)}, u32[]{:S(2)}, u32[]{:S(2)}) collective-permute-start(bf16[1024,512]{1,0:T(8,128)(2,1)} %bitcast.208), channel_id=1, source_target_pairs={{0,1},{1,0},{2,3},{3,2},{4,5},{5,4},{6,7},{7,6},{8,9},{9,8},{10,11... | collective-permute-start | bytes 3145736 | tf_op jit(solution)/shard_map/ppermute | solution.py:52
  134.3 25.9 %collective-permute-start.13 = (bf16[2,4,64,1024]{3,2,1,0:T(8,128)(2,1)}, bf16[2,4,64,1024]{3,2,1,0:T(8,128)(2,1)}, u32[]{:S(2)}, u32[]{:S(2)}) collective-permute-start(bf16[2,4,64,1024]{3,2,1,0:T(8,128)(2,1)} %pad_maximum_fusion.10.refs_2_), channel_id=1, source_target_pairs={{0,2},{2,0},{1,3},{3,1},{4,6},{6,4},{5,7},{7,5},{8,10},{10,8},{9,1... | collective-permute-start | bytes 3145736 | tf_op jit(solution)/shard_map/ppermute | solution.py:52
  134.9 25.4 %collective-permute-start.12 = (bf16[2,4,64,1024]{3,2,1,0:T(8,128)(2,1)S(1)}, bf16[2,4,64,1024]{3,2,1,0:T(8,128)(2,1)}, u32[]{:S(2)}, u32[]{:S(2)}) collective-permute-start(bf16[2,4,64,1024]{3,2,1,0:T(8,128)(2,1)S(1)} %pad_maximum_fusion.9.refs_0_), channel_id=1, source_target_pairs={{0,4},{4,0},{1,5},{5,1},{2,6},{6,2},{3,7},{7,3},{8,12},{12,8},{9,1... | collective-permute-start | bytes 3145736 | tf_op jit(solution)/shard_map/ppermute | solution.py:52
  160.3 29.7 %collective-permute-start.16 = (bf16[2,4,128,512]{3,2,1,0:T(8,128)(2,1)}, bf16[2,4,128,512]{3,2,1,0:T(8,128)(2,1)}, u32[]{:S(2)}, u32[]{:S(2)}) collective-permute-start(bf16[2,4,128,512]{3,2,1,0:T(8,128)(2,1)} %get-tuple-element.77.refs_0_), channel_id=1, source_target_pairs={{0,4},{4,0},{1,5},{5,1},{2,6},{6,2},{3,7},{7,3},{8,12},{12,8},{9,1... | collective-permute-start | bytes 3145736 | tf_op jit(solution)/shard_map/ppermute | solution.py:52
  160.8 29.2 %collective-permute-start.17 = (bf16[2,4,128,512]{3,2,1,0:T(8,128)(2,1)}, bf16[2,4,128,512]{3,2,1,0:T(8,128)(2,1)}, u32[]{:S(2)}, u32[]{:S(2)}) collective-permute-start(bf16[2,4,128,512]{3,2,1,0:T(8,128)(2,1)} %get-tuple-element.78.refs_2_), channel_id=1, source_target_pairs={{0,2},{2,0},{1,3},{3,1},{4,6},{6,4},{5,7},{7,5},{8,10},{10,8},{9,1... | collective-permute-start | bytes 3145736 | tf_op jit(solution)/shard_map/ppermute | solution.py:52
  204.8 31.1 %collective-permute-start.18 = (bf16[512,1024]{1,0:T(8,128)(2,1)}, bf16[512,1024]{1,0:T(8,128)(2,1)}, u32[]{:S(2)}, u32[]{:S(2)}) collective-permute-start(bf16[512,1024]{1,0:T(8,128)(2,1)} %fusion.33), channel_id=1, source_target_pairs={{0,1},{1,0},{2,3},{3,2},{4,5},{5,4},{6,7},{7,6},{8,9},{9,8},{10,11... | collective-permute-start | bytes 3145736 | tf_op jit(solution)/shard_map/ppermute | solution.py:52
  218.2 32.7 %collective-permute-start.20 = (bf16[4,2,64,1024]{3,2,1,0:T(8,128)(2,1)}, bf16[4,2,64,1024]{3,2,1,0:T(8,128)(2,1)S(1)}, u32[]{:S(2)}, u32[]{:S(2)}) collective-permute-start(bf16[4,2,64,1024]{3,2,1,0:T(8,128)(2,1)} %get-tuple-element.84), channel_id=1, source_target_pairs={{0,2},{2,0},{1,3},{3,1},{4,6},{6,4},{5,7},{7,5},{8,10},{10,8},{9,1... | collective-permute-start | bytes 3145736 | tf_op jit(solution)/shard_map/ppermute | solution.py:52
  219.1 31.8 %collective-permute-start.21 = (bf16[4,2,64,1024]{3,2,1,0:T(8,128)(2,1)}, bf16[4,2,64,1024]{3,2,1,0:T(8,128)(2,1)}, u32[]{:S(2)}, u32[]{:S(2)}) collective-permute-start(bf16[4,2,64,1024]{3,2,1,0:T(8,128)(2,1)} %get-tuple-element.86), channel_id=1, source_target_pairs={{0,4},{4,0},{1,5},{5,1},{2,6},{6,2},{3,7},{7,3},{8,12},{12,8},{9,1... | collective-permute-start | bytes 3145736 | tf_op jit(solution)/shard_map/ppermute | solution.py:52
  231.6 61.6 %all-to-all-start.5 = ((bf16[4,128,1024]{2,1,0:T(8,128)(2,1)}), bf16[4,128,1024]{2,1,0:T(8,128)(2,1)}, u32[]{:S(2)}, u32[]{:S(2)}) async-start(bf16[4,128,1024]{2,1,0:T(8,128)(2,1)} %split_over_z.3), calls=%async_computation.5 | async-start | bytes 2097152 | tf_op jit(solution)/shard_map/all_to_all | solution.py:276
  247.2 27.2 %collective-permute-start.26 = (bf16[1024,512]{1,0:T(8,128)(2,1)S(1)}, bf16[1024,512]{1,0:T(8,128)(2,1)S(1)}, u32[]{:S(2)}, u32[]{:S(2)}) collective-permute-start(bf16[1024,512]{1,0:T(8,128)(2,1)S(1)} %convolution_convert_fusion), channel_id=1, source_target_pairs={{0,1},{1,0},{2,3},{3,2},{4,5},{5,4},{6,7},{7,6},{8,9},{9,8},{10,11... | collective-permute-start | bytes 3145736 | tf_op jit(solution)/shard_map/ppermute | solution.py:52
  253.5 30.4 %collective-permute-start.27 = (bf16[4,64,1024]{2,1,0:T(8,128)(2,1)S(1)}, bf16[4,64,1024]{2,1,0:T(8,128)(2,1)S(1)}, u32[]{:S(2)}, u32[]{:S(2)}) collective-permute-start(bf16[4,64,1024]{2,1,0:T(8,128)(2,1)S(1)} %get-tuple-element.100), channel_id=1, source_target_pairs={{0,4},{4,0},{1,5},{5,1},{2,6},{6,2},{3,7},{7,3},{8,12},{12,8},{9,1... | collective-permute-start | bytes 1572872 | tf_op jit(solution)/shard_map/ppermute | solution.py:52
  255.1 28.9 %collective-permute-start.28 = (bf16[4,64,1024]{2,1,0:T(8,128)(2,1)S(1)}, bf16[4,64,1024]{2,1,0:T(8,128)(2,1)S(1)}, u32[]{:S(2)}, u32[]{:S(2)}) collective-permute-start(bf16[4,64,1024]{2,1,0:T(8,128)(2,1)S(1)} %get-tuple-element.102), channel_id=1, source_target_pairs={{0,2},{2,0},{1,3},{3,1},{4,6},{6,4},{5,7},{7,5},{8,10},{10,8},{9,1... | collective-permute-start | bytes 1572872 | tf_op jit(solution)/shard_map/ppermute | solution.py:52
  292.1 26.3 %collective-permute-start.30 = (bf16[4,2,64,1024]{3,2,1,0:T(8,128)(2,1)}, bf16[4,2,64,1024]{3,2,1,0:T(8,128)(2,1)}, u32[]{:S(2)}, u32[]{:S(2)}) collective-permute-start(bf16[4,2,64,1024]{3,2,1,0:T(8,128)(2,1)} %copy-done.20), channel_id=1, source_target_pairs={{0,2},{2,0},{1,3},{3,1},{4,6},{6,4},{5,7},{7,5},{8,10},{10,8},{9,1... | collective-permute-start | bytes 3145736 | tf_op jit(solution)/shard_map/ppermute | solution.py:52
  292.7 25.6 %collective-permute-start.31 = (bf16[4,2,64,1024]{3,2,1,0:T(8,128)(2,1)}, bf16[4,2,64,1024]{3,2,1,0:T(8,128)(2,1)}, u32[]{:S(2)}, u32[]{:S(2)}) collective-permute-start(bf16[4,2,64,1024]{3,2,1,0:T(8,128)(2,1)} %copy-done.21), channel_id=1, source_target_pairs={{0,4},{4,0},{1,5},{5,1},{2,6},{6,2},{3,7},{7,3},{8,12},{12,8},{9,1... | collective-permute-start | bytes 3145736 | tf_op jit(solution)/shard_map/ppermute | solution.py:52
  293.2 49.1 %all-to-all-start.4 = ((bf16[4,64,2048]{2,1,0:T(8,128)(2,1)}), bf16[4,64,2048]{2,1,0:T(8,128)(2,1)}, u32[]{:S(2)}, u32[]{:S(2)}) async-start(bf16[4,64,2048]{2,1,0:T(8,128)(2,1)} %copy-done.5), calls=%async_computation.4 | async-start | bytes 2097152 | tf_op jit(solution)/shard_map/all_to_all | solution.py:276
  311.3 36.7 %collective-permute-start.34 = (bf16[256,1024]{1,0:T(8,128)(2,1)}, bf16[256,1024]{1,0:T(8,128)(2,1)}, u32[]{:S(2)}, u32[]{:S(2)}) collective-permute-start(bf16[256,1024]{1,0:T(8,128)(2,1)} %slice.300), channel_id=1, source_target_pairs={{0,2},{2,0},{1,3},{3,1},{4,6},{6,4},{5,7},{7,5},{8,10},{10,8},{9,1... | collective-permute-start | bytes 1572872 | tf_op jit(solution)/shard_map/ppermute | solution.py:52
  342.3 32.5 %all-to-all-start.3 = ((bf16[4,72,2048]{2,1,0:T(8,128)(2,1)}), bf16[4,72,2048]{2,1,0:T(8,128)(2,1)S(1)}, u32[]{:S(2)}, u32[]{:S(2)}) async-start(bf16[4,72,2048]{2,1,0:T(8,128)(2,1)} %split_over_z.5), calls=%async_computation.3 | async-start | bytes 2359296 | tf_op jit(solution)/shard_map/all_to_all | solution.py:276
  (82 other events, 698.5 us)

commit v4 on v3

--- a/solution.py
+++ b/solution.py
@@ -40,7 +40,7 @@
 
 
 def cost(microseconds):
-    return pl.CostEstimate(flops=int(microseconds * 2.70e8), bytes_accessed=int(microseconds * 0.90e6), transcendentals=0)
+    return pl.CostEstimate(flops=int(microseconds * 0.9e8), bytes_accessed=int(microseconds * 0.3e6), transcendentals=0)
 
 
 def after(value, *others):
@@ -74,6 +74,18 @@
         block = lax.dynamic_index_in_dim(value, lax.rem(here + k, size), at, keepdims=False)
         parts.append(shift(block, axis, k) if k else block)
     return by_place(parts, axis, -1)
+
+
+def reduce_axes(value, axes, at):
+    size = 1
+    for axis in axes:
+        size = size * lax.axis_size(axis)
+    here = lax.axis_index(axes)
+    total = lax.dynamic_index_in_dim(value, here, at, keepdims=False)
+    for k in range(1, size):
+        block = lax.dynamic_index_in_dim(value, lax.rem(here + k, size), at, keepdims=False)
+        total = total + lax.ppermute(block, axes, [(i, (i + k) % size) for i in range(size)])
+    return total
 
 
 def reduce_axis(value, axis, at):
@@ -142,51 +154,45 @@
     return gather_relative(first, "y"), gather_relative(second, "g")
 
 
-def weight_grad_kernel(sizes, place_ref, left_ref, right_ref, *refs):
+def weight_grad(place, sizes, left, right, more=()):
     nz, ny, ng = sizes
-    middle = (len(refs) - 1) - (ny + ng)
-    kept, outs, total = refs[:middle], refs[middle:-1], refs[-1]
-    y, g = place_ref[1], place_ref[2]
-    width = right_ref.shape[1]
-    total[:, :width] = dot(left_ref[...], right_ref[...], (0, 0))
-    if kept:
-        total[:, width:] = kept[0][...].astype(F32)
-    columns = total.shape[1] // 2
-    rows = total.shape[0] // (ny * ng)
-    for k in range(ng):
-        at = lax.rem(g + k, ng)
-        for i in range(ny):
-            start = pl.multiple_of((i * ng + at) * rows, rows)
-            outs[k][0, i] = half(total[pl.ds(start, rows), :columns])
-    for k in range(ny):
-        at = lax.rem(y + k, ny)
-        for i in range(ng):
-            start = pl.multiple_of((at * ng + i) * rows, rows)
-            outs[ng + k][0, i] = half(total[pl.ds(start, rows), columns:])
-
-
-def weight_grad(place, sizes, left, right, more=None):
-    nz, ny, ng = sizes
-    tokens, height = left.shape
-    width = right.shape[1] + (more.shape[1] if more is not None else 0)
+    n, m = len(left), len(more)
+    tokens, height = left[0].shape
+    right_width = right.shape[1]
+    width = right_width + (more[0].shape[1] if more else 0)
     rows, columns = height // (nz * ny * ng), width // 2
 
-    def kernel(*refs):
-        weight_grad_kernel(sizes, *refs)
+    def kernel(place_ref, *refs):
+        lefts, right_ref, mores, outs, total = refs[:n], refs[n], refs[n + 1 : n + 1 + m], refs[n + 1 + m : -1], refs[-1]
+        y, g = place_ref[1], place_ref[2]
+        value = dot(lefts[0][...], right_ref[:tokens], (0, 0))
+        for i in range(1, n):
+            value = value + dot(lefts[i][...], right_ref[i * tokens : (i + 1) * tokens], (0, 0))
+        total[:, :right_width] = value
+        if mores:
+            total[:, right_width:] = total_of(mores, slice(None))
+        for k in range(ng):
+            at = lax.rem(g + k, ng)
+            for i in range(ny):
+                start = pl.multiple_of((i * ng + at) * rows, rows)
+                outs[k][0, i] = half(total[pl.ds(start, rows), :columns])
+        for k in range(ny):
+            at = lax.rem(y + k, ny)
+            for i in range(ng):
+                start = pl.multiple_of((at * ng + i) * rows, rows)
+                outs[ng + k][0, i] = half(total[pl.ds(start, rows), columns:])
 
     first = jax.ShapeDtypeStruct((nz, ny, rows, columns), BF)
     second = jax.ShapeDtypeStruct((nz, ng, rows, columns), BF)
     step = height // nz
-    extra = [] if more is None else [more]
+    skip = (more[0].shape[0] - height) // step if more else 0
     outs = pl.pallas_call(
         kernel,
         grid=(nz,),
-        in_specs=[
-            whole(pltpu.SMEM),
-            pl.BlockSpec((tokens, step), lambda i: (0, i)),
-            pl.BlockSpec((tokens, right.shape[1]), lambda i: (0, 0)),
-        ]
-        + [pl.BlockSpec((step, m.shape[1]), lambda i: (i, 0)) for m in extra],
+        in_specs=[whole(pltpu.SMEM)]
+        + [pl.BlockSpec((tokens, step), lambda i: (0, i))] * n
+        + [pl.BlockSpec((n * tokens, right_width), lambda i: (0, 0))]
+        + [pl.BlockSpec((step, v.shape[1]), lambda i: (i + skip, 0)) for v in more],
         out_specs=[pl.BlockSpec((1, ny, rows, columns), lambda i: (i, 0, 0, 0))] * ng
         + [pl.BlockSpec((1, ng, rows, columns), lambda i: (i, 0, 0, 0))] * ny,
         out_shape=[first] * ng + [second] * ny,
@@ -194,7 +200,7 @@
         compiler_params=pltpu.CompilerParams(vmem_limit_bytes=20 << 20),
         cost_estimate=cost(7),
         name="weight_grad",
-    )(place, *[left, right, *extra])
+    )(place, *left, right, *more)
     return outs[:ng], outs[ng:]
 
 
@@ -260,6 +266,35 @@
     )(*first, *second, *extra)
 
 
+def split_both_over_z(first, second, third, fourth):
+    ny, ng = len(first), len(second)
+    nz, rows, columns = first[0].shape
+    high, low_columns = third[0].shape[1:]
+    groups = high // rows
+
+    def kernel(*refs):
+        parts = (refs[:ny], refs[ny : ny + ng], refs[ny + ng : 2 * ny + ng], refs[2 * ny + ng : -1])
+        out = refs[-1]
+        for i in range(2):
+            out[0, :rows, i * columns : (i + 1) * columns] = half(total_of(parts[i], 0))
+            total = half(total_of(parts[2 + i], 0))
+            for j in range(groups):
+                start = (2 * j + i) * low_columns
+                out[0, rows:, start : start + low_columns] = total[j * rows : (j + 1) * rows]
+
+    return pl.pallas_call(
+        kernel,
+        grid=(nz,),
+        in_specs=[pl.BlockSpec((1, rows, columns), lambda i: (i, 0, 0))] * (ny + ng)
+        + [pl.BlockSpec((1, high, low_columns), lambda i: (i, 0, 0))] * (ny + ng),
+        out_specs=pl.BlockSpec((1, 2 * rows, 2 * columns), lambda i: (i, 0, 0)),
+        out_shape=jax.ShapeDtypeStruct((nz, 2 * rows, 2 * columns), BF),
+        compiler_params=pltpu.CompilerParams(vmem_limit_bytes=12 << 20),
+        cost_estimate=cost(3),
+        name="split_both_over_z",
+    )(*first, *second, *third, *fourth)
+
+
 def send_parts(first, second, axis_first, axis_second):
     first = [first[0]] + [shift(b, axis_first, k) for k, b in enumerate(first) if k]
     second = [second[0]] + [shift(b, axis_second, k) for k, b in enumerate(second) if k]
@@ -272,12 +307,12 @@
     return send_parts(*add_split(place, sizes, first, second), "y", "g")
 
 
-def sum_over_z(blocks):
-    return jnp.sum(lax.all_to_all(blocks, "z", 0, 0, tiled=True).astype(F32), axis=0)
+def over_z(blocks):
+    return lax.all_to_all(blocks, "z", 0, 0, tiled=True)
 
 
 def total_sum(blocks):
-    total = blocks[0]
+    total = blocks[0].astype(F32)
     for block in blocks[1:]:
         total = total + block.astype(F32)
     return total
@@ -369,14 +404,16 @@
     local,
     order_ref,
     qkv_ref,
-    g_ref,
+    g_refs,
     log_ref,
     first_ref,
     out_ref,
+    sum_ref,
     q_s,
     k_s,
     v_s,
     g_s,
+    g_raw,
     query_grad,
     key_sum,
     value_sum,
@@ -388,7 +425,10 @@
     scale = head_dim ** (-0.5)
     for i, into in enumerate((q_s, k_s, v_s)):
         load_in_order(order_ref, qkv_ref, into, local, slice(i * lanes, (i + 1) * lanes))
-    load_in_order(order_ref, g_ref, g_s, local, slice(None))
+    own = g_refs[0].shape[0]
+    for i, ref in enumerate(g_refs):
+        g_raw[i * own : (i + 1) * own] = ref[...]
+    load_in_order(order_ref, g_raw, g_s, local, slice(None))
     k_t = k_s[...].T
     for start in range(0, length, block):
         q_heads = for_heads(q_s[start : start + block] * scale, head_dim)
@@ -426,7 +466,9 @@
                 value_sum[low : low + block] += dv[rows]
         query_grad[start : start + block] = (heads_of(dq, head_dim, block) * scale).T
     for i, source in enumerate((query_grad, key_sum, value_sum)):
-        store_in_order(order_ref, source, out_ref, local, slice(i * lanes, (i + 1) * lanes))
+        columns = slice(i * lanes, (i + 1) * lanes)
+        store_in_order(order_ref, source, out_ref, local, columns)
+        sum_ref[:, columns] = jnp.sum(half(source[...]).astype(F32), axis=0, keepdims=True)
 
 
 def attend(qkv, first, order, local, head_dim):
@@ -469,8 +511,11 @@
     lanes = 2 * head_dim
     steps = width // (3 * lanes)
 
-    def kernel(*refs):
-        attend_back_kernel(block, 64, head_dim, local, *refs)
+    n = len(grad_out)
+    own = length // n
+
+    def kernel(order_ref, qkv_ref, *refs):
+        attend_back_kernel(block, 64, head_dim, local, order_ref, qkv_ref, refs[:n], *refs[n:])
 
     return pl.pallas_call(
         kernel,
@@ -478,19 +523,180 @@
         in_specs=[
             whole(pltpu.SMEM),
             pl.BlockSpec((length, 3 * lanes), lambda i: (0, i)),
-            pl.BlockSpec((length, lanes), lambda i: (0, i)),
+        ]
+        + [pl.BlockSpec((own, lanes), lambda i: (0, i))] * n
+        + [
             pl.BlockSpec((1, 2, length), lambda i: (i, 0, 0)),
             pl.BlockSpec((1, length), lambda i: (0, 0)),
         ],
-        out_specs=pl.BlockSpec((length, 3 * lanes), lambda i: (0, i)),
-        out_shape=jax.ShapeDtypeStruct((length, width), BF),
-        scratch_shapes=[pltpu.VMEM((length, lanes), BF)] * 4
+        out_specs=[
+            pl.BlockSpec((length, 3 * lanes), lambda i: (0, i)),
+            pl.BlockSpec((1, 3 * lanes), lambda i: (0, i)),
+        ],
+        out_shape=[jax.ShapeDtypeStruct((length, width), BF), jax.ShapeDtypeStruct((1, width), F32)],
+        scratch_shapes=[pltpu.VMEM((length, lanes), BF)] * 5
         + [pltpu.VMEM((length, lanes), F32)] * 3
         + [pltpu.VMEM((window, 2 * block), F32)] * 2,
         compiler_params=pltpu.CompilerParams(vmem_limit_bytes=20 << 20),
         cost_estimate=cost(18 * steps / 4),
         name="attend_back",
-    )(order, qkv, grad_out, logs, first[None])
+    )(order, qkv, *grad_out, logs, first[None])
+
+
+def product(left, right, contract, kind, bias=None, rows=None, part=0):
+    rows = left.shape[0] if rows is None else rows
+    depth = left.shape[1]
+    width = right.shape[1 - contract[1]]
+    block = min(256, width)
+    extra = [] if bias is None else [bias[None]]
+
+    def kernel(left_ref, right_ref, *refs):
+        out = dot(left_ref[...], right_ref[...], contract)
+        if extra:
+            out = out + refs[0][...]
+        refs[-1][...] = out.astype(kind)
+
+    if contract[1] == 0:
+        right_spec = pl.BlockSpec((depth, block), lambda i: (0, i))
+    else:
+        right_spec = pl.BlockSpec((block, depth), lambda i: (i, 0))
+    return pl.pallas_call(
+        kernel,
+        grid=(width // block,),
+        in_specs=[pl.BlockSpec((rows, depth), lambda i: (part, 0)), right_spec]
+        + [pl.BlockSpec((1, block), lambda i: (0, i)) for _ in extra],
+        out_specs=pl.BlockSpec((rows, block), lambda i: (0, i)),
+        out_shape=jax.ShapeDtypeStruct((rows, width), kind),
+        compiler_params=pltpu.CompilerParams(vmem_limit_bytes=16 << 20),
+        cost_estimate=cost(2.3 * rows * width * depth / 2**30),
+        name="product",
+    )(left, right, *extra)
+
+
+def norm_back_part(summands, values, gain, added, scale=None):
+    tokens, width = values.shape
+    block = min(128, tokens)
+    n = len(summands)
+
+    def kernel(*refs):
+        ins, outs = refs[: n + 3], refs[n + 3 :]
+
+        @pl.when(pl.program_id(0) == 0)
+        def _():
+            for ref in outs[1 if scale is None else 2 :]:
+                ref[...] = jnp.zeros_like(ref)
+
+        grad = ins[0][...].astype(F32)
+        for ref in ins[1:n]:
+            grad = grad + ref[...].astype(F32)
+        normal, inverse = norm_parts(ins[n][...].astype(F32))
+        out = ins[n + 2][...].astype(F32) + norm_back(grad, normal, inverse, ins[n + 1][...])
+        sums = [grad * normal, grad]
+        if scale is None:
+            outs[0][...] = half(out)
+            rest = outs[1:]
+        else:
+            outs[0][...] = out
+            scaled = half(scale * out)
+            outs[1][...] = scaled
+            sums.append(scaled.astype(F32))
+            rest = outs[2:]
+        for ref, value in zip(rest, sums):
+            ref[...] += jnp.sum(value, axis=0, keepdims=True)
+
+    row = pl.BlockSpec((block, width), lambda i: (i, 0))
+    one = pl.BlockSpec((1, width), lambda i: (0, 0))
+    total = jax.ShapeDtypeStruct((1, width), F32)
+    if scale is None:
+        out_specs, out_shape = [row, one, one], [jax.ShapeDtypeStruct((tokens, width), BF), total, total]
+    else:
+        out_specs = [row, row, one, one, one]
+        out_shape = [
+            jax.ShapeDtypeStruct((tokens, width), F32),
+            jax.ShapeDtypeStruct((tokens, width), BF),
+            total,
+            total,
+            total,
+        ]
+    return pl.pallas_call(
+        kernel,
+        grid=(tokens // block,),
+        in_specs=[row] * n + [row, one, row],
+        out_specs=out_specs,
+        out_shape=out_shape,
+        compiler_params=pltpu.CompilerParams(vmem_limit_bytes=16 << 20),
+        cost_estimate=cost(3),
+        name="norm_back_part",
+    )(*summands, values, gain[None], added)
+
+
+def proj_norm(here, parts, weights, bias, gain, shift_by, x, depth):
+    nt = len(parts)
+    tokens, width = x.shape
+    part = width // nt
+    block = min(128, tokens)
+
+    def kernel(here_ref, *refs):
+        parts_in, weights_in = refs[:nt], refs[nt : 2 * nt]
+        bias_ref, gain_ref, shift_ref, x_ref, hidden_ref, normed_ref = refs[2 * nt :]
+        t = here_ref[0]
+        for j in range(nt):
+            total = 0.0
+            for k in range(nt):
+                rows = pl.ds(pl.multiple_of(lax.rem(t + k, nt) * part, part), part)
+                total = total + dot(parts_in[k][...], weights_in[j][rows, :], (1, 0))
+            columns = pl.ds(pl.multiple_of(lax.rem(t - j + nt, nt) * part, part), part)
+            hidden_ref[:, columns] = x_ref[:, columns].astype(F32) + depth * (total + bias_ref[:, columns])
+        normal, _ = norm_parts(hidden_ref[...])
+        normed_ref[...] = half(normal * gain_ref[...] + shift_ref[...])
+
+    row = pl.BlockSpec((block, width), lambda i: (i, 0))
+    one = pl.BlockSpec((1, width), lambda i: (0, 0))
+    return pl.pallas_call(
+        kernel,
+        grid=(tokens // block,),
+        in_specs=[whole(pltpu.SMEM)]
+        + [pl.BlockSpec((block, part), lambda i: (i, 0))] * nt
+        + [pl.BlockSpec((width, part), lambda i: (0, 0))] * nt
+        + [one, one, one, row],
+        out_specs=[row, row],
+        out_shape=[jax.ShapeDtypeStruct((tokens, width), F32), jax.ShapeDtypeStruct((tokens, width), BF)],
+        compiler_params=pltpu.CompilerParams(vmem_limit_bytes=16 << 20),
+        cost_estimate=cost(3),
+        name="proj_norm",
+    )(here, *parts, *weights, bias[None], gain[None], shift_by[None], x)
+
+
+def proj_back(here, grad, parts, weights):
+    nt = len(parts)
+    tokens, width = grad.shape
+    part = width // nt
+
+    def kernel(here_ref, grad_ref, *refs):
+        parts_in, weights_in, outs = refs[:nt], refs[nt : 2 * nt], refs[2 * nt :]
+        t = here_ref[0]
+
+        def place(step, offset=0):
+            return pl.ds(pl.multiple_of(lax.rem(t + step + nt, nt) * part + offset, 128), part)
+
+        for k in range(nt):
+            total = 0.0
+            for j in range(nt):
+                total = total + dot(grad_ref[:, place(-j)], weights_in[j][place(k), :], (1, 1))
+            outs[k][:tokens] = half(total)
+        for k in range(nt):
+            for m in range(nt):
+                outs[k][place(m, tokens), :] = half(dot(parts_in[m][...], grad_ref[:, place(k)], (0, 0)))
+
+    return pl.pallas_call(
+        kernel,
+        in_specs=[whole(pltpu.SMEM)] + [whole()] * (1 + 2 * nt),
+        out_specs=[whole()] * nt,
+        out_shape=[jax.ShapeDtypeStruct((tokens + width, part), BF)] * nt,
+        compiler_params=pltpu.CompilerParams(vmem_limit_bytes=24 << 20),
+        cost_estimate=cost(4),
+        name="proj_back",
+    )(here, grad, *parts, *weights)
 
 
 def gelu_parts(u):
@@ -502,40 +708,44 @@
 
 
 def up_part(normed, weight, bias):
-    tokens, width = normed.shape
+    n = len(normed)
+    tokens, width = normed[0].shape
     ff = weight.shape[1]
     block = min(256, ff)
-    rows = min(256, tokens)
-
-    def kernel(x_ref, w_ref, b_ref, active_ref, slope_ref):
-        for r in range(0, tokens, rows):
-            u = dot(x_ref[r : r + rows], w_ref[...], (1, 0)) + b_ref[...]
-            value, slope = gelu_parts(u)
-            active_ref[r : r + rows] = half(value)
-            slope_ref[r : r + rows] = slope
-
-    column = pl.BlockSpec((tokens, block), lambda i: (0, i))
+    rows = min(512, tokens)
+
+    def kernel(*refs):
+        w_ref, b_ref, active_ref, slope_ref = refs[n:]
+        for i in range(n):
+            for r in range(0, tokens, rows):
+                u = dot(refs[i][r : r + rows], w_ref[...], (1, 0)) + b_ref[...]
+                value, slope = gelu_parts(u)
+                at = slice(i * tokens + r, i * tokens + r + rows)
+                active_ref[at] = half(value)
+                slope_ref[at] = slope
+
+    column = pl.BlockSpec((n * tokens, block), lambda i: (0, i))
     return pl.pallas_call(
         kernel,
         grid=(ff // block,),
-        in_specs=[
-            pl.BlockSpec((tokens, width), lambda i: (0, 0)),
+        in_specs=[pl.BlockSpec((tokens, width), lambda i: (0, 0))] * n
+        + [
             pl.BlockSpec((width, block), lambda i: (0, i)),
             pl.BlockSpec((1, block), lambda i: (0, i)),
         ],
         out_specs=[column, column],
-        out_shape=[jax.ShapeDtypeStruct((tokens, ff), BF), jax.ShapeDtypeStruct((tokens, ff), F32)],
+        out_shape=[jax.ShapeDtypeStruct((n * tokens, ff), BF), jax.ShapeDtypeStruct((n * tokens, ff), F32)],
         compiler_params=pltpu.CompilerParams(vmem_limit_bytes=16 << 20),
         cost_estimate=cost(7),
         name="up_part",
-    )(*[normed, weight], bias[None])
+    )(*normed, weight, bias[None])
 
 
 def up_back(grad_down, weight, slope):
     tokens, width = grad_down.shape
     ff = weight.shape[0]
     block = min(256, ff)
-    rows = min(256, tokens)
+    rows = min(512, tokens)
 
     def kernel(g_ref, w_ref, slope_ref, out_ref, sum_ref):
         total = jnp.zeros((8, block), F32)
@@ -609,7 +819,7 @@
         block = lax.dynamic_index_in_dim(both, lax.rem(g + k, ng), 0, keepdims=False)
         parts.append(shift(block, "g", k) if k else block)
     both_own = jnp.concatenate(parts, axis=1)
-    x_own, grad_own = both_own[0].astype(F32), both_own[1].astype(F32)
+    x_own, grad_own = both_own[0], both_own[1]
     both_all = jnp.concatenate(gather_relative(both_own, "t"), axis=1)
 
     vectors = [gain_attn, shift_attn, bias_qv, bias_proj, gain_mlp, shift_mlp, bias_up, bias_down]
@@ -671,16 +881,26 @@
     normal_all, _ = norm_parts(both_all[0].astype(F32))
     normed_attn = half(normal_all * h_gain_attn + h_shift_attn)
     grad_down = half(depth * both_all[1].astype(F32))
-    qkv = half(dot(after(normed_attn, first_u, second_u), wqkv, (1, 0)) + bias_qkv)
+    d_bias_down = jnp.sum(grad_down[:own], axis=0, dtype=F32)
+    normed_attn = after(normed_attn, d_bias_down)
+    qkv = product(normed_attn, wqkv, (1, 0), BF, bias_qkv)
+    qkv = after(qkv, first_u, second_u)
     attended_heads, logs = attend(qkv, first_token, order, local, head_dim)
     first_u, second_u = gather_twice(first_u, second_u)
-    wo = jnp.concatenate(by_place(gather_relative(wo, "t"), "t", -1), axis=1)
-    attended = return_relative([attended_heads[k * own : (k + 1) * own] for k in range(nt)], "t")
-    attended = jnp.concatenate(by_place(attended, "t", 1), axis=1)
-    hidden = x_own + depth * (dot(attended, wo, (1, 0)) + h_bias_proj)
-    normal_two, inverse_two = norm_parts(hidden)
-    normed_own = half(normal_two * h_gain_mlp + h_shift_mlp)
-    normed_mlp = jnp.concatenate(gather_relative(normed_own, "t"), axis=0)
+    wo_parts = gather_relative(wo, "t")
+    attended_parts = return_relative([attended_heads[k * own : (k + 1) * own] for k in range(nt)], "t")
+    here = t.astype(jnp.int32)[None]
+    hidden, normed_own = proj_norm(
+        here,
+        attended_parts,
+        wo_parts,
+        h_bias_proj,
+        h_gain_mlp,
+        h_shift_mlp,
+        after(x_own, *first_u, *second_u),
+        depth,
+    )
+    normed_mlp = gather_relative(normed_own, "t")
     (wu,) = assemble(
         place,
         first_u,
@@ -693,12 +913,12 @@
     first_d, second_d = gather_twice(after(first_d, *first_u, *second_u), after(second_d, *first_u, *second_u))
     active, slope = up_part(normed_mlp, wu, h_bias_up)
 
-    def own_sum(left, right):
-        blocks = [half(dot(left[k * own : (k + 1) * own], right, (1, 1))) for k in range(1, nt)]
-        mine = dot(after(left[:own], *blocks), right, (1, 1))
-        return total_sum([mine] + [shift(block, "t", -k - 1) for k, block in enumerate(blocks)])
-
-    down_blocks = weight_grad(place, sizes, active, grad_down)
+    def own_sum(left, right, contract):
+        blocks = [product(left, right, contract, BF, rows=own, part=k) for k in range(1, nt)]
+        mine = product(after(left, *blocks), right, contract, F32, rows=own)
+        return [mine] + [shift(block, "t", -k - 1) for k, block in enumerate(blocks)]
+
+    down_blocks = weight_grad(place, sizes, [active], grad_down)
     down_parts = send_parts(*down_blocks, "g", "y")
     (wd,) = assemble(
         place,
@@ -712,59 +932,44 @@
     up_blocks = weight_grad(place, sizes, normed_mlp, grad_up)
     down_parts = reduce_in_layer(place, sizes, down_parts, *up_blocks[0])
     up_parts = send_parts(*up_blocks, "g", "y")
-    e2 = own_sum(grad_up, wu)
-
-    d_gain_mlp = jnp.sum(e2 * normal_two, axis=0)
-    d_shift_mlp = jnp.sum(e2, axis=0)
-    grad_hidden = grad_own + norm_back(e2, normal_two, inverse_two, h_gain_mlp)
-    grad_branch = half(depth * grad_hidden)
-    d_bias_proj = jnp.sum(grad_branch, axis=0, dtype=F32)
-
-    attended_back, d_proj = [], []
-    for k in range(nt):
-        at = lax.rem(t + k, nt) * part
-        attended_back.append(half(dot(grad_branch, lax.dynamic_slice_in_dim(wo, at, part, 0), (1, 1))))
-        d_proj.append(half(dot(attended, lax.dynamic_slice_in_dim(grad_branch, at, part, 1), (0, 0))))
-    grad_attended = jnp.concatenate(
-        [attended_back[0]] + [shift(b, "t", k) for k, b in enumerate(attended_back) if k], axis=0
+    e2 = own_sum(after(grad_up, up_blocks[0][0]), wu, (1, 1))
+
+    grad_hidden, grad_branch, d_gain_mlp, d_shift_mlp, d_bias_proj = norm_back_part(
+        e2, after(hidden, down_parts[0][0]), h_gain_mlp, grad_own, depth
     )
-    d_proj = total_sum([d_proj[0].astype(F32)] + [shift(b, "t", k) for k, b in enumerate(d_proj) if k])
+
 
     def to_rows(blocks):
         return jnp.stack(by_place(return_relative([blocks[k] for k in range(ng)], "g"), "g", 1), axis=0)
 
-    up_parts = reduce_in_layer(place, sizes, up_parts, grad_attended)
-    down_blocks = split_over_z(*down_parts, None)
-    sum_down = sum_over_z(down_blocks)
-    grad_attended = after(grad_attended, up_parts[0][0], down_blocks)
-    d_qkv = attend_back(qkv, grad_attended, logs, first_token, order, local, head_dim)
-    a_blocks = weight_grad(place, sizes, normed_attn, d_qkv, half(d_proj))
+    lowered = own_sum(after(active, grad_branch), wd, (1, 0))
+    up_parts = reduce_in_layer(place, sizes, up_parts, lowered[0])
+    back_parts = proj_back(here, after(grad_branch, up_parts[0][0]), attended_parts, wo_parts)
+    back_parts = [back_parts[0]] + [shift(b, "t", k) for k, b in enumerate(back_parts) if k]
+    block_out = half(hidden + depth * (total_sum(lowered) + h_bias_down)).reshape(ng, local, width)
+    grad_attended = [after(b, block_out) for b in back_parts]
+
+    def to_rows(blocks):
+        return jnp.stack(by_place(return_relative([blocks[k] for k in range(ng)], "g"), "g", 1), axis=0)
+
+    d_qkv, d_bias_qkv = attend_back(qkv, grad_attended, logs, first_token, order, local, head_dim)
+    a_blocks = weight_grad(place, sizes, [normed_attn], d_qkv, back_parts)
     a_parts = send_parts(*a_blocks, "g", "y")
-    up_blocks = split_over_z([after(up_parts[0][0], *a_blocks[0])] + up_parts[0][1:], up_parts[1], None)
-    sum_up = sum_over_z(up_blocks)
-    e1 = own_sum(after(d_qkv, up_blocks), wqkv)
-    normal_one, inverse_one = norm_parts(x_own)
-    d_gain_attn = jnp.sum(e1 * normal_one, axis=0)
-    d_shift_attn = jnp.sum(e1, axis=0)
-    grad_input = grad_hidden + norm_back(e1, normal_one, inverse_one, h_gain_attn)
-    a_parts = reduce_in_layer(place, sizes, a_parts, e1)
-    lowered = dot(after(active, a_parts[0][0]), wd, (1, 0))
-    lowered = total_sum(
-        [lowered[:own]] + [shift(half(lowered[k * own : (k + 1) * own]), "t", -k) for k in range(1, nt)]
-    )
-    block_out = to_rows(half(hidden + depth * (lowered + h_bias_down)).reshape(ng, local, width))
-    grad_input = to_rows(half(grad_input).reshape(ng, local, width)).astype(F32)
-
+    d_qkv = after(d_qkv, *a_blocks[0])
+    both_split = split_both_over_z([after(up_parts[0][0], d_qkv)] + up_parts[0][1:], up_parts[1], *down_parts)
+    both_sent = over_z(both_split)
+    d_qkv = after(d_qkv, both_split)
+    e1 = own_sum(d_qkv, wqkv, (1, 1))
+    grad_input, d_gain_attn, d_shift_attn = norm_back_part(e1, x_own, h_gain_attn, grad_hidden)
     def by_owner(full):
         return full.reshape(chips, nt, -1)
 
-    d_bias_qkv = jnp.sum(d_qkv, axis=0, dtype=F32).reshape(pairs, 3, lanes)
+    d_bias_qkv = d_bias_qkv.reshape(pairs, 3, lanes)
     d_bias_qv = jnp.zeros((2 * width,), F32)
     d_bias_qv = lax.dynamic_update_slice_in_dim(d_bias_qv, d_bias_qkv[:, 0].reshape(-1), t * part, 0)
     d_bias_qv = lax.dynamic_update_slice_in_dim(d_bias_qv, d_bias_qkv[:, 2].reshape(-1), width + t * part, 0)
     d_bias_up = d_bias_up.reshape(chips, 1, ff_shard)
     d_bias_up = jnp.where(lax.broadcasted_iota(jnp.int32, (chips, nt, 1), 1) == t, d_bias_up, 0.0)
-    d_bias_down = jnp.sum(grad_down[:own], axis=0, dtype=F32)
     sums = jnp.concatenate(
         [
             by_owner(d_gain_attn),
@@ -778,19 +983,29 @@
         ],
         axis=2,
     )
-    sums = reduce_axis(sums, "t", 1).reshape(nz, ny, ng, count)
-    sums = reduce_axis(reduce_axis(sums, "g", 2), "y", 1)
+    sums = sums.reshape(nz, ny * ng, nt * count)
+    a_parts = reduce_in_layer(place, sizes, a_parts, sums)
+    sums = reduce_axes(sums, ("y", "g"), 1)
     high = half(sums)
     more = jnp.stack([high.astype(F32), sums - high.astype(F32)], axis=1)
-    more = jnp.pad(more, ((0, 0), (0, 6), (0, 4 * part - count)))
-    sum_a = sum_over_z(split_over_z(*a_parts, more))
-    sums = sum_a[block_rows, :count] + sum_a[block_rows + 1, :count]
-    sum_a = sum_a[:block_rows]
+    more = jnp.pad(more, ((0, 0), (0, 6), (0, 4 * part - nt * count)))
+    a_blocks = split_over_z(*a_parts, after(more, both_sent))
+    block_out = to_rows(after(block_out, a_blocks))
+    grad_input = to_rows(after(grad_input, a_blocks).reshape(ng, local, width)).astype(F32)
+    both = jnp.sum(after(both_sent, a_blocks).astype(F32), axis=0)
+    sum_up = both[:block_rows]
+    sum_down = jnp.concatenate(jnp.split(both[block_rows:], ff_part // width, axis=1), axis=0)
+    sum_a = jnp.sum(over_z(a_blocks).astype(F32), axis=0)
+    sums = (sum_a[block_rows, : nt * count] + sum_a[block_rows + 1, : nt * count]).reshape(nt, 1, count)
+    sums = jnp.pad(sums, ((0, 0), (0, 7), (0, 4 * part - count)))
+    rest = jnp.concatenate([sum_a[:block_rows].reshape(nt, shard, 4 * part), sums], axis=1)
+    rest = swap_axis(rest, "t", 0)
+    sums = total_sum([r[shard, :count] for r in rest])
+    rest = [r[:shard] for r in rest]
     out_vectors = [sums[offsets[i] : offsets[i + 1]] for i in range(len(counts))]
 
     up = swap_axis(sum_up.reshape(nt, shard, ff_part), "t", 0)
     sum_up = jnp.stack([u.reshape(shard, chips, ff_shard) for u in up], axis=2).reshape(shard, hidden_width)
-    rest = swap_axis(sum_a.reshape(nt, shard, 4 * part), "t", 0)
     sum_qkv = jnp.stack([r[:, : 3 * part].reshape(shard, pairs, 3, lanes) for r in rest], axis=1)
     sum_qkv = sum_qkv.transpose(0, 3, 1, 2, 4).reshape(shard, 3 * width)
     sum_proj = jnp.concatenate([r[:, 3 * part :] for r in rest], axis=1)

time: 386 us -> 386 us (level)
  Pallas kernels: 89 us -> 131 us
  matrix products: 33.2 us -> 0 us
  waiting for transfers between devices: 103 us -> 82.1 us
  local copies, waits for them, and re-layouts: 39.4 us -> 52.8 us
  other arithmetic: 53.7 us -> 49.4 us
    pallas_call x3 -> x15, Pallas kernels: 20.6 us -> 64 us  [the longest x7 24.8 us: product(): pl.pallas_call(kernel, grid=(width // block,), in_specs=[pl.BlockSpec((ro...]
    dot_general x11 -> x0, matrix products: 33.2 us -> none  [dot(): lax.dot_general(left, right, ((contract[:1], contract[1:]), ((), ())), pr...]
    ppermute x42 -> x38, waiting for transfers between devices: 82.6 us -> 52.1 us  [shift(): lax.ppermute(value, axis, [(i, (i + step) % size) for i in range(size)])]
    unnamed x118 -> x149, local copies, waits for them, and re-layouts: 14.7 us -> 28.2 us
    all_to_all x3 -> x2, waiting for transfers between devices: 6.48 us -> 15.9 us  [over_z(): return lax.all_to_all(blocks, 'z', 0, 0, tiled=True)]
    reduce_sum x6 -> x2, other arithmetic: 9.28 us -> 2.26 us  [the longest x1 2.07 us: body(): both = jnp.sum(after(both_sent, a_blocks).astype(F32), axis=0)]
    all_to_all x3 -> x2, starting transfers between devices: 12.9 us -> 9.73 us  [over_z(): return lax.all_to_all(blocks, 'z', 0, 0, tiled=True)]
    ppermute x42 -> x38, starting transfers between devices: 32.3 us -> 34.8 us  [shift(): lax.ppermute(value, axis, [(i, (i + step) % size) for i in range(size)])]
  transfers between devices with their start and end apart: 48 -> 46, of which waited for: 18 -> 18; matrix products, arithmetic and copies ran while one was open for 28% -> 17% of each run, Pallas kernels for 23% -> 32%
where the time goes in v4:
time: 386 us; the launch traced here: 380 us
  Pallas kernels  131 us (34%)
  waiting for transfers between devices  82.1 us (21%)
  starting transfers between devices  61.9 us (16%)
  local copies, waits for them, and re-layouts  52.8 us (14%)
  other arithmetic  49.4 us (13%)
    ppermute x38, waiting for transfers between devices, shift(): lax.ppermute(value, axis, [(i, (i + step) % size) for i in range(size)])  52.1 us
    ppermute x38, starting transfers between devices, shift(): lax.ppermute(value, axis, [(i, (i + step) % size) for i in range(size)])  34.8 us
    unnamed x149, local copies, waits for them, and re-layouts  28.2 us
    pallas_call x7, Pallas kernels, product(): pl.pallas_call(kernel, grid=(width // block,), in_specs=[pl.BlockSpec((ro...  24.8 us
    pallas_call x3, Pallas kernels, weight_grad(): pl.pallas_call(kernel, grid=(nz,), in_specs=[whole(pltpu.SMEM)] + [pl.Blo...  22 us
    pallas_call x1, Pallas kernels, attend_back(): pl.pallas_call(kernel, grid=(steps,), in_specs=[whole(pltpu.SMEM), pl.Blo...  18.6 us
    all_to_all x2, waiting for transfers between devices, over_z(): return lax.all_to_all(blocks, 'z', 0, 0, tiled=True)  15.9 us
    all_to_all x3, waiting for transfers between devices, gather_over_z(): return lax.all_to_all(copies, 'z', 0, 0, tiled=True)  14.1 us
  transfers between devices with their start and end apart: 46, of which 18 were waited for; matrix products, arithmetic and copies ran while one was open for 17% of the time, Pallas kernels for 32%

profile of v4, /device:TPU:0, one launch (start us, length us, event | category | flops | bytes accessed | tf_op | source)
XLA Modules:
  0.0 379.6 jit_solution(1055666689465951453)
XLA Ops:
  12.0 4.9 %all-to-all-start = ((bf16[4,72,2048]{2,1,0:T(8,128)(2,1)}), bf16[4,72,2048]{2,1,0:T(8,128)(2,1)S(1)}, u32[]{:S(2)}, u32[]{:S(2)}) async-start(bf16[4,72,2048]{2,1,0:T(8,128)(2,1)} %broadcast_in_dim.37), calls=%async_computation | async-start | bytes 2359296 | tf_op jit(solution)/shard_map/all_to_all | solution.py:141
  16.8 17.1 %collective-permute-done = bf16[2,256,1024]{2,1,0:T(8,128)(2,1)S(1)} collective-permute-done((bf16[2,256,1024]{2,1,0:T(8,128)(2,1)}, bf16[2,256,1024]{2,1,0:T(8,128)(2,1)S(1)}, u32[]{:S(2)}, u32[]{:S(2)}) %collective-permute-start) | collective-permute-done | bytes 1048608 | tf_op jit(solution)/shard_map/ppermute | solution.py:52
  39.0 6.1 %all-to-all-done = bf16[4,72,2048]{2,1,0:T(8,128)(2,1)S(1)} async-done(((bf16[4,72,2048]{2,1,0:T(8,128)(2,1)}), bf16[4,72,2048]{2,1,0:T(8,128)(2,1)S(1)}, u32[]{:S(2)}, u32[]{:S(2)}) %all-to-all-start) | async-done | bytes 1179680 | tf_op jit(solution)/shard_map/all_to_all | solution.py:141
  49.7 4.3 %all-to-all-start.1 = ((bf16[4,64,2048]{2,1,0:T(8,128)(2,1)}), bf16[4,64,2048]{2,1,0:T(8,128)(2,1)}, u32[]{:S(2)}, u32[]{:S(2)}) async-start(bf16[4,64,2048]{2,1,0:T(8,128)(2,1)} %broadcast_in_dim.38), calls=%async_computation.1 | async-start | bytes 2097152 | tf_op jit(solution)/shard_map/all_to_all | solution.py:141
  70.7 8.0 %all-to-all-done.1 = bf16[4,64,2048]{2,1,0:T(8,128)(2,1)} async-done(((bf16[4,64,2048]{2,1,0:T(8,128)(2,1)}), bf16[4,64,2048]{2,1,0:T(8,128)(2,1)}, u32[]{:S(2)}, u32[]{:S(2)}) %all-to-all-start.1) | async-done | bytes 1048608 | tf_op jit(solution)/shard_map/all_to_all | solution.py:141
  82.5 4.6 %all-to-all-start.2 = ((bf16[4,4,128,512]{3,2,1,0:T(8,128)(2,1)}), bf16[4,4,128,512]{3,2,1,0:T(8,128)(2,1)}, u32[]{:S(2)}, u32[]{:S(2)}) async-start(bf16[4,4,128,512]{3,2,1,0:T(8,128)(2,1)} %broadcast_in_dim.79), calls=%async_computation.2 | async-start | bytes 4194304 | tf_op jit(solution)/shard_map/all_to_all | solution.py:141
  119.1 4.7 %product.7.refs_1_.qkv_ref = bf16[1024,1536]{1,0:T(8,128)(2,1)S(1)} custom-call(bf16[1024,1024]{1,0:T(8,128)(2,1)S(1)} %copy-done.6, bf16[1024,1536]{1,0:T(8,128)(2,1)S(1)} %bitcast.155, f32[1,1536]{1,0:T(1,128)S(1)} %broadcast_in_dim_reshape.4.refs_0_), custom_call_target="tpu_custom_call" | custom-call | flops 310500000 | bytes 1034999 | tf_op jit(solution)/shard_map/product/pallas_call | solution.py:563
  123.9 11.3 %attend.1 = (bf16[1024,512]{1,0:T(8,128)(2,1)S(1)}, f32[4,2,1024]{2,1,0:T(2,128)S(1)}) custom-call(s32[4]{0:T(128)S(1)} %copy-done.48, bf16[1024,1536]{1,0:T(8,128)(2,1)S(1)} %product.7.refs_1_.qkv_ref, s32[1,1024]{1,0:T(1,128)S(1)} %bitcast.161), custom_call_target="tpu_custom_call" | custom-call | flops 1035000000 | bytes 3450000 | tf_op jit(solution)/shard_map/attend/pallas_call | solution.py:484
  142.0 5.2 %proj_norm.1 = (f32[512,1024]{1,0:T(8,128)S(1)}, bf16[512,1024]{1,0:T(8,128)(2,1)}) custom-call(s32[1]{0:T(128)} %bitcast.here_ref, bf16[512,512]{1,0:T(8,128)(2,1)S(1)} %copy-done.22, bf16[512,512]{1,0:T(8,128)(2,1)} %collective-permute-done.9.refs_1_, bf16[1024,512]{1,0:T(8,128)(2,1)S(1)} %bitcast.159, bf16[1024,512]{1,0:T(8,128)(2,1)} %collective-permute-done.10.refs_3_, ...), custom_call_target="tpu_custom_call" | custom-call | flops 270000000 | bytes 900000 | tf_op jit(solution)/shard_map/proj_norm/pallas_call | solution.py:655
  158.4 12.3 %up_part.1 = (bf16[1024,2048]{1,0:T(8,128)(2,1)S(1)}, f32[1024,2048]{1,0:T(8,128)S(1)}) custom-call(bf16[512,1024]{1,0:T(8,128)(2,1)} %get-tuple-element.101.refs_0_, bf16[512,1024]{1,0:T(8,128)(2,1)} %collective-permute-done.13.refs_1_, bf16[1024,2048]{1,0:T(8,128)(2,1)S(1)} %bitcast.152, f32[1,2048]{1,0:T(1,128)S(1)} %bitcast_convert_fusion.refs_3_), custom_call_target="tpu_custom_call" | custom-call | flops 630000000 | bytes 2100000 | tf_op jit(solution)/shard_map/up_part/pallas_call | solution.py:728
  170.7 6.9 %weight_grad.3 = (bf16[4,2,128,512]{3,2,1,0:T(8,128)(2,1)S(1)}, bf16[4,2,128,512]{3,2,1,0:T(8,128)(2,1)S(1)}, bf16[4,2,128,512]{3,2,1,0:T(8,128)(2,1)S(1)}, bf16[4,2,128,512]{3,2,1,0:T(8,128)(2,1)S(1)}) custom-call(s32[3]{0:T(128)S(1)} %pad_add_fusion.place_ref, bf16[1024,2048]{1,0:T(8,128)(2,1)S(1)} %get-tuple-element.122.refs_0_.left_ref, ...), custom_call_target="tpu_custom_call" | custom-call | flops 630000000 | bytes 2100000 | tf_op jit(solution)/shard_map/weight_grad/pallas_call | solution.py:189
  182.8 7.3 %up_back.1 = (bf16[1024,2048]{1,0:T(8,128)(2,1)S(1)}, f32[1,2048]{1,0:T(1,128)S(1)}) custom-call(bf16[1024,1024]{1,0:T(8,128)(2,1)S(1)} %copy-done.5, bf16[2048,1024]{1,0:T(8,128)(2,1)S(1)} %bitcast.149, f32[1024,2048]{1,0:T(8,128)S(1)} %get-tuple-element.109.slope_ref), custom_call_target="tpu_custom_call" | custom-call | flops 585000000 | bytes 1950000 | tf_op jit(solution)/shard_map/up_back/pallas_call | solution.py:759
  190.2 7.2 %weight_grad.4 = (bf16[4,2,64,1024]{3,2,1,0:T(8,128)(2,1)S(1)}, bf16[4,2,64,1024]{3,2,1,0:T(8,128)(2,1)S(1)}, bf16[4,2,64,1024]{3,2,1,0:T(8,128)(2,1)S(1)}, bf16[4,2,64,1024]{3,2,1,0:T(8,128)(2,1)S(1)}) custom-call(s32[3]{0:T(128)S(1)} %pad_add_fusion.place_ref, bf16[512,1024]{1,0:T(8,128)(2,1)} %get-tuple-element.101.refs_0_, ...), custom_call_target="tpu_custom_call" | custom-call | flops 630000000 | bytes 2100000 | tf_op jit(solution)/shard_map/weight_grad/pallas_call | solution.py:189
  212.4 4.2 %product.10 = bf16[512,1024]{1,0:T(8,128)(2,1)} custom-call(bf16[1024,2048]{1,0:T(8,128)(2,1)S(1)} %get-tuple-element.122.refs_0_.left_ref, bf16[2048,1024]{1,0:T(8,128)(2,1)S(1)} %bitcast.150), custom_call_target="tpu_custom_call" | custom-call | flops 207000000 | bytes 690000 | tf_op jit(solution)/shard_map/product/pallas_call | solution.py:563
  221.5 4.8 %collective-permute-done.23.refs_3_ = bf16[4,2,64,1024]{3,2,1,0:T(8,128)(2,1)S(1)} collective-permute-done((bf16[4,2,64,1024]{3,2,1,0:T(8,128)(2,1)S(1)}, bf16[4,2,64,1024]{3,2,1,0:T(8,128)(2,1)S(1)}, u32[]{:S(2)}, u32[]{:S(2)}) %collective-permute-start.23) | collective-permute-done | bytes 1048608 | tf_op jit(solution)/shard_map/ppermute | solution.py:52
  229.6 5.3 %proj_back.1 = (bf16[1536,512]{1,0:T(8,128)(2,1)S(1)}, bf16[1536,512]{1,0:T(8,128)(2,1)}) custom-call(s32[1]{0:T(128)} %bitcast.here_ref, bf16[512,1024]{1,0:T(8,128)(2,1)S(1)} %get-tuple-element.127.grad_ref, bf16[512,512]{1,0:T(8,128)(2,1)S(1)} %copy-done.23, bf16[512,512]{1,0:T(8,128)(2,1)} %collective-permute-done.9.refs_1_, ...), custom_call_target="tpu_custom_call" | custom-call | flops 360000000 | bytes 1200000 | tf_op jit(solution)/shard_map/proj_back/pallas_call | solution.py:691
  247.1 18.6 %attend_back.1 = (bf16[1024,1536]{1,0:T(8,128)(2,1)S(1)}, f32[1,1536]{1,0:T(1,128)S(1)}) custom-call(s32[4]{0:T(128)S(1)} %copy-done.48, bf16[1024,1536]{1,0:T(8,128)(2,1)S(1)} %copy-done.9, bf16[1536,512]{1,0:T(8,128)(2,1)S(1)} %copy-done.17, bf16[1536,512]{1,0:T(8,128)(2,1)} %collective-permute-done.24.refs_1_.refs_3_, ...), custom_call_target="tpu_custom_call" | custom-call | flops 1620000000 | bytes 5400000 | tf_op jit(solution)/shard_map/attend_back/pallas_call | solution.py:520
  265.8 7.9 %weight_grad.5 = (bf16[4,2,64,1024]{3,2,1,0:T(8,128)(2,1)S(1)}, bf16[4,2,64,1024]{3,2,1,0:T(8,128)(2,1)}, bf16[4,2,64,1024]{3,2,1,0:T(8,128)(2,1)S(1)}, bf16[4,2,64,1024]{3,2,1,0:T(8,128)(2,1)}) custom-call(s32[3]{0:T(128)S(1)} %pad_add_fusion.place_ref, bf16[1024,1024]{1,0:T(8,128)(2,1)S(1)} %copy-done.7, ...), custom_call_target="tpu_custom_call" | custom-call | flops 630000000 | bytes 2100000 | tf_op jit(solution)/shard_map/weight_grad/pallas_call | solution.py:189
  277.8 4.7 %all-to-all-start.3 = ((bf16[4,128,2048]{2,1,0:T(8,128)(2,1)}), bf16[4,128,2048]{2,1,0:T(8,128)(2,1)}, u32[]{:S(2)}, u32[]{:S(2)}) async-start(bf16[4,128,2048]{2,1,0:T(8,128)(2,1)} %copy-done.12), calls=%async_computation.3 | async-start | bytes 4194304 | tf_op jit(solution)/shard_map/all_to_all | solution.py:311
  306.8 6.9 %collective-permute-done.31.refs_3_ = bf16[4,2,64,1024]{3,2,1,0:T(8,128)(2,1)} collective-permute-done((bf16[4,2,64,1024]{3,2,1,0:T(8,128)(2,1)}, bf16[4,2,64,1024]{3,2,1,0:T(8,128)(2,1)}, u32[]{:S(2)}, u32[]{:S(2)}) %collective-permute-start.31) | collective-permute-done | bytes 1048608 | tf_op jit(solution)/shard_map/ppermute | solution.py:52
  321.4 9.4 %all-to-all-done.3 = bf16[4,128,2048]{2,1,0:T(8,128)(2,1)} async-done(((bf16[4,128,2048]{2,1,0:T(8,128)(2,1)}), bf16[4,128,2048]{2,1,0:T(8,128)(2,1)}, u32[]{:S(2)}, u32[]{:S(2)}) %all-to-all-start.3) | async-done | bytes 2097184 | tf_op jit(solution)/shard_map/all_to_all | solution.py:311
  337.5 5.1 %all-to-all-start.4 = ((bf16[4,72,2048]{2,1,0:T(8,128)(2,1)}), bf16[4,72,2048]{2,1,0:T(8,128)(2,1)S(1)}, u32[]{:S(2)}, u32[]{:S(2)}) async-start(bf16[4,72,2048]{2,1,0:T(8,128)(2,1)} %split_over_z.1), calls=%async_computation.4 | async-start | bytes 2359296 | tf_op jit(solution)/shard_map/all_to_all | solution.py:311
  353.5 7.2 %collective-permute-done.38 = bf16[256,1024]{1,0:T(8,128)(2,1)} collective-permute-done((bf16[256,1024]{1,0:T(8,128)(2,1)}, bf16[256,1024]{1,0:T(8,128)(2,1)}, u32[]{:S(2)}, u32[]{:S(2)}) %collective-permute-start.38) | collective-permute-done | bytes 524320 | tf_op jit(solution)/shard_map/ppermute | solution.py:52
  362.8 6.4 %all-to-all-done.4 = bf16[4,72,2048]{2,1,0:T(8,128)(2,1)S(1)} async-done(((bf16[4,72,2048]{2,1,0:T(8,128)(2,1)}), bf16[4,72,2048]{2,1,0:T(8,128)(2,1)S(1)}, u32[]{:S(2)}, u32[]{:S(2)}) %all-to-all-start.4) | async-done | bytes 1179680 | tf_op jit(solution)/shard_map/all_to_all | solution.py:311
  (381 shorter events, 196.8 us)
Async XLA Ops:
  7.6 26.3 %collective-permute-start = (bf16[2,256,1024]{2,1,0:T(8,128)(2,1)}, bf16[2,256,1024]{2,1,0:T(8,128)(2,1)S(1)}, u32[]{:S(2)}, u32[]{:S(2)}) collective-permute-start(bf16[2,256,1024]{2,1,0:T(8,128)(2,1)} %get-tuple-element.176), channel_id=1, source_target_pairs={{0,2},{2,0},{1,3},{3,1},{4,6},{6,4},{5,7},{7,5},{8,10},{10,8},{9,1... | collective-permute-start | bytes 3145736 | tf_op jit(solution)/shard_map/ppermute | solution.py:52
  12.0 33.2 %all-to-all-start = ((bf16[4,72,2048]{2,1,0:T(8,128)(2,1)}), bf16[4,72,2048]{2,1,0:T(8,128)(2,1)S(1)}, u32[]{:S(2)}, u32[]{:S(2)}) async-start(bf16[4,72,2048]{2,1,0:T(8,128)(2,1)} %broadcast_in_dim.37), calls=%async_computation | async-start | bytes 2359296 | tf_op jit(solution)/shard_map/all_to_all | solution.py:141
  35.6 29.9 %collective-permute-start.1 = (bf16[2,512,1024]{2,1,0:T(8,128)(2,1)}, bf16[2,512,1024]{2,1,0:T(8,128)(2,1)}, u32[]{:S(2)}, u32[]{:S(2)}) collective-permute-start(bf16[2,512,1024]{2,1,0:T(8,128)(2,1)} %pad_maximum_fusion.1), channel_id=1, source_target_pairs={{0,1},{1,0},{2,3},{3,2},{4,5},{5,4},{6,7},{7,6},{8,9},{9,8},{10,11... | collective-permute-start | bytes 6291464 | tf_op jit(solution)/shard_map/ppermute | solution.py:52
  49.7 29.0 %all-to-all-start.1 = ((bf16[4,64,2048]{2,1,0:T(8,128)(2,1)}), bf16[4,64,2048]{2,1,0:T(8,128)(2,1)}, u32[]{:S(2)}, u32[]{:S(2)}) async-start(bf16[4,64,2048]{2,1,0:T(8,128)(2,1)} %broadcast_in_dim.38), calls=%async_computation.1 | async-start | bytes 2097152 | tf_op jit(solution)/shard_map/all_to_all | solution.py:141
  60.9 31.4 %collective-permute-start.4 = (bf16[2,4,72,1024]{3,2,1,0:T(8,128)(2,1)S(1)}, bf16[2,4,72,1024]{3,2,1,0:T(8,128)(2,1)S(1)}, u32[]{:S(2)}, u32[]{:S(2)}) collective-permute-start(bf16[2,4,72,1024]{3,2,1,0:T(8,128)(2,1)S(1)} %pad_maximum_fusion.2.refs_0_), channel_id=1, source_target_pairs={{0,4},{4,0},{1,5},{5,1},{2,6},{6,2},{3,7},{7,3},{8,12},{12,8},{9,1... | collective-permute-start | bytes 3538952 | tf_op jit(solution)/shard_map/ppermute | solution.py:52
  64.6 28.6 %collective-permute-start.6 = (bf16[2,4,72,1024]{3,2,1,0:T(8,128)(2,1)S(1)}, bf16[2,4,72,1024]{3,2,1,0:T(8,128)(2,1)}, u32[]{:S(2)}, u32[]{:S(2)}) collective-permute-start(bf16[2,4,72,1024]{3,2,1,0:T(8,128)(2,1)S(1)} %pad_maximum_fusion.3.refs_2_), channel_id=1, source_target_pairs={{0,2},{2,0},{1,3},{3,1},{4,6},{6,4},{5,7},{7,5},{8,10},{10,8},{9,1... | collective-permute-start | bytes 3538952 | tf_op jit(solution)/shard_map/ppermute | solution.py:52
  82.5 66.1 %all-to-all-start.2 = ((bf16[4,4,128,512]{3,2,1,0:T(8,128)(2,1)}), bf16[4,4,128,512]{3,2,1,0:T(8,128)(2,1)}, u32[]{:S(2)}, u32[]{:S(2)}) async-start(bf16[4,4,128,512]{3,2,1,0:T(8,128)(2,1)} %broadcast_in_dim.79), calls=%async_computation.2 | async-start | bytes 4194304 | tf_op jit(solution)/shard_map/all_to_all | solution.py:141
  101.0 37.5 %collective-permute-start.10 = (bf16[1024,512]{1,0:T(8,128)(2,1)}, bf16[1024,512]{1,0:T(8,128)(2,1)}, u32[]{:S(2)}, u32[]{:S(2)}) collective-permute-start(bf16[1024,512]{1,0:T(8,128)(2,1)} %bitcast.158), channel_id=1, source_target_pairs={{0,1},{1,0},{2,3},{3,2},{4,5},{5,4},{6,7},{7,6},{8,9},{9,8},{10,11... | collective-permute-start | bytes 3145736 | tf_op jit(solution)/shard_map/ppermute | solution.py:52
  108.8 29.2 %collective-permute-start.12 = (bf16[2,4,64,1024]{3,2,1,0:T(8,128)(2,1)}, bf16[2,4,64,1024]{3,2,1,0:T(8,128)(2,1)}, u32[]{:S(2)}, u32[]{:S(2)}) collective-permute-start(bf16[2,4,64,1024]{3,2,1,0:T(8,128)(2,1)} %pad_maximum_fusion.5.refs_2_), channel_id=1, source_target_pairs={{0,2},{2,0},{1,3},{3,1},{4,6},{6,4},{5,7},{7,5},{8,10},{10,8},{9,1... | collective-permute-start | bytes 3145736 | tf_op jit(solution)/shard_map/ppermute | solution.py:52
  151.9 27.4 %collective-permute-start.16 = (bf16[2,4,128,512]{3,2,1,0:T(8,128)(2,1)}, bf16[2,4,128,512]{3,2,1,0:T(8,128)(2,1)}, u32[]{:S(2)}, u32[]{:S(2)}) collective-permute-start(bf16[2,4,128,512]{3,2,1,0:T(8,128)(2,1)} %get-tuple-element.107.refs_0_), channel_id=1, source_target_pairs={{0,4},{4,0},{1,5},{5,1},{2,6},{6,2},{3,7},{7,3},{8,12},{12,8},{9,1... | collective-permute-start | bytes 3145736 | tf_op jit(solution)/shard_map/ppermute | solution.py:52
  152.5 26.8 %collective-permute-start.17 = (bf16[2,4,128,512]{3,2,1,0:T(8,128)(2,1)}, bf16[2,4,128,512]{3,2,1,0:T(8,128)(2,1)}, u32[]{:S(2)}, u32[]{:S(2)}) collective-permute-start(bf16[2,4,128,512]{3,2,1,0:T(8,128)(2,1)} %get-tuple-element.108.refs_2_), channel_id=1, source_target_pairs={{0,2},{2,0},{1,3},{3,1},{4,6},{6,4},{5,7},{7,5},{8,10},{10,8},{9,1... | collective-permute-start | bytes 3145736 | tf_op jit(solution)/shard_map/ppermute | solution.py:52
  177.6 25.7 %collective-permute-start.19 = (bf16[4,2,128,512]{3,2,1,0:T(8,128)(2,1)S(1)}, bf16[4,2,128,512]{3,2,1,0:T(8,128)(2,1)S(1)}, u32[]{:S(2)}, u32[]{:S(2)}) collective-permute-start(bf16[4,2,128,512]{3,2,1,0:T(8,128)(2,1)S(1)} %get-tuple-element.104), channel_id=1, source_target_pairs={{0,2},{2,0},{1,3},{3,1},{4,6},{6,4},{5,7},{7,5},{8,10},{10,8},{9,1... | collective-permute-start | bytes 3145736 | tf_op jit(solution)/shard_map/ppermute | solution.py:52
  177.7 25.6 %collective-permute-start.20 = (bf16[4,2,128,512]{3,2,1,0:T(8,128)(2,1)S(1)}, bf16[4,2,128,512]{3,2,1,0:T(8,128)(2,1)S(1)}, u32[]{:S(2)}, u32[]{:S(2)}) collective-permute-start(bf16[4,2,128,512]{3,2,1,0:T(8,128)(2,1)S(1)} %get-tuple-element.117), channel_id=1, source_target_pairs={{0,4},{4,0},{1,5},{5,1},{2,6},{6,2},{3,7},{7,3},{8,12},{12,8},{9,1... | collective-permute-start | bytes 3145736 | tf_op jit(solution)/shard_map/ppermute | solution.py:52
  200.8 25.6 %collective-permute-start.23 = (bf16[4,2,64,1024]{3,2,1,0:T(8,128)(2,1)S(1)}, bf16[4,2,64,1024]{3,2,1,0:T(8,128)(2,1)S(1)}, u32[]{:S(2)}, u32[]{:S(2)}) collective-permute-start(bf16[4,2,64,1024]{3,2,1,0:T(8,128)(2,1)S(1)} %get-tuple-element.125), channel_id=1, source_target_pairs={{0,4},{4,0},{1,5},{5,1},{2,6},{6,2},{3,7},{7,3},{8,12},{12,8},{9,1... | collective-permute-start | bytes 3145736 | tf_op jit(solution)/shard_map/ppermute | solution.py:52
  201.5 25.3 %collective-permute-start.22 = (bf16[4,2,64,1024]{3,2,1,0:T(8,128)(2,1)S(1)}, bf16[4,2,64,1024]{3,2,1,0:T(8,128)(2,1)S(1)}, u32[]{:S(2)}, u32[]{:S(2)}) collective-permute-start(bf16[4,2,64,1024]{3,2,1,0:T(8,128)(2,1)S(1)} %get-tuple-element.114), channel_id=1, source_target_pairs={{0,2},{2,0},{1,3},{3,1},{4,6},{6,4},{5,7},{7,5},{8,10},{10,8},{9,1... | collective-permute-start | bytes 3145736 | tf_op jit(solution)/shard_map/ppermute | solution.py:52
  236.6 39.0 %collective-permute-start.27 = (bf16[4,128,512]{2,1,0:T(8,128)(2,1)}, bf16[4,128,512]{2,1,0:T(8,128)(2,1)S(1)}, u32[]{:S(2)}, u32[]{:S(2)}) collective-permute-start(bf16[4,128,512]{2,1,0:T(8,128)(2,1)} %copy-done.50), channel_id=1, source_target_pairs={{0,4},{4,0},{1,5},{5,1},{2,6},{6,2},{3,7},{7,3},{8,12},{12,8},{9,1... | collective-permute-start | bytes 1572872 | tf_op jit(solution)/shard_map/ppermute | solution.py:52
  238.1 37.5 %collective-permute-start.28 = (bf16[4,128,512]{2,1,0:T(8,128)(2,1)}, bf16[4,128,512]{2,1,0:T(8,128)(2,1)S(1)}, u32[]{:S(2)}, u32[]{:S(2)}) collective-permute-start(bf16[4,128,512]{2,1,0:T(8,128)(2,1)} %copy-done.49), channel_id=1, source_target_pairs={{0,2},{2,0},{1,3},{3,1},{4,6},{6,4},{5,7},{7,5},{8,10},{10,8},{9,1... | collective-permute-start | bytes 1572872 | tf_op jit(solution)/shard_map/ppermute | solution.py:52
  239.8 35.8 %collective-permute-start.25 = (bf16[4,64,1024]{2,1,0:T(8,128)(2,1)}, bf16[4,64,1024]{2,1,0:T(8,128)(2,1)S(1)}, u32[]{:S(2)}, u32[]{:S(2)}) collective-permute-start(bf16[4,64,1024]{2,1,0:T(8,128)(2,1)} %copy-done.52), channel_id=1, source_target_pairs={{0,4},{4,0},{1,5},{5,1},{2,6},{6,2},{3,7},{7,3},{8,12},{12,8},{9,1... | collective-permute-start | bytes 1572872 | tf_op jit(solution)/shard_map/ppermute | solution.py:52
  241.3 34.4 %collective-permute-start.26 = (bf16[4,64,1024]{2,1,0:T(8,128)(2,1)}, bf16[4,64,1024]{2,1,0:T(8,128)(2,1)S(1)}, u32[]{:S(2)}, u32[]{:S(2)}) collective-permute-start(bf16[4,64,1024]{2,1,0:T(8,128)(2,1)} %copy-done.51), channel_id=1, source_target_pairs={{0,2},{2,0},{1,3},{3,1},{4,6},{6,4},{5,7},{7,5},{8,10},{10,8},{9,1... | collective-permute-start | bytes 1572872 | tf_op jit(solution)/shard_map/ppermute | solution.py:52
  277.8 53.0 %all-to-all-start.3 = ((bf16[4,128,2048]{2,1,0:T(8,128)(2,1)}), bf16[4,128,2048]{2,1,0:T(8,128)(2,1)}, u32[]{:S(2)}, u32[]{:S(2)}) async-start(bf16[4,128,2048]{2,1,0:T(8,128)(2,1)} %copy-done.12), calls=%async_computation.3 | async-start | bytes 4194304 | tf_op jit(solution)/shard_map/all_to_all | solution.py:311
  287.7 26.0 %collective-permute-start.31 = (bf16[4,2,64,1024]{3,2,1,0:T(8,128)(2,1)}, bf16[4,2,64,1024]{3,2,1,0:T(8,128)(2,1)}, u32[]{:S(2)}, u32[]{:S(2)}) collective-permute-start(bf16[4,2,64,1024]{3,2,1,0:T(8,128)(2,1)} %get-tuple-element.156), channel_id=1, source_target_pairs={{0,4},{4,0},{1,5},{5,1},{2,6},{6,2},{3,7},{7,3},{8,12},{12,8},{9,1... | collective-permute-start | bytes 3145736 | tf_op jit(solution)/shard_map/ppermute | solution.py:52
  289.1 25.9 %collective-permute-start.30 = (bf16[4,2,64,1024]{3,2,1,0:T(8,128)(2,1)}, bf16[4,2,64,1024]{3,2,1,0:T(8,128)(2,1)}, u32[]{:S(2)}, u32[]{:S(2)}) collective-permute-start(bf16[4,2,64,1024]{3,2,1,0:T(8,128)(2,1)} %get-tuple-element.135), channel_id=1, source_target_pairs={{0,2},{2,0},{1,3},{3,1},{4,6},{6,4},{5,7},{7,5},{8,10},{10,8},{9,1... | collective-permute-start | bytes 3145736 | tf_op jit(solution)/shard_map/ppermute | solution.py:52
  337.5 31.8 %all-to-all-start.4 = ((bf16[4,72,2048]{2,1,0:T(8,128)(2,1)}), bf16[4,72,2048]{2,1,0:T(8,128)(2,1)S(1)}, u32[]{:S(2)}, u32[]{:S(2)}) async-start(bf16[4,72,2048]{2,1,0:T(8,128)(2,1)} %split_over_z.1), calls=%async_computation.4 | async-start | bytes 2359296 | tf_op jit(solution)/shard_map/all_to_all | solution.py:311
  347.0 24.5 %collective-permute-start.37 = (bf16[256,1024]{1,0:T(8,128)(2,1)}, bf16[256,1024]{1,0:T(8,128)(2,1)}, u32[]{:S(2)}, u32[]{:S(2)}) collective-permute-start(bf16[256,1024]{1,0:T(8,128)(2,1)} %slice_bitcast_fusion), channel_id=1, source_target_pairs={{0,2},{2,0},{1,3},{3,1},{4,6},{6,4},{5,7},{7,5},{8,10},{10,8},{9,1... | collective-permute-start | bytes 1572872 | tf_op jit(solution)/shard_map/ppermute | solution.py:52
  (95 other events, 671.5 us)

commit v5 on v4

--- a/solution.py
+++ b/solution.py
@@ -570,7 +570,7 @@
         compiler_params=pltpu.CompilerParams(vmem_limit_bytes=16 << 20),
         cost_estimate=cost(2.3 * rows * width * depth / 2**30),
         name="product",
-    )(left, right, *extra)
+    )(*(pltpu.with_memory_space_constraint(a, pltpu.HBM) for a in (left, right)), *extra)
 
 
 def norm_back_part(summands, values, gain, added, scale=None):
@@ -722,7 +722,7 @@
                 value, slope = gelu_parts(u)
                 at = slice(i * tokens + r, i * tokens + r + rows)
                 active_ref[at] = half(value)
-                slope_ref[at] = slope
+                slope_ref[at] = half(slope)
 
     column = pl.BlockSpec((n * tokens, block), lambda i: (0, i))
     return pl.pallas_call(
@@ -734,7 +734,7 @@
             pl.BlockSpec((1, block), lambda i: (0, i)),
         ],
         out_specs=[column, column],
-        out_shape=[jax.ShapeDtypeStruct((n * tokens, ff), BF), jax.ShapeDtypeStruct((n * tokens, ff), F32)],
+        out_shape=[jax.ShapeDtypeStruct((n * tokens, ff), BF)] * 2,
         compiler_params=pltpu.CompilerParams(vmem_limit_bytes=16 << 20),
         cost_estimate=cost(7),
         name="up_part",

time: 386 us -> 385 us (level)
  Pallas kernels: 131 us -> 149 us
  waiting for transfers between devices: 82.1 us -> 74.2 us
  local copies, waits for them, and re-layouts: 52.8 us -> 45.1 us
    pallas_call x7, Pallas kernels: 24.8 us -> 41 us  [product(): pl.pallas_call(kernel, grid=(width // block,), in_specs=[pl.BlockSpec((ro...]
    unnamed x149 -> x121, local copies, waits for them, and re-layouts: 28.2 us -> 17.3 us
    ppermute x38, waiting for transfers between devices: 52.1 us -> 46.3 us  [shift(): lax.ppermute(value, axis, [(i, (i + step) % size) for i in range(size)])]
    ppermute x38, starting transfers between devices: 34.8 us -> 29.6 us  [shift(): lax.ppermute(value, axis, [(i, (i + step) % size) for i in range(size)])]
  transfers between devices with their start and end apart: 46 -> 46, of which waited for: 18 -> 19; matrix products, arithmetic and copies ran while one was open for 17% -> 18% of each run, Pallas kernels for 32% -> 37%
where the time goes in v5:
time: 385 us; the launch traced here: 379 us
  Pallas kernels  149 us (39%)
  waiting for transfers between devices  74.2 us (19%)
  starting transfers between devices  58.7 us (15%)
  other arithmetic  49.1 us (13%)
  local copies, waits for them, and re-layouts  45.1 us (12%)
    ppermute x38, waiting for transfers between devices, shift(): lax.ppermute(value, axis, [(i, (i + step) % size) for i in range(size)])  46.3 us
    pallas_call x7, Pallas kernels, product(): pl.pallas_call(kernel, grid=(width // block,), in_specs=[pl.BlockSpec((ro...  41 us
    ppermute x38, starting transfers between devices, shift(): lax.ppermute(value, axis, [(i, (i + step) % size) for i in range(size)])  29.6 us
    pallas_call x3, Pallas kernels, weight_grad(): pl.pallas_call(kernel, grid=(nz,), in_specs=[whole(pltpu.SMEM)] + [pl.Blo...  22.2 us
    pallas_call x1, Pallas kernels, attend_back(): pl.pallas_call(kernel, grid=(steps,), in_specs=[whole(pltpu.SMEM), pl.Blo...  18.6 us
    unnamed x121, local copies, waits for them, and re-layouts  17.3 us
    all_to_all x2, waiting for transfers between devices, over_z(): return lax.all_to_all(blocks, 'z', 0, 0, tiled=True)  15.8 us
    all_to_all x3, starting transfers between devices, gather_over_z(): return lax.all_to_all(copies, 'z', 0, 0, tiled=True)  13.7 us
  transfers between devices with their start and end apart: 46, of which 19 were waited for; matrix products, arithmetic and copies ran while one was open for 18% of the time, Pallas kernels for 37%

profile of v5, /device:TPU:0, one launch (start us, length us, event | category | flops | bytes accessed | tf_op | source)
XLA Modules:
  0.0 378.6 jit_solution(10215588998136530463)
XLA Ops:
  16.8 17.1 %collective-permute-done = bf16[2,256,1024]{2,1,0:T(8,128)(2,1)S(1)} collective-permute-done((bf16[2,256,1024]{2,1,0:T(8,128)(2,1)}, bf16[2,256,1024]{2,1,0:T(8,128)(2,1)S(1)}, u32[]{:S(2)}, u32[]{:S(2)}) %collective-permute-start) | collective-permute-done | bytes 1048608 | tf_op jit(solution)/shard_map/ppermute | solution.py:52
  39.6 5.5 %all-to-all-done = bf16[4,72,2048]{2,1,0:T(8,128)(2,1)S(1)} async-done(((bf16[4,72,2048]{2,1,0:T(8,128)(2,1)}), bf16[4,72,2048]{2,1,0:T(8,128)(2,1)S(1)}, u32[]{:S(2)}, u32[]{:S(2)}) %all-to-all-start) | async-done | bytes 1179680 | tf_op jit(solution)/shard_map/all_to_all | solution.py:141
  72.4 6.5 %all-to-all-done.1 = bf16[4,64,2048]{2,1,0:T(8,128)(2,1)} async-done(((bf16[4,64,2048]{2,1,0:T(8,128)(2,1)}), bf16[4,64,2048]{2,1,0:T(8,128)(2,1)}, u32[]{:S(2)}, u32[]{:S(2)}) %all-to-all-start.1) | async-done | bytes 1048608 | tf_op jit(solution)/shard_map/all_to_all | solution.py:141
  114.3 6.9 %product.7.refs_1_.qkv_ref = bf16[1024,1536]{1,0:T(8,128)(2,1)S(1)} custom-call(bf16[1024,1024]{1,0:T(8,128)(2,1)} %fusion.6.left_ref.refs_0_, bf16[1024,1536]{1,0:T(8,128)(2,1)} %bitcast.155, f32[1,1536]{1,0:T(1,128)S(1)} %broadcast_in_dim_reshape.4.refs_0_), custom_call_target="tpu_custom_call" | custom-call | flops 310500000 | bytes 1034999 | tf_op jit(solution)/shard_map/product/pallas_call | solution.py:563
  121.3 11.3 %attend.1 = (bf16[1024,512]{1,0:T(8,128)(2,1)S(1)}, f32[4,2,1024]{2,1,0:T(2,128)S(1)}) custom-call(s32[4]{0:T(128)S(1)} %fusion.28.refs_0_.order_ref, bf16[1024,1536]{1,0:T(8,128)(2,1)S(1)} %product.7.refs_1_.qkv_ref, s32[1,1024]{1,0:T(1,128)S(1)} %bitcast.161), custom_call_target="tpu_custom_call" | custom-call | flops 1035000000 | bytes 3450000 | tf_op jit(solution)/shard_map/attend/pallas_call | solution.py:484
  138.2 5.2 %proj_norm.1 = (f32[512,1024]{1,0:T(8,128)S(1)}, bf16[512,1024]{1,0:T(8,128)(2,1)}) custom-call(s32[1]{0:T(128)} %bitcast.here_ref, bf16[512,512]{1,0:T(8,128)(2,1)S(1)} %copy-done.17, bf16[512,512]{1,0:T(8,128)(2,1)} %collective-permute-done.9.refs_1_, bf16[1024,512]{1,0:T(8,128)(2,1)S(1)} %bitcast.159, bf16[1024,512]{1,0:T(8,128)(2,1)} %collective-permute-done.10.refs_3_, ...), custom_call_target="tpu_custom_call" | custom-call | flops 270000000 | bytes 900000 | tf_op jit(solution)/shard_map/proj_norm/pallas_call | solution.py:655
  153.3 12.8 %up_part.1 = (bf16[1024,2048]{1,0:T(8,128)(2,1)S(1)}, bf16[1024,2048]{1,0:T(8,128)(2,1)S(1)}) custom-call(bf16[512,1024]{1,0:T(8,128)(2,1)} %get-tuple-element.101.refs_0_, bf16[512,1024]{1,0:T(8,128)(2,1)S(1)} %collective-permute-done.13.refs_1_, bf16[1024,2048]{1,0:T(8,128)(2,1)S(1)} %bitcast.149, f32[1,2048]{1,0:T(1,128)S(1)} %bitcast_convert_fusion.refs_3_), custom_call_target="tpu_custom_call" | custom-call | flops 630000000 | bytes 2100000 | tf_op jit(solution)/shard_map/up_part/pallas_call | solution.py:728
  166.2 6.9 %weight_grad.3 = (bf16[4,2,128,512]{3,2,1,0:T(8,128)(2,1)S(1)}, bf16[4,2,128,512]{3,2,1,0:T(8,128)(2,1)S(1)}, bf16[4,2,128,512]{3,2,1,0:T(8,128)(2,1)S(1)}, bf16[4,2,128,512]{3,2,1,0:T(8,128)(2,1)S(1)}) custom-call(s32[3]{0:T(128)S(1)} %pad_add_fusion.place_ref, bf16[1024,2048]{1,0:T(8,128)(2,1)S(1)} %get-tuple-element.122.refs_0_.left_ref, ...), custom_call_target="tpu_custom_call" | custom-call | flops 630000000 | bytes 2100000 | tf_op jit(solution)/shard_map/weight_grad/pallas_call | solution.py:189
  179.3 7.5 %up_back.1 = (bf16[1024,2048]{1,0:T(8,128)(2,1)S(1)}, f32[1,2048]{1,0:T(1,128)S(1)}) custom-call(bf16[1024,1024]{1,0:T(8,128)(2,1)S(1)} %get-tuple-element.105.refs_1_.g_ref, bf16[2048,1024]{1,0:T(8,128)(2,1)S(1)} %bitcast.152, bf16[1024,2048]{1,0:T(8,128)(2,1)S(1)} %get-tuple-element.109.slope_ref), custom_call_target="tpu_custom_call" | custom-call | flops 585000000 | bytes 1950000 | tf_op jit(solution)/shard_map/up_back/pallas_call | solution.py:759
  186.8 7.4 %weight_grad.4 = (bf16[4,2,64,1024]{3,2,1,0:T(8,128)(2,1)S(1)}, bf16[4,2,64,1024]{3,2,1,0:T(8,128)(2,1)S(1)}, bf16[4,2,64,1024]{3,2,1,0:T(8,128)(2,1)S(1)}, bf16[4,2,64,1024]{3,2,1,0:T(8,128)(2,1)S(1)}) custom-call(s32[3]{0:T(128)S(1)} %pad_add_fusion.place_ref, bf16[512,1024]{1,0:T(8,128)(2,1)} %get-tuple-element.101.refs_0_, ...), custom_call_target="tpu_custom_call" | custom-call | flops 630000000 | bytes 2100000 | tf_op jit(solution)/shard_map/weight_grad/pallas_call | solution.py:189
  194.2 5.8 %product.8 = bf16[512,1024]{1,0:T(8,128)(2,1)S(1)} custom-call(bf16[1024,2048]{1,0:T(8,128)(2,1)} %copy-done.5, bf16[1024,2048]{1,0:T(8,128)(2,1)} %bitcast.150), custom_call_target="tpu_custom_call" | custom-call | flops 207000000 | bytes 690000 | tf_op jit(solution)/shard_map/product/pallas_call | solution.py:563
  203.6 6.1 %product.9.refs_0_ = f32[512,1024]{1,0:T(8,128)S(1)} custom-call(bf16[1024,2048]{1,0:T(8,128)(2,1)} %copy-done.5, bf16[1024,2048]{1,0:T(8,128)(2,1)} %bitcast.151), custom_call_target="tpu_custom_call" | custom-call | flops 207000000 | bytes 690000 | tf_op jit(solution)/shard_map/product/pallas_call | solution.py:563
  212.1 6.2 %product.10 = bf16[512,1024]{1,0:T(8,128)(2,1)S(1)} custom-call(bf16[1024,2048]{1,0:T(8,128)(2,1)} %copy-done.4, bf16[2048,1024]{1,0:T(8,128)(2,1)} %bitcast.153), custom_call_target="tpu_custom_call" | custom-call | flops 207000000 | bytes 690000 | tf_op jit(solution)/shard_map/product/pallas_call | solution.py:563
  218.3 5.5 %product.11 = f32[512,1024]{1,0:T(8,128)S(1)} custom-call(bf16[1024,2048]{1,0:T(8,128)(2,1)} %copy-done.4, bf16[2048,1024]{1,0:T(8,128)(2,1)} %bitcast.154), custom_call_target="tpu_custom_call" | custom-call | flops 207000000 | bytes 690000 | tf_op jit(solution)/shard_map/product/pallas_call | solution.py:563
  230.7 4.9 %proj_back.1 = (bf16[1536,512]{1,0:T(8,128)(2,1)S(1)}, bf16[1536,512]{1,0:T(8,128)(2,1)}) custom-call(s32[1]{0:T(128)} %bitcast.here_ref, bf16[512,1024]{1,0:T(8,128)(2,1)S(1)} %get-tuple-element.127.grad_ref, bf16[512,512]{1,0:T(8,128)(2,1)S(1)} %copy-done.18, bf16[512,512]{1,0:T(8,128)(2,1)} %collective-permute-done.9.refs_1_, ...), custom_call_target="tpu_custom_call" | custom-call | flops 360000000 | bytes 1200000 | tf_op jit(solution)/shard_map/proj_back/pallas_call | solution.py:691
  245.7 18.6 %attend_back.1 = (bf16[1024,1536]{1,0:T(8,128)(2,1)S(1)}, f32[1,1536]{1,0:T(1,128)S(1)}) custom-call(s32[4]{0:T(128)S(1)} %fusion.28.refs_0_.order_ref, bf16[1024,1536]{1,0:T(8,128)(2,1)S(1)} %copy-done.10, bf16[1536,512]{1,0:T(8,128)(2,1)S(1)} %copy-done.16, bf16[1536,512]{1,0:T(8,128)(2,1)} %collective-permute-done.24.refs_1_.refs_3_, ...), custom_call_target="tpu_custom_call" | custom-call | flops 1620000000 | bytes 5400000 | tf_op jit(solution)/shard_map/attend_back/pallas_call | solution.py:520
  264.3 7.9 %weight_grad.5 = (bf16[4,2,64,1024]{3,2,1,0:T(8,128)(2,1)S(1)}, bf16[4,2,64,1024]{3,2,1,0:T(8,128)(2,1)}, bf16[4,2,64,1024]{3,2,1,0:T(8,128)(2,1)S(1)}, bf16[4,2,64,1024]{3,2,1,0:T(8,128)(2,1)}) custom-call(s32[3]{0:T(128)S(1)} %pad_add_fusion.place_ref, bf16[1024,1024]{1,0:T(8,128)(2,1)S(1)} %copy-done.8, ...), custom_call_target="tpu_custom_call" | custom-call | flops 630000000 | bytes 2100000 | tf_op jit(solution)/shard_map/weight_grad/pallas_call | solution.py:189
  274.4 6.8 %all-to-all-start.3 = ((bf16[4,128,2048]{2,1,0:T(8,128)(2,1)}), bf16[4,128,2048]{2,1,0:T(8,128)(2,1)}, u32[]{:S(2)}, u32[]{:S(2)}) async-start(bf16[4,128,2048]{2,1,0:T(8,128)(2,1)} %split_both_over_z.1), calls=%async_computation.3 | async-start | bytes 4194304 | tf_op jit(solution)/shard_map/all_to_all | solution.py:311
  281.2 5.6 %product.12 = bf16[512,1024]{1,0:T(8,128)(2,1)} custom-call(bf16[1024,1536]{1,0:T(8,128)(2,1)} %copy-done.7, bf16[1024,1536]{1,0:T(8,128)(2,1)} %bitcast.156), custom_call_target="tpu_custom_call" | custom-call | flops 155250000 | bytes 517499 | tf_op jit(solution)/shard_map/product/pallas_call | solution.py:563
  292.4 4.9 %product.13.refs_0_ = f32[512,1024]{1,0:T(8,128)S(1)} custom-call(bf16[1024,1536]{1,0:T(8,128)(2,1)} %copy-done.7, bf16[1024,1536]{1,0:T(8,128)(2,1)} %bitcast.157), custom_call_target="tpu_custom_call" | custom-call | flops 155250000 | bytes 517499 | tf_op jit(solution)/shard_map/product/pallas_call | solution.py:563
  307.1 5.5 %collective-permute-done.31.refs_3_ = bf16[4,2,64,1024]{3,2,1,0:T(8,128)(2,1)S(1)} collective-permute-done((bf16[4,2,64,1024]{3,2,1,0:T(8,128)(2,1)}, bf16[4,2,64,1024]{3,2,1,0:T(8,128)(2,1)S(1)}, u32[]{:S(2)}, u32[]{:S(2)}) %collective-permute-start.31) | collective-permute-done | bytes 1048608 | tf_op jit(solution)/shard_map/ppermute | solution.py:52
  320.2 9.5 %all-to-all-done.3 = bf16[4,128,2048]{2,1,0:T(8,128)(2,1)} async-done(((bf16[4,128,2048]{2,1,0:T(8,128)(2,1)}), bf16[4,128,2048]{2,1,0:T(8,128)(2,1)}, u32[]{:S(2)}, u32[]{:S(2)}) %all-to-all-start.3) | async-done | bytes 2097184 | tf_op jit(solution)/shard_map/all_to_all | solution.py:311
  336.4 5.1 %all-to-all-start.4 = ((bf16[4,72,2048]{2,1,0:T(8,128)(2,1)}), bf16[4,72,2048]{2,1,0:T(8,128)(2,1)S(1)}, u32[]{:S(2)}, u32[]{:S(2)}) async-start(bf16[4,72,2048]{2,1,0:T(8,128)(2,1)} %split_over_z.1), calls=%async_computation.4 | async-start | bytes 2359296 | tf_op jit(solution)/shard_map/all_to_all | solution.py:311
  361.8 6.3 %all-to-all-done.4 = bf16[4,72,2048]{2,1,0:T(8,128)(2,1)S(1)} async-done(((bf16[4,72,2048]{2,1,0:T(8,128)(2,1)}), bf16[4,72,2048]{2,1,0:T(8,128)(2,1)S(1)}, u32[]{:S(2)}, u32[]{:S(2)}) %all-to-all-start.4) | async-done | bytes 1179680 | tf_op jit(solution)/shard_map/all_to_all | solution.py:311
  (353 shorter events, 190.3 us)
Async XLA Ops:
  7.6 26.3 %collective-permute-start = (bf16[2,256,1024]{2,1,0:T(8,128)(2,1)}, bf16[2,256,1024]{2,1,0:T(8,128)(2,1)S(1)}, u32[]{:S(2)}, u32[]{:S(2)}) collective-permute-start(bf16[2,256,1024]{2,1,0:T(8,128)(2,1)} %get-tuple-element.176), channel_id=1, source_target_pairs={{0,2},{2,0},{1,3},{3,1},{4,6},{6,4},{5,7},{7,5},{8,10},{10,8},{9,1... | collective-permute-start | bytes 3145736 | tf_op jit(solution)/shard_map/ppermute | solution.py:52
  12.0 33.2 %all-to-all-start = ((bf16[4,72,2048]{2,1,0:T(8,128)(2,1)}), bf16[4,72,2048]{2,1,0:T(8,128)(2,1)S(1)}, u32[]{:S(2)}, u32[]{:S(2)}) async-start(bf16[4,72,2048]{2,1,0:T(8,128)(2,1)} %broadcast_in_dim.37), calls=%async_computation | async-start | bytes 2359296 | tf_op jit(solution)/shard_map/all_to_all | solution.py:141
  35.4 32.4 %collective-permute-start.1 = (bf16[2,512,1024]{2,1,0:T(8,128)(2,1)}, bf16[2,512,1024]{2,1,0:T(8,128)(2,1)}, u32[]{:S(2)}, u32[]{:S(2)}) collective-permute-start(bf16[2,512,1024]{2,1,0:T(8,128)(2,1)} %pad_maximum_fusion.1), channel_id=1, source_target_pairs={{0,1},{1,0},{2,3},{3,2},{4,5},{5,4},{6,7},{7,6},{8,9},{9,8},{10,11... | collective-permute-start | bytes 6291464 | tf_op jit(solution)/shard_map/ppermute | solution.py:52
  49.9 29.0 %all-to-all-start.1 = ((bf16[4,64,2048]{2,1,0:T(8,128)(2,1)}), bf16[4,64,2048]{2,1,0:T(8,128)(2,1)}, u32[]{:S(2)}, u32[]{:S(2)}) async-start(bf16[4,64,2048]{2,1,0:T(8,128)(2,1)} %broadcast_in_dim.38), calls=%async_computation.1 | async-start | bytes 2097152 | tf_op jit(solution)/shard_map/all_to_all | solution.py:141
  63.4 27.7 %collective-permute-start.4 = (bf16[2,4,72,1024]{3,2,1,0:T(8,128)(2,1)S(1)}, bf16[2,4,72,1024]{3,2,1,0:T(8,128)(2,1)}, u32[]{:S(2)}, u32[]{:S(2)}) collective-permute-start(bf16[2,4,72,1024]{3,2,1,0:T(8,128)(2,1)S(1)} %pad_maximum_fusion.2.refs_0_), channel_id=1, source_target_pairs={{0,4},{4,0},{1,5},{5,1},{2,6},{6,2},{3,7},{7,3},{8,12},{12,8},{9,1... | collective-permute-start | bytes 3538952 | tf_op jit(solution)/shard_map/ppermute | solution.py:52
  67.3 26.1 %collective-permute-start.6 = (bf16[2,4,72,1024]{3,2,1,0:T(8,128)(2,1)}, bf16[2,4,72,1024]{3,2,1,0:T(8,128)(2,1)}, u32[]{:S(2)}, u32[]{:S(2)}) collective-permute-start(bf16[2,4,72,1024]{3,2,1,0:T(8,128)(2,1)} %pad_maximum_fusion.3.refs_2_), channel_id=1, source_target_pairs={{0,2},{2,0},{1,3},{3,1},{4,6},{6,4},{5,7},{7,5},{8,10},{10,8},{9,1... | collective-permute-start | bytes 3538952 | tf_op jit(solution)/shard_map/ppermute | solution.py:52
  82.8 62.1 %all-to-all-start.2 = ((bf16[4,4,128,512]{3,2,1,0:T(8,128)(2,1)}), bf16[4,4,128,512]{3,2,1,0:T(8,128)(2,1)}, u32[]{:S(2)}, u32[]{:S(2)}) async-start(bf16[4,4,128,512]{3,2,1,0:T(8,128)(2,1)} %broadcast_in_dim.79), calls=%async_computation.2 | async-start | bytes 4194304 | tf_op jit(solution)/shard_map/all_to_all | solution.py:141
  101.0 34.9 %collective-permute-start.10 = (bf16[1024,512]{1,0:T(8,128)(2,1)}, bf16[1024,512]{1,0:T(8,128)(2,1)}, u32[]{:S(2)}, u32[]{:S(2)}) collective-permute-start(bf16[1024,512]{1,0:T(8,128)(2,1)} %bitcast.158), channel_id=1, source_target_pairs={{0,1},{1,0},{2,3},{3,2},{4,5},{5,4},{6,7},{7,6},{8,9},{9,8},{10,11... | collective-permute-start | bytes 3145736 | tf_op jit(solution)/shard_map/ppermute | solution.py:52
  107.3 27.8 %collective-permute-start.12 = (bf16[2,4,64,1024]{3,2,1,0:T(8,128)(2,1)}, bf16[2,4,64,1024]{3,2,1,0:T(8,128)(2,1)}, u32[]{:S(2)}, u32[]{:S(2)}) collective-permute-start(bf16[2,4,64,1024]{3,2,1,0:T(8,128)(2,1)} %pad_maximum_fusion.5.refs_2_), channel_id=1, source_target_pairs={{0,2},{2,0},{1,3},{3,1},{4,6},{6,4},{5,7},{7,5},{8,10},{10,8},{9,1... | collective-permute-start | bytes 3145736 | tf_op jit(solution)/shard_map/ppermute | solution.py:52
  148.2 27.6 %collective-permute-start.16 = (bf16[2,4,128,512]{3,2,1,0:T(8,128)(2,1)}, bf16[2,4,128,512]{3,2,1,0:T(8,128)(2,1)}, u32[]{:S(2)}, u32[]{:S(2)}) collective-permute-start(bf16[2,4,128,512]{3,2,1,0:T(8,128)(2,1)} %get-tuple-element.107.refs_0_), channel_id=1, source_target_pairs={{0,4},{4,0},{1,5},{5,1},{2,6},{6,2},{3,7},{7,3},{8,12},{12,8},{9,1... | collective-permute-start | bytes 3145736 | tf_op jit(solution)/shard_map/ppermute | solution.py:52
  149.1 26.6 %collective-permute-start.17 = (bf16[2,4,128,512]{3,2,1,0:T(8,128)(2,1)}, bf16[2,4,128,512]{3,2,1,0:T(8,128)(2,1)}, u32[]{:S(2)}, u32[]{:S(2)}) collective-permute-start(bf16[2,4,128,512]{3,2,1,0:T(8,128)(2,1)} %get-tuple-element.108.refs_2_), channel_id=1, source_target_pairs={{0,2},{2,0},{1,3},{3,1},{4,6},{6,4},{5,7},{7,5},{8,10},{10,8},{9,1... | collective-permute-start | bytes 3145736 | tf_op jit(solution)/shard_map/ppermute | solution.py:52
  173.1 28.5 %collective-permute-start.19 = (bf16[4,2,128,512]{3,2,1,0:T(8,128)(2,1)S(1)}, bf16[4,2,128,512]{3,2,1,0:T(8,128)(2,1)S(1)}, u32[]{:S(2)}, u32[]{:S(2)}) collective-permute-start(bf16[4,2,128,512]{3,2,1,0:T(8,128)(2,1)S(1)} %get-tuple-element.104), channel_id=1, source_target_pairs={{0,2},{2,0},{1,3},{3,1},{4,6},{6,4},{5,7},{7,5},{8,10},{10,8},{9,1... | collective-permute-start | bytes 3145736 | tf_op jit(solution)/shard_map/ppermute | solution.py:52
  174.6 26.9 %collective-permute-start.20 = (bf16[4,2,128,512]{3,2,1,0:T(8,128)(2,1)S(1)}, bf16[4,2,128,512]{3,2,1,0:T(8,128)(2,1)S(1)}, u32[]{:S(2)}, u32[]{:S(2)}) collective-permute-start(bf16[4,2,128,512]{3,2,1,0:T(8,128)(2,1)S(1)} %get-tuple-element.117), channel_id=1, source_target_pairs={{0,4},{4,0},{1,5},{5,1},{2,6},{6,2},{3,7},{7,3},{8,12},{12,8},{9,1... | collective-permute-start | bytes 3145736 | tf_op jit(solution)/shard_map/ppermute | solution.py:52
  200.1 25.6 %collective-permute-start.23 = (bf16[4,2,64,1024]{3,2,1,0:T(8,128)(2,1)S(1)}, bf16[4,2,64,1024]{3,2,1,0:T(8,128)(2,1)S(1)}, u32[]{:S(2)}, u32[]{:S(2)}) collective-permute-start(bf16[4,2,64,1024]{3,2,1,0:T(8,128)(2,1)S(1)} %get-tuple-element.125), channel_id=1, source_target_pairs={{0,4},{4,0},{1,5},{5,1},{2,6},{6,2},{3,7},{7,3},{8,12},{12,8},{9,1... | collective-permute-start | bytes 3145736 | tf_op jit(solution)/shard_map/ppermute | solution.py:52
  201.1 25.2 %collective-permute-start.22 = (bf16[4,2,64,1024]{3,2,1,0:T(8,128)(2,1)S(1)}, bf16[4,2,64,1024]{3,2,1,0:T(8,128)(2,1)S(1)}, u32[]{:S(2)}, u32[]{:S(2)}) collective-permute-start(bf16[4,2,64,1024]{3,2,1,0:T(8,128)(2,1)S(1)} %get-tuple-element.114), channel_id=1, source_target_pairs={{0,2},{2,0},{1,3},{3,1},{4,6},{6,4},{5,7},{7,5},{8,10},{10,8},{9,1... | collective-permute-start | bytes 3145736 | tf_op jit(solution)/shard_map/ppermute | solution.py:52
  237.3 34.9 %collective-permute-start.27 = (bf16[4,128,512]{2,1,0:T(8,128)(2,1)}, bf16[4,128,512]{2,1,0:T(8,128)(2,1)S(1)}, u32[]{:S(2)}, u32[]{:S(2)}) collective-permute-start(bf16[4,128,512]{2,1,0:T(8,128)(2,1)} %copy-done.40), channel_id=1, source_target_pairs={{0,4},{4,0},{1,5},{5,1},{2,6},{6,2},{3,7},{7,3},{8,12},{12,8},{9,1... | collective-permute-start | bytes 1572872 | tf_op jit(solution)/shard_map/ppermute | solution.py:52
  238.4 33.9 %collective-permute-start.28 = (bf16[4,128,512]{2,1,0:T(8,128)(2,1)}, bf16[4,128,512]{2,1,0:T(8,128)(2,1)S(1)}, u32[]{:S(2)}, u32[]{:S(2)}) collective-permute-start(bf16[4,128,512]{2,1,0:T(8,128)(2,1)} %copy-done.39), channel_id=1, source_target_pairs={{0,2},{2,0},{1,3},{3,1},{4,6},{6,4},{5,7},{7,5},{8,10},{10,8},{9,1... | collective-permute-start | bytes 1572872 | tf_op jit(solution)/shard_map/ppermute | solution.py:52
  239.4 32.9 %collective-permute-start.25 = (bf16[4,64,1024]{2,1,0:T(8,128)(2,1)}, bf16[4,64,1024]{2,1,0:T(8,128)(2,1)S(1)}, u32[]{:S(2)}, u32[]{:S(2)}) collective-permute-start(bf16[4,64,1024]{2,1,0:T(8,128)(2,1)} %copy-done.42), channel_id=1, source_target_pairs={{0,4},{4,0},{1,5},{5,1},{2,6},{6,2},{3,7},{7,3},{8,12},{12,8},{9,1... | collective-permute-start | bytes 1572872 | tf_op jit(solution)/shard_map/ppermute | solution.py:52
  241.4 30.9 %collective-permute-start.26 = (bf16[4,64,1024]{2,1,0:T(8,128)(2,1)}, bf16[4,64,1024]{2,1,0:T(8,128)(2,1)S(1)}, u32[]{:S(2)}, u32[]{:S(2)}) collective-permute-start(bf16[4,64,1024]{2,1,0:T(8,128)(2,1)} %copy-done.41), channel_id=1, source_target_pairs={{0,2},{2,0},{1,3},{3,1},{4,6},{6,4},{5,7},{7,5},{8,10},{10,8},{9,1... | collective-permute-start | bytes 1572872 | tf_op jit(solution)/shard_map/ppermute | solution.py:52
  274.4 55.3 %all-to-all-start.3 = ((bf16[4,128,2048]{2,1,0:T(8,128)(2,1)}), bf16[4,128,2048]{2,1,0:T(8,128)(2,1)}, u32[]{:S(2)}, u32[]{:S(2)}) async-start(bf16[4,128,2048]{2,1,0:T(8,128)(2,1)} %split_both_over_z.1), calls=%async_computation.3 | async-start | bytes 4194304 | tf_op jit(solution)/shard_map/all_to_all | solution.py:311
  286.7 25.9 %collective-permute-start.31 = (bf16[4,2,64,1024]{3,2,1,0:T(8,128)(2,1)}, bf16[4,2,64,1024]{3,2,1,0:T(8,128)(2,1)S(1)}, u32[]{:S(2)}, u32[]{:S(2)}) collective-permute-start(bf16[4,2,64,1024]{3,2,1,0:T(8,128)(2,1)} %get-tuple-element.156), channel_id=1, source_target_pairs={{0,4},{4,0},{1,5},{5,1},{2,6},{6,2},{3,7},{7,3},{8,12},{12,8},{9,1... | collective-permute-start | bytes 3145736 | tf_op jit(solution)/shard_map/ppermute | solution.py:52
  288.2 25.9 %collective-permute-start.30 = (bf16[4,2,64,1024]{3,2,1,0:T(8,128)(2,1)}, bf16[4,2,64,1024]{3,2,1,0:T(8,128)(2,1)}, u32[]{:S(2)}, u32[]{:S(2)}) collective-permute-start(bf16[4,2,64,1024]{3,2,1,0:T(8,128)(2,1)} %get-tuple-element.135), channel_id=1, source_target_pairs={{0,2},{2,0},{1,3},{3,1},{4,6},{6,4},{5,7},{7,5},{8,10},{10,8},{9,1... | collective-permute-start | bytes 3145736 | tf_op jit(solution)/shard_map/ppermute | solution.py:52
  336.4 31.8 %all-to-all-start.4 = ((bf16[4,72,2048]{2,1,0:T(8,128)(2,1)}), bf16[4,72,2048]{2,1,0:T(8,128)(2,1)S(1)}, u32[]{:S(2)}, u32[]{:S(2)}) async-start(bf16[4,72,2048]{2,1,0:T(8,128)(2,1)} %split_over_z.1), calls=%async_computation.4 | async-start | bytes 2359296 | tf_op jit(solution)/shard_map/all_to_all | solution.py:311
  346.0 24.6 %collective-permute-start.37 = (bf16[256,1024]{1,0:T(8,128)(2,1)}, bf16[256,1024]{1,0:T(8,128)(2,1)}, u32[]{:S(2)}, u32[]{:S(2)}) collective-permute-start(bf16[256,1024]{1,0:T(8,128)(2,1)} %slice_bitcast_fusion), channel_id=1, source_target_pairs={{0,2},{2,0},{1,3},{3,1},{4,6},{6,4},{5,7},{7,5},{8,10},{10,8},{9,1... | collective-permute-start | bytes 1572872 | tf_op jit(solution)/shard_map/ppermute | solution.py:52
  (81 other events, 674.1 us)
